TPU v7x, 32 devices: a whole 2x2x4 slice. The times are simulated.
32 devices in a mesh: dp: 16 (over z, y, core), mp: 2 (over x).
Axes of the slice: x: 2, y: 2, z: 4, core: 2. Of those that a mesh axis runs over, the one named last changes fastest.
Arguments:
- tokens: float32 [16384, 1472], P(('dp', 'mp')), may hold values from -6 to 6
- cotangent: float32 [16384, 1472], P(('dp', 'mp')), may hold values from -6 to 6
- doc_lengths: int32 [16, 4], P('dp'), may hold values from 1 to 512, 1024 in all within a row
- pad_mask: int32 [16, 1024], P('dp'), may hold values 0 or 1
- attn_gain: float32 [1472], replicated, may hold values from 0.5 to 1.5
- qkv_weight: bfloat16 [1472, 3, 384], P(None, None, 'mp'), may hold values from -0.078125 to 0.078125
- rel_table: float32 [32, 6], P(None, 'mp'), may hold values from -6 to 6
- out_weight: bfloat16 [1472, 384], P(None, 'mp'), may hold values from -0.4375 to 0.4375
- ff_gain: float32 [1472], replicated, may hold values from 0.5 to 1.5
- ff_in_weight: bfloat16 [1472, 2, 3584], P(None, None, 'mp'), may hold values from -0.15625 to 0.15625
- ff_out_weight: bfloat16 [1472, 3584], P(None, 'mp'), may hold values from -0.1875 to 0.1875
Outputs:
- result: float32 [16384, 1472], P(('dp', 'mp'))
- input_grad: float32 [16384, 1472], P(('dp', 'mp'))
- attn_gain_grad: float32 [1472], replicated
- qkv_weight_grad: float32 [1472, 3, 384], P('dp', None, 'mp')
- rel_table_grad: float32 [32, 6], replicated
- out_weight_grad: float32 [1472, 384], P('dp', 'mp')
- ff_gain_grad: float32 [1472], replicated
- ff_in_grad: float32 [1472, 2, 3584], P('dp', None, 'mp')
- ff_out_grad: float32 [1472, 3584], P('dp', 'mp')
All inputs are finite; a program needn't handle non-finite values. No bound on the sum of `pad_mask` on one device may be relied on, other than what follows from the above.
Results may differ from a plain program's by a relative error of at most 0.035.
Values may be sent and summed in bfloat16 or wider, within the bound.
A program may use at most 256 MiB of HBM per device.

v0:
```python
import functools

import jax
import jax.numpy as jnp
import numpy as np
from jax import lax
from jax.experimental import pallas as pl
from jax.experimental.pallas import tpu as pltpu
from jax.sharding import PartitionSpec as P

MAXDIST = 128
norm_eps = 1e-06
BLK = 256
SPAN = 6 * BLK
REACH = 2
BF = jnp.bfloat16
F32 = jnp.float32
VMEM_LIMIT = 56 << 20
FF_VMEM = 63 << 20


def bucket_of(offsets, buckets, reach):
    half_range = buckets // 2
    upper_half = (offsets > 0).astype(np.int32) * half_range
    distance = np.abs(offsets)
    exact_range = half_range // 2
    safe_dist = np.maximum(distance, 1)
    log_bucket = exact_range + (
        np.log(safe_dist / exact_range) / np.log(reach / exact_range) * (half_range - exact_range)
    ).astype(np.int32)
    log_bucket = np.minimum(log_bucket, half_range - 1)
    return (upper_half + np.where(distance < exact_range, distance, log_bucket)).astype(np.int32)


def lane_buckets(buckets):
    lanes = np.arange(SPAN)
    shifted = np.where(lanes < 5 * BLK, lanes, lanes - SPAN)
    return bucket_of(REACH * BLK - shifted, buckets, MAXDIST).reshape(1, SPAN)


def dot(a, b, contract):
    return lax.dot_general(a, b, (contract, ((), ())), preferred_element_type=F32)


def diagonal_of(key_block, query_block, x, blocks):
    half = blocks // 2
    key_true = lax.rem(key_block + half * x, blocks)
    query_true = lax.rem(query_block + half * x, blocks)
    return jnp.clip(key_true - query_true, -REACH, REACH) + REACH


def attn_fwd_kernel(
    heads, dk, buckets, blocks,
    x_ref, rel_ref, bid_ref, doc_ref, code_ref, q_ref, k_ref, v_ref,
    e_ref, inv_ref, ctx_ref,
    table, vt, mask, score, acc,
):
    qb, h = pl.program_id(0), pl.program_id(1)
    x = x_ref[0]

    @pl.when((qb == 0) & (h == 0))
    def _():
        vt[...] = v_ref[...].astype(F32).T.astype(BF)
        ids = bid_ref[...]
        for hh in range(heads):
            line = jnp.zeros((1, SPAN), F32)
            for b in range(buckets):
                line = jnp.where(ids == b, rel_ref[b, hh], line)
            rows = pltpu.roll(
                jnp.broadcast_to(line, (BLK, SPAN)), 0, 1, stride=1, stride_axis=0
            )
            for d in range(5):
                table[hh, d] = rows[:, BLK * (4 - d) : BLK * (5 - d)]

    @pl.when(h == 0)
    def _():
        row = lax.broadcasted_iota(jnp.int32, (BLK, BLK), 0)
        col = lax.broadcasted_iota(jnp.int32, (BLK, BLK), 1)
        for kb in range(blocks):
            same = code_ref[kb * BLK : (kb + 1) * BLK, :] == doc_ref[...]
            diag = (row + kb * BLK) == (col + qb * BLK)
            mask[kb * BLK : (kb + 1) * BLK, :] = jnp.where(same | diag, 0.0, -1000000000.0)

    lane = lax.broadcasted_iota(jnp.int32, q_ref.shape, 1)
    qm = jnp.where(lane // dk == h, q_ref[...], jnp.zeros_like(q_ref[...]))
    peak = None
    for kb in range(blocks):
        rows = slice(kb * BLK, (kb + 1) * BLK)
        s = dot(k_ref[rows, :], qm, ((1,), (1,)))
        s = s + table[h, diagonal_of(kb, qb, x, blocks)] + mask[rows, :]
        score[rows, :] = s
        top = jnp.max(s, axis=0, keepdims=True)
        peak = top if peak is None else jnp.maximum(peak, top)
    total = jnp.zeros((1, BLK), F32)
    ctx = jnp.zeros((dk, BLK), F32)
    hrows = pl.ds(pl.multiple_of(h * dk, dk), dk)
    for kb in range(blocks):
        rows = slice(kb * BLK, (kb + 1) * BLK)
        e = jnp.exp(score[rows, :] - peak)
        total = total + jnp.sum(e, axis=0, keepdims=True)
        e_low = e.astype(BF)
        e_ref[0, 0, rows, :] = e_low
        ctx = ctx + dot(vt[hrows, rows], e_low, ((1,), (0,)))
    inv = 1.0 / total
    inv_ref[0, 0] = inv
    acc[hrows, :] = ctx * inv

    @pl.when(h == heads - 1)
    def _():
        ctx_ref[...] = acc[...].T.astype(BF)


def attn_fwd(x, rel, doc, code, q, k, v, heads, dk):
    seq, cols = q.shape
    blocks = seq // BLK
    buckets = rel.shape[0]
    bids = jnp.asarray(lane_buckets(buckets))
    whole = lambda i, h: (0, 0)
    return pl.pallas_call(
        functools.partial(attn_fwd_kernel, heads, dk, buckets, blocks),
        grid=(blocks, heads),
        in_specs=[
            pl.BlockSpec(memory_space=pltpu.SMEM),
            pl.BlockSpec(memory_space=pltpu.SMEM),
            pl.BlockSpec((1, SPAN), whole),
            pl.BlockSpec((1, BLK), lambda i, h: (0, i)),
            pl.BlockSpec((seq, 1), whole),
            pl.BlockSpec((BLK, cols), lambda i, h: (i, 0)),
            pl.BlockSpec((seq, cols), whole),
            pl.BlockSpec((seq, cols), whole),
        ],
        out_specs=[
            pl.BlockSpec((1, 1, seq, BLK), lambda i, h: (h, i, 0, 0)),
            pl.BlockSpec((1, 1, 1, BLK), lambda i, h: (h, i, 0, 0)),
            pl.BlockSpec((BLK, cols), lambda i, h: (i, 0)),
        ],
        out_shape=[
            jax.ShapeDtypeStruct((heads, blocks, seq, BLK), BF),
            jax.ShapeDtypeStruct((heads, blocks, 1, BLK), F32),
            jax.ShapeDtypeStruct((seq, cols), BF),
        ],
        scratch_shapes=[
            pltpu.VMEM((heads, 5, BLK, BLK), F32),
            pltpu.VMEM((cols, seq), BF),
            pltpu.VMEM((seq, BLK), F32),
            pltpu.VMEM((seq, BLK), F32),
            pltpu.VMEM((cols, BLK), F32),
        ],
        compiler_params=pltpu.CompilerParams(vmem_limit_bytes=VMEM_LIMIT),
        cost_estimate=pl.CostEstimate(
            flops=16 * heads * seq * seq * dk,
            bytes_accessed=2 * heads * seq * seq + 8 * seq * cols,
            transcendentals=heads * seq * seq,
        ),
    )(x, rel, bids, doc, code, q, k, v)


def flip(index, mask):
    out = index
    bit = 1
    while bit <= mask:
        if mask & bit:
            out = out + bit * (1 - 2 * (index // bit % 2))
        bit *= 2
    return out


GROUP_MASKS = (1, 2, 4, 12)


def group_coords(g):
    b = [g // (1 << i) % 2 for i in range(4)]
    return [b[0], b[1], (b[2] + b[3]) % 2, b[3]]


def block_position(k):
    b = [k >> i & 1 for i in range(4)]
    c = [b[0], b[1], b[2] ^ b[3], b[3]]
    return c[0] * 8 + c[1] * 4 + c[2] * 2 + c[3]


def ff_kernel(
    steps, extra,
    x_ref, c_ref, xt_ref, ct_ref, wg_ref, wu_ref, wo_hbm,
    grads_ref, din_hbm, near_hbm, far_hbm,
    wo, hid, dg, du, din, stage, r1, r2, r3, r4, xs, xr, of,
    wo_sem, s1, s2, s3, s4, t1, t2, t3, t4, xsem, osem,
):
    j = pl.program_id(0)
    last = j == steps - 1
    total, f = hid.shape
    rows = total // 2
    d = xt_ref.shape[0]
    shard = d // 16
    dp, mp = lax.axis_index("dp"), lax.axis_index("mp")
    a = group_coords(dp // extra)
    peers = [flip(dp, m * extra) for m in GROUP_MASKS]
    bufs = (r1, r2, r3, r4)
    sends, recvs = (s1, s2, s3, s4), (t1, t2, t3, t4)
    mesh = pl.DeviceIdType.MESH

    def wo_copy(i):
        cols = pl.ds(pl.multiple_of(i * BLK, BLK), BLK)
        return pltpu.make_async_copy(wo_hbm.at[:, cols], wo.at[:, cols], wo_sem.at[i])

    def hop(level, s, w):
        half = 8 >> level
        away = pl.ds((1 - a[level]) * half, half)
        src = stage.at[w, away] if level == 0 else bufs[level - 1].at[s, away]
        return pltpu.make_async_remote_copy(
            src_ref=src,
            dst_ref=bufs[level].at[s],
            send_sem=sends[level].at[s],
            recv_sem=recvs[level].at[s],
            device_id=(peers[level], mp),
            device_id_type=mesh,
        )

    def absorb(level, step, w):
        s = step * 3 + w
        half = 8 >> level
        copy = hop(level, s, w)
        copy.wait_recv()
        copy.wait_send()
        keep = pl.ds(a[level] * half, half)
        kept = stage[w, keep] if level == 0 else bufs[level - 1][s, keep]
        both = kept.astype(F32) + bufs[level][s].astype(F32)
        if level < 3:
            bufs[level][s] = both.astype(BF)
            hop(level + 1, s, w).start()
        else:
            cols = pl.ds(pl.multiple_of(step * BLK, BLK), BLK)
            grads_ref[w, :, cols] = both[0]

    def absorb_step(level, step):
        def one(w, carry):
            absorb(level, step, w)
            return carry

        lax.fori_loop(0, 3, one, 0)

    @pl.when(j == 0)
    def _():
        barrier = pltpu.get_barrier_semaphore()
        for peer in peers:
            pl.semaphore_signal(barrier, inc=1, device_id=(peer, mp), device_id_type=mesh)
        pl.semaphore_signal(barrier, inc=1, device_id=(dp, 1 - mp), device_id_type=mesh)
        pl.semaphore_wait(barrier, 5)
        for i in range(steps):
            wo_copy(i).start()
        din[...] = jnp.zeros_like(din)
        stage[...] = jnp.zeros_like(stage)

    wo_copy(j).wait()
    cols = pl.ds(pl.multiple_of(j * BLK, BLK), BLK)
    scale = np.float32(np.sqrt(2 / np.pi))
    for r in range(total // BLK):
        rs = slice(r * BLK, (r + 1) * BLK)
        gate = dot(x_ref[rs, :], wg_ref[...], ((1,), (0,)))
        up = dot(x_ref[rs, :], wu_ref[...], ((1,), (0,)))
        dh = dot(c_ref[rs, :], wo[:, cols], ((1,), (0,)))
        sq = gate * gate
        t = jnp.tanh(scale * gate * (1.0 + 0.044715 * sq))
        half = 0.5 * (1.0 + t)
        act = gate * half
        slope = half + 0.5 * gate * (1.0 - t * t) * (scale * (1.0 + (3 * 0.044715) * sq))
        hid[rs, cols] = (act * up).astype(BF)
        dgr = (dh * up * slope).astype(BF)
        dur = (dh * act).astype(BF)
        dg[rs, :] = dgr
        du[rs, :] = dur
        din[rs, :] += dot(dgr, wg_ref[...], ((1,), (1,))) + dot(dur, wu_ref[...], ((1,), (1,)))

    x_copy = pltpu.make_async_remote_copy(
        src_ref=xs,
        dst_ref=xr,
        send_sem=xsem.at[0],
        recv_sem=xsem.at[1],
        device_id=(dp, 1 - mp),
        device_id_type=mesh,
    )

    @pl.when(last)
    def _():
        xs[...] = din[rows:, :].astype(BF)
        x_copy.start()

    @pl.when(j > 0)
    def _():
        absorb(0, j - 1, 2)

    per = 4 * shard
    for w in range(3):
        left = ct_ref if w == 0 else xt_ref
        right = hid[:, cols] if w == 0 else (dg[...] if w == 1 else du[...])
        for q in range(4):
            part = dot(left[q * per : (q + 1) * per, :], right, ((1,), (0,)))
            for k in range(4):
                stage[w, block_position(4 * q + k), 0:shard, :] = part[
                    k * shard : (k + 1) * shard
                ].astype(BF)
        hop(0, j * 3 + w, w).start()
        if w > 0:
            absorb(0, j, w - 1)

    for level, lag in ((1, 3), (2, 4), (3, 5)):
        @pl.when(j >= lag)
        def _():
            absorb_step(level, j - lag)

    @pl.when(last)
    def _():
        end = steps - 1
        absorb(0, end, 2)
        for r in (2, 3):
            rs = slice(r * BLK, (r + 1) * BLK)
            o = dot(hid[rs, :], wo[...], ((1,), (1,)))
            of[(r - 2) * BLK : (r - 1) * BLK, :] = o.astype(BF)
        far_copy = pltpu.make_async_copy(of, far_hbm, osem.at[0])
        far_copy.start()
        absorb_step(1, end - 2)
        absorb_step(2, end - 3)
        absorb_step(3, end - 4)
        for r in (0, 1):
            rs = slice(r * BLK, (r + 1) * BLK)
            o = dot(hid[rs, :], wo[...], ((1,), (1,)))
            din[rows + r * BLK : rows + (r + 1) * BLK, :] = o
        near_copy = pltpu.make_async_copy(din.at[rows:], near_hbm, osem.at[1])
        near_copy.start()
        absorb_step(1, end - 1)
        absorb_step(2, end - 2)
        absorb_step(3, end - 3)
        absorb_step(1, end)
        absorb_step(2, end - 1)
        absorb_step(3, end - 2)
        x_copy.wait()
        din[:rows, :] += xr[...].astype(F32)
        din_copy = pltpu.make_async_copy(din.at[:rows], din_hbm, osem.at[2])
        din_copy.start()
        absorb_step(2, end)
        absorb_step(3, end - 1)
        absorb_step(3, end)
        far_copy.wait()
        near_copy.wait()
        din_copy.wait()


def ff_all(x, c, xt, ct, w2, wo, extra):
    total, dpad = x.shape
    d = xt.shape[0]
    f = wo.shape[1]
    rows = total // 2
    steps = f // BLK
    chunks = 3 * steps
    shard = d // 16
    spad = -(-shard // 16) * 16
    one = pl.Buffered(1)
    whole = lambda j: (0, 0)
    dma = pltpu.SemaphoreType.DMA
    any_spec = pl.BlockSpec(memory_space=pl.ANY)
    return pl.pallas_call(
        functools.partial(ff_kernel, steps, extra),
        grid=(steps,),
        in_specs=[
            pl.BlockSpec((total, dpad), whole, pipeline_mode=one),
            pl.BlockSpec((total, dpad), whole, pipeline_mode=one),
            pl.BlockSpec((d, total), whole, pipeline_mode=one),
            pl.BlockSpec((d, total), whole, pipeline_mode=one),
            pl.BlockSpec((None, dpad, BLK), lambda j: (0, 0, j)),
            pl.BlockSpec((None, dpad, BLK), lambda j: (1, 0, j)),
            any_spec,
        ],
        out_specs=[
            pl.BlockSpec((3, spad, f), lambda j: (0, 0, 0)),
            any_spec,
            any_spec,
            any_spec,
        ],
        out_shape=[
            jax.ShapeDtypeStruct((3, spad, f), F32),
            jax.ShapeDtypeStruct((rows, dpad), F32),
            jax.ShapeDtypeStruct((rows, dpad), F32),
            jax.ShapeDtypeStruct((rows, dpad), BF),
        ],
        scratch_shapes=[
            pltpu.VMEM((dpad, f), BF),
            pltpu.VMEM((total, f), BF),
            pltpu.VMEM((total, BLK), BF),
            pltpu.VMEM((total, BLK), BF),
            pltpu.VMEM((total, dpad), F32),
            pltpu.VMEM((3, 16, spad, BLK), BF),
            pltpu.VMEM((chunks, 8, spad, BLK), BF),
            pltpu.VMEM((chunks, 4, spad, BLK), BF),
            pltpu.VMEM((chunks, 2, spad, BLK), BF),
            pltpu.VMEM((chunks, 1, spad, BLK), BF),
            pltpu.VMEM((rows, dpad), BF),
            pltpu.VMEM((rows, dpad), BF),
            pltpu.VMEM((rows, dpad), BF),
            dma((steps,)),
            dma((chunks,)), dma((chunks,)), dma((chunks,)), dma((chunks,)),
            dma((chunks,)), dma((chunks,)), dma((chunks,)), dma((chunks,)),
            dma((2,)),
            dma((3,)),
        ],
        compiler_params=pltpu.CompilerParams(
            vmem_limit_bytes=FF_VMEM, collective_id=0, has_side_effects=True
        ),
        cost_estimate=pl.CostEstimate(
            flops=18 * total * d * f,
            bytes_accessed=6 * d * f + 16 * total * d,
            transcendentals=total * f,
        ),
    )(x, c, xt, ct, w2, w2, wo)


def tail_kernel(
    heads, dk, buckets, blocks, extra,
    bid_ref, q_ref, k_ref, v_ref, e_ref, inv_ref, wo_ref, wof_ref, ctx_ref, ctxf_ref, ag_ref, fg_ref,
    din_hbm, mid_hbm, cot_hbm, tok_hbm, nrm_hbm, wfl_hbm, far_hbm,
    ig_hbm, g_ref, small_ref, back_hbm,
    f1, f2, f3, nrm, wfl, alow, dctx, dcs, osend, orecv, gsum, fsum,
    kt, dct, dp_s, dka, dva, dqa, tally, dproj, grad, dns, dnr,
    stage, t1, t2, t3, t4, sb, rb,
    lsem, xs_sem, xr_sem, cs_sem, cr_sem, bs_sem, br_sem,
):
    qb, h = pl.program_id(0), pl.program_id(1)
    dp, x = lax.axis_index("dp"), lax.axis_index("mp")
    rows, d = f2.shape
    cols = dctx.shape[1]
    shard = d // 16
    mesh = pl.DeviceIdType.MESH
    a = group_coords(dp // extra)
    peers = [flip(dp, m * extra) for m in GROUP_MASKS]
    other = (dp, 1 - x)
    bufs = (stage, t1, t2, t3, t4)

    def remote(src, dst, send, recv, who):
        return pltpu.make_async_remote_copy(
            src_ref=src, dst_ref=dst, send_sem=send, recv_sem=recv, device_id=who, device_id_type=mesh
        )

    def local(i):
        src, dst = (
            (din_hbm, f1), (mid_hbm, f2), (cot_hbm, f3), (tok_hbm, f2), (nrm_hbm, nrm), (wfl_hbm, wfl)
        )[i]
        return pltpu.make_async_copy(src, dst, lsem.at[i])

    dctx_copy = remote(dcs, dctx.at[pl.ds(rows, rows)], xs_sem.at[0], xr_sem.at[0], other)
    o_copy = remote(osend, orecv, xs_sem.at[1], xr_sem.at[1], other)
    back_copy = remote(far_hbm, back_hbm, xs_sem.at[2], xr_sem.at[2], other)

    def dn_copy(r):
        return remote(dns.at[r], dnr.at[r], xs_sem.at[3 + r], xr_sem.at[3 + r], other)

    def hop(level):
        half = 8 >> level
        away = pl.ds((1 - a[level]) * half, half)
        return remote(
            bufs[level].at[away], bufs[level + 1], cs_sem.at[level], cr_sem.at[level], (peers[level], x)
        )

    def absorb(level):
        half = 8 >> level
        copy = hop(level)
        copy.wait()
        both = bufs[level][pl.ds(a[level] * half, half)].astype(F32) + bufs[level + 1][...].astype(F32)
        if level < 3:
            bufs[level + 1][...] = both.astype(BF)
            hop(level + 1).start()
        else:
            g_ref[...] = both[0]

    def round_copy(i):
        who = other if i == 4 else (peers[i], x)
        return remote(sb.at[i], rb.at[i], bs_sem.at[i], br_sem.at[i], who)

    def round_end(i):
        round_copy(i).wait()
        sb[i + 1] = sb[i] + rb[i]
        if i < 4:
            round_copy(i + 1).start()

    def out_copy(r):
        rs = pl.ds(r * BLK, BLK)
        return pltpu.make_async_copy(f3.at[rs], ig_hbm.at[rs], lsem.at[6 + r])

    @pl.when((qb == 0) & (h == 0))
    def _():
        barrier = pltpu.get_barrier_semaphore()
        for i in range(3):
            local(i).start()
        for peer in peers:
            pl.semaphore_signal(barrier, inc=1, device_id=(peer, x), device_id_type=mesh)
        pl.semaphore_signal(barrier, inc=1, device_id=other, device_id_type=mesh)
        pl.semaphore_wait(barrier, 5)
        kt[...] = k_ref[...].astype(F32).T.astype(BF)
        dka[...] = jnp.zeros_like(dka)
        dva[...] = jnp.zeros_like(dva)
        tally[...] = jnp.zeros_like(tally)
        stage[...] = jnp.zeros_like(stage)
        fsum[...] = jnp.zeros_like(fsum)
        gsum[...] = jnp.zeros_like(gsum)
        for i in range(3):
            local(i).wait()
        for r in range(rows // BLK):
            rs = slice(r * BLK, (r + 1) * BLK)
            v = f2[rs, :]
            c = f1[rs, :d]
            scale = lax.rsqrt(jnp.mean(v * v, axis=-1, keepdims=True) + norm_eps)
            n = v * scale
            cg = c * fg_ref[...]
            m = jnp.mean(cg * n, axis=-1, keepdims=True)
            gm = f3[rs, :] + scale * (cg - n * m)
            fsum[...] += jnp.sum(c * n, axis=0, keepdims=True)
            f1[rs, :d] = gm
            alow[rs, :] = gm.astype(BF)
        for i in range(3, 6):
            local(i).start()
        dcs[...] = dot(alow[...], wof_ref[...], ((1,), (0,))).astype(BF)
        dctx_copy.start()
        dctx[:rows, :] = dot(alow[...], wo_ref[...], ((1,), (0,))).astype(BF)
        osend[...] = dot(alow[...], ctxf_ref[...], ((0,), (0,))).astype(BF)
        grad[:, 3 * cols : 4 * cols] = dot(alow[...], ctx_ref[...], ((0,), (0,)))
        dctx_copy.wait()
        o_copy.start()
        back_copy.start()

    qrows = pl.ds(pl.multiple_of(qb * BLK, BLK), BLK)

    @pl.when(h == 0)
    def _():
        dct[...] = dctx[qrows, :].astype(F32).T

    lane = lax.broadcasted_iota(jnp.int32, q_ref.shape, 1)
    qm = jnp.where(lane // dk == h, q_ref[...], jnp.zeros_like(q_ref[...]))
    row = lax.broadcasted_iota(jnp.int32, dct.shape, 0)
    inv = inv_ref[0, 0]
    ds_t = jnp.where(row // dk == h, dct[...] * inv, 0.0)
    scaled_t = ds_t.astype(BF)
    scaled = ds_t.T.astype(BF)
    inner = jnp.zeros((1, BLK), F32)
    for kb in range(blocks):
        krows = slice(kb * BLK, (kb + 1) * BLK)
        g = dot(v_ref[krows, :], scaled_t, ((1,), (0,)))
        dp_s[krows, :] = g
        inner = inner + jnp.sum(e_ref[0, 0, krows, :].astype(F32) * g, axis=0, keepdims=True)
    inner = inner * inv
    hrows = pl.ds(pl.multiple_of(h * dk, dk), dk)
    dq = jnp.zeros((dk, BLK), F32)
    q_true = (qb + blocks // 2 * x) % blocks
    for kb in range(blocks):
        krows = slice(kb * BLK, (kb + 1) * BLK)
        e = e_ref[0, 0, krows, :]
        ds = (e.astype(F32) * (dp_s[krows, :] - inner)).astype(BF)
        dka[krows, :] += dot(ds, qm, ((1,), (0,)))
        dva[krows, :] += dot(e, scaled, ((1,), (0,)))
        dq = dq + dot(kt[hrows, krows], ds, ((1,), (0,)))
        diag = (kb + blocks // 2 * x) % blocks - q_true + blocks - 1
        tally[h, diag] += ds.astype(F32)
    dqa[hrows, :] = dq

    @pl.when(h == heads - 1)
    def _():
        dproj[qrows, 0:cols] = dqa[...].T.astype(BF)

    @pl.when((h == heads - 1) & (qb == blocks - 1))
    def _():
        dproj[:, cols : 2 * cols] = dka[...].astype(BF)
        dproj[:, 2 * cols : 3 * cols] = dva[...].astype(BF)
        for i in range(3, 6):
            local(i).wait()
        for r in range(rows // BLK):
            rs = slice(rows + r * BLK, rows + (r + 1) * BLK)
            part = dot(dproj[rs, :], wfl[...], ((1,), (1,)))
            dns[r] = part.astype(BF)
            dn_copy(r).start()
            gsum[...] += jnp.sum(nrm[rs, :].astype(F32) * part, axis=0, keepdims=True)
        step = 3 * 128
        for c in range(0, d, step):
            cs = slice(c, min(c + step, d))
            grad[cs, 0 : 3 * cols] = dot(nrm[:, cs], dproj[...], ((0,), (0,)))
        o_copy.wait()
        grad[:, 3 * cols : 4 * cols] += orecv[...].astype(F32)
        for k in range(16):
            stage[block_position(k), 0:shard, :] = grad[k * shard : (k + 1) * shard, :].astype(BF)
        hop(0).start()
        for r in range(rows // BLK):
            rs = slice(r * BLK, (r + 1) * BLK)
            part = dot(dproj[rs, :], wfl[...], ((1,), (1,)))
            f3[rs, :] = part
            gsum[...] += jnp.sum(nrm[rs, :].astype(F32) * part, axis=0, keepdims=True)
        absorb(0)
        ids = bid_ref[...]
        hot = ids == lax.broadcasted_iota(jnp.int32, (buckets, SPAN), 0)
        out_lane = lax.broadcasted_iota(jnp.int32, (buckets, 128), 1)
        sub = lax.broadcasted_iota(jnp.int32, (8, SPAN), 0)
        out = jnp.zeros((buckets, 128), F32)
        for hh in range(heads):
            line = jnp.zeros((8, SPAN), F32)
            for g in range(BLK // 8):
                group = slice(8 * g, 8 * g + 8)
                t = [tally[hh, i, group, :] for i in range(7)]
                parts = [t[5] + t[6], t[4], t[3], t[2], t[1] + t[0]]
                strip = jnp.concatenate(parts + [jnp.zeros((8, BLK), F32)], axis=1)
                line = line + (strip if g == 0 else pltpu.roll(strip, SPAN - 8 * g, 1))
            for bit in (1, 2, 4):
                line = jnp.where((sub // bit) % 2 == 1, pltpu.roll(line, SPAN - bit, 1), line)
            sums = jnp.sum(line, axis=0, keepdims=True)
            col = jnp.sum(jnp.where(hot, sums, 0.0), axis=1, keepdims=True)
            out = jnp.where(out_lane == x * heads + hh, col, out)
        sb[0] = jnp.zeros(sb.shape[1:], F32)
        sb[0, 0:buckets, :] = out
        again = gsum[...] / ag_ref[...]
        lines = -(-d // 128)
        for i in range(lines):
            n = min(128, d - 128 * i)
            sb[0, buckets + i : buckets + i + 1, 0:n] = again[:, 128 * i : 128 * i + n]
            sb[0, buckets + lines + i : buckets + lines + i + 1, 0:n] = fsum[:, 128 * i : 128 * i + n]
        round_copy(0).start()
        absorb(1)
        round_end(0)
        round_end(1)
        for r in range(rows // BLK):
            rs = slice(r * BLK, (r + 1) * BLK)
            dn_copy(r).wait()
            c = f3[rs, :] + dnr[r].astype(F32)
            v = f2[rs, :]
            scale = lax.rsqrt(jnp.mean(v * v, axis=-1, keepdims=True) + norm_eps)
            n = v * scale
            cg = c * ag_ref[...]
            m = jnp.mean(cg * n, axis=-1, keepdims=True)
            f3[rs, :] = f1[rs, :d] + scale * (cg - n * m)
            out_copy(r).start()
            if r == 0:
                absorb(2)
                round_end(2)
                round_end(3)
        absorb(3)
        round_end(4)
        small_ref[...] = sb[5]
        back_copy.wait()
        for r in range(rows // BLK):
            out_copy(r).wait()


def tail(q, k, v, e, inv, wo, wof, ctx, ctxf, again, fgain, din, mid, cot, tok, nrm, wfl, far,
         buckets, heads, dk, extra):
    seq, cols = q.shape
    rows, d = tok.shape
    dpad = din.shape[1]
    blocks = seq // BLK
    shard = d // 16
    spad = -(-shard // 16) * 16
    lines = -(-(buckets + 2 * -(-d // 128)) // 8) * 8
    bids = jnp.asarray(lane_buckets(buckets))
    one = pl.Buffered(1)
    whole = lambda i, h: (0, 0)
    dma = pltpu.SemaphoreType.DMA
    any_spec = pl.BlockSpec(memory_space=pl.ANY)

    def full(v):
        return pl.BlockSpec(v.shape, whole, pipeline_mode=one)

    return pl.pallas_call(
        functools.partial(tail_kernel, heads, dk, buckets, blocks, extra),
        grid=(blocks, heads),
        in_specs=[
            full(bids),
            pl.BlockSpec((BLK, cols), lambda i, h: (i, 0)),
            full(k),
            full(v),
            pl.BlockSpec((1, 1, seq, BLK), lambda i, h: (h, i, 0, 0)),
            pl.BlockSpec((1, 1, 1, BLK), lambda i, h: (h, i, 0, 0)),
            full(wo),
            full(wof),
            full(ctx),
            full(ctxf),
            full(again),
            full(fgain),
        ]
        + [any_spec] * 7,
        out_specs=[
            any_spec,
            pl.BlockSpec((spad, 4 * cols), whole),
            pl.BlockSpec((lines, 128), whole),
            any_spec,
        ],
        out_shape=[
            jax.ShapeDtypeStruct((rows, d), F32),
            jax.ShapeDtypeStruct((spad, 4 * cols), F32),
            jax.ShapeDtypeStruct((lines, 128), F32),
            jax.ShapeDtypeStruct(far.shape, BF),
        ],
        scratch_shapes=[
            pltpu.VMEM((rows, dpad), F32),
            pltpu.VMEM((rows, d), F32),
            pltpu.VMEM((rows, d), F32),
            pltpu.VMEM((seq, d), BF),
            pltpu.VMEM((d, 3 * cols), BF),
            pltpu.VMEM((rows, d), BF),
            pltpu.VMEM((seq, cols), BF),
            pltpu.VMEM((rows, cols), BF),
            pltpu.VMEM((d, cols), BF),
            pltpu.VMEM((d, cols), BF),
            pltpu.VMEM((1, d), F32),
            pltpu.VMEM((1, d), F32),
            pltpu.VMEM((cols, seq), BF),
            pltpu.VMEM((cols, BLK), F32),
            pltpu.VMEM((seq, BLK), F32),
            pltpu.VMEM((seq, cols), F32),
            pltpu.VMEM((seq, cols), F32),
            pltpu.VMEM((cols, BLK), F32),
            pltpu.VMEM((heads, 7, BLK, BLK), F32),
            pltpu.VMEM((seq, 3 * cols), BF),
            pltpu.VMEM((d, 4 * cols), F32),
            pltpu.VMEM((rows // BLK, BLK, d), BF),
            pltpu.VMEM((rows // BLK, BLK, d), BF),
            pltpu.VMEM((16, spad, 4 * cols), BF),
            pltpu.VMEM((8, spad, 4 * cols), BF),
            pltpu.VMEM((4, spad, 4 * cols), BF),
            pltpu.VMEM((2, spad, 4 * cols), BF),
            pltpu.VMEM((1, spad, 4 * cols), BF),
            pltpu.VMEM((6, lines, 128), F32),
            pltpu.VMEM((5, lines, 128), F32),
            dma((6 + rows // BLK,)),
            dma((3 + rows // BLK,)),
            dma((3 + rows // BLK,)),
            dma((4,)), dma((4,)),
            dma((5,)), dma((5,)),
        ],
        compiler_params=pltpu.CompilerParams(
            vmem_limit_bytes=FF_VMEM, collective_id=1, has_side_effects=True
        ),
        cost_estimate=pl.CostEstimate(
            flops=32 * heads * seq * seq * dk + 8 * seq * d * 3 * cols,
            bytes_accessed=2 * heads * seq * seq + 30 * rows * d,
            transcendentals=0,
        ),
    )(bids, q, k, v, e, inv, wo, wof, ctx, ctxf, again, fgain, din, mid, cot, tok, nrm, wfl, far)


def rms_scale(v, gain):
    return v * lax.rsqrt(jnp.mean(v * v, axis=-1, keepdims=True) + norm_eps) * gain


def take(array, index):
    return lax.dynamic_index_in_dim(array, index, 0, keepdims=False)


def per_device(
    tokens,
    cotangent,
    doc_lengths,
    pad_mask,
    attn_gain,
    qkv_weight,
    rel_table,
    out_weight,
    ff_gain,
    ff_in_weight,
    ff_out_weight,
):
    rows, d = tokens.shape
    n_dp = lax.axis_size("dp")
    n_mp = lax.axis_size("mp")
    seq = rows * n_mp
    cols = qkv_weight.shape[2]
    buckets, heads = rel_table.shape
    dk = cols // heads
    x = lax.axis_index("mp")
    me = lax.axis_index("dp")
    xs = x.astype(jnp.int32).reshape(1)
    bits = n_dp.bit_length() - 1
    shard = d // n_dp
    extra = n_dp // 16
    pad_d = -d % BLK

    def swap(v):
        return lax.ppermute(v, "mp", [(0, 1), (1, 0)])

    def hop(v, mask):
        return lax.ppermute(v, "dp", [(i, i ^ mask) for i in range(n_dp)])

    def after(v, *first):
        return lax.optimization_barrier((v,) + first)[0]

    def bit(b):
        return (me >> b) & 1

    def reduce_rest(parts, low_bits):
        for b in reversed(range(low_bits)):
            halves = [p.reshape((2, p.shape[0] // 2) + p.shape[1:]) for p in parts]
            away = sum(take(p, 1 - bit(b)).astype(F32) for p in halves).astype(BF)
            parts = [take(p, bit(b)) for p in halves] + [hop(away, 1 << b)]
        return sum(p.astype(F32) for p in parts)[0]

    tok_low = tokens.astype(BF)
    tok_far = swap(tok_low)
    w_out_far = swap(after(out_weight, tok_far))
    out_low = cotangent.astype(BF)
    cot_far = swap(after(out_low, tok_far))
    w2 = jnp.pad(jnp.transpose(ff_in_weight, (1, 0, 2)), ((0, 0), (0, pad_d), (0, 0)))
    wo = jnp.pad(ff_out_weight, ((0, pad_d), (0, 0)))
    c_all = jnp.concatenate([out_low, cot_far], axis=0)
    c_t = c_all.T
    c_all = jnp.pad(c_all, ((0, 0), (0, pad_d)))
    wq, wk, wv = (qkv_weight[:, i, :] for i in range(3))

    bounds = jnp.cumsum(doc_lengths[0])
    position = lax.rem(jnp.arange(seq, dtype=jnp.int32) + rows * x, seq)
    doc_of = jnp.sum((position[:, None] >= bounds[None, :]).astype(jnp.int32), axis=1)
    valid = jnp.concatenate(
        [lax.dynamic_slice(pad_mask[0], (rows * x,), (rows,)),
         lax.dynamic_slice(pad_mask[0], (rows * (1 - x),), (rows,))]
    )
    code = jnp.where(valid == 1, doc_of, -1).reshape(seq, 1)
    doc_row = doc_of.reshape(1, seq)

    far = tok_far.astype(F32)
    normed = jnp.concatenate(
        [rms_scale(tokens, attn_gain).astype(BF), rms_scale(far, attn_gain).astype(BF)], axis=0
    )

    def project(w):
        return jnp.dot(normed, w, preferred_element_type=F32).astype(BF)

    q, k, v = project(wq), project(wk), project(wv)
    e, inv, ctx = attn_fwd(xs, rel_table, doc_row, code, q, k, v, heads, dk)
    ctx_far = swap(ctx)
    ctx_far = jnp.concatenate([ctx_far[rows:], ctx_far[:rows]], axis=0)

    def out_proj(r):
        return jnp.einsum("sc,dc->sd", ctx[r], out_weight, preferred_element_type=F32) + jnp.einsum(
            "sc,dc->sd", ctx_far[r], w_out_far, preferred_element_type=F32
        )

    middle = tokens + out_proj(slice(0, rows))
    near_ff = rms_scale(middle, ff_gain).astype(BF)
    far_ff = rms_scale(far + out_proj(slice(rows, seq)), ff_gain).astype(BF)

    x_all = jnp.concatenate([near_ff, far_ff], axis=0)
    grads, din, out_near, out_far = ff_all(
        jnp.pad(x_all, ((0, 0), (0, pad_d))), c_all, x_all.T, c_t, w2, wo, extra
    )
    def finish(g):
        g = g[: d // 16]
        if extra == 1:
            return g
        return reduce_rest([g.reshape(extra, shard, g.shape[1])], extra.bit_length() - 1)

    ffo = finish(grads[0])
    ffi = jnp.stack([finish(grads[1]), finish(grads[2])], axis=1)

    w_flat = jnp.concatenate([wq, wk, wv], axis=1)
    input_grad, last, small, out_back = tail(
        q, k, v, e, inv, out_weight, w_out_far, ctx[:rows], ctx_far[:rows],
        attn_gain.reshape(1, d), ff_gain.reshape(1, d),
        din, middle, cotangent, tokens, normed, w_flat, out_far,
        buckets, heads, dk, extra,
    )
    result = middle + out_near[:, :d] + out_back[:, :d].astype(F32)
    last = finish(last)
    grad_qkv = last[:, : 3 * cols].reshape(shard, 3, cols)
    grad_out = last[:, 3 * cols :]
    for b in range(extra.bit_length() - 1):
        small = small + hop(small, 1 << b)
    lines = -(-d // 128)
    rel_grad = small[:buckets, : heads * n_mp]
    attn_gain_grad = small[buckets : buckets + lines].reshape(-1)[:d]
    ff_gain_grad = small[buckets + lines : buckets + 2 * lines].reshape(-1)[:d]
    return (
        result,
        input_grad,
        attn_gain_grad,
        grad_qkv,
        rel_grad,
        grad_out,
        ff_gain_grad,
        ffi,
        ffo,
    )


def solution(mesh):
    return jax.shard_map(
        per_device,
        mesh=mesh,
        in_specs=(
            P(("dp", "mp"), None),
            P(("dp", "mp"), None),
            P("dp", None),
            P("dp", None),
            P(),
            P(None, None, "mp"),
            P(None, "mp"),
            P(None, "mp"),
            P(),
            P(None, None, "mp"),
            P(None, "mp"),
        ),
        out_specs=(
            P(("dp", "mp"), None),
            P(("dp", "mp"), None),
            P(),
            P("dp", None, "mp"),
            P(),
            P("dp", "mp"),
            P(),
            P("dp", None, "mp"),
            P("dp", "mp"),
        ),
        check_vma=False,
    )
```

profile of v0, /device:TPU:0, one launch (start us, length us, event | category | flops | bytes accessed | tf_op | source)
XLA Modules:
  0.0 409.3 jit_solution(13443615485690564992)
XLA Ops:
  0.6 4.4 %multiply_reduce_fusion.2 = (f32[512]{0:T(512)S(1)}, bf16[512,1472]{0,1:T(8,128)(2,1)}) fusion(f32[512,1472]{0,1:T(8,128)} %param.13), kind=kLoop, calls=%fused_computation.19 | loop fusion | flops 2260480 | bytes 4524032 | tf_op jit(solution)/shard_map/reduce_sum | solution.py:743
  5.0 2.9 collective-permute-start
  8.0 2.4 copy.152.tok_hbm
  10.3 4.3 %convert_element_type.53 = bf16[512,1472]{0,1:T(8,128)(2,1)} convert(f32[512,1472]{0,1:T(8,128)} %param.14) | non-fusion elementwise | flops 753664 | bytes 4521984 | tf_op jit(solution)/shard_map/convert_element_type | solution.py:800
  14.7 3.6 copy.160.cot_hbm
  20.5 7.2 %copy.180 = bf16[1472,2,1792]{2,0,1:T(8,128)(2,1)S(1)} copy(bf16[1472,2,1792]{2,1,0:T(2,128)(2,1)} %param.22) | data formatting | bytes 21102592 | tf_op args[9]
  27.7 4.9 %pad.17.wg_ref.wu_ref = bf16[2,1536,1792]{2,1,0:T(8,128)(2,1)} pad(bf16[2,1472,1792]{2,1,0:T(8,128)(2,1)S(1)} %bitcast.45, bf16[]{:T(256)} %constant.37.clone.1), padding=0_0x0_64x0_0 | pad | bytes 21561346 | tf_op jit(solution)/shard_map/jit(_pad)/pad | solution.py:802
  32.6 2.8 pad.18.wo_hbm
  36.7 2.2 copy.175
  38.9 2.3 copy.176
  41.2 2.2 copy.177
  43.4 2.2 copy.158.wo_ref
  48.7 3.6 pad_maximum_fusion.3.wfl_hbm
  52.3 2.6 copy.142
  56.7 2.2 multiply_convert_fusion.2
  64.4 16.4 %shard_map.196 = (bf16[3,4,1024,256]{3,2,1,0:T(8,128)(2,1)}, f32[3,4,1,256]{3,2,1,0:T(1,128)}, bf16[1024,192]{1,0:T(8,128)(2,1)}) custom-call(s32[1]{0:T(128)} %bitcast.x_ref, f32[32,3]{1,0:T(8,128)} %copy.149.rel_ref, s32[1,1536]{1,0:T(1,128)} %constant.38.clone.bid_ref, s32[1,1024]{1,0:T(1,128)} %bitcast.53, s32[1024,1]{1,0:T(8,128)} %broadcast_select_fusion.code_ref, ...), custom_call_target="tpu_custom_call" | custom-call | flops 3221225472 | bytes 7864320 | tf_op jit(solution)/shard_map/pallas_call | solution.py:119
  82.5 2.0 collective-permute-start.2
  87.8 9.5 %collective-permute-done.1 = bf16[1024,192]{1,0:T(8,128)(2,1)S(1)} collective-permute-done((bf16[1024,192]{1,0:T(8,128)(2,1)S(1)}, bf16[1024,192]{1,0:T(8,128)(2,1)S(1)}, u32[]{:S(2)}, u32[]{:S(2)}) %collective-permute-start.1) | collective-permute-done | bytes 393248 | tf_op jit(solution)/shard_map/ppermute | solution.py:779
  98.1 11.9 %collective-permute-done.2 = bf16[1472,192]{0,1:T(8,128)(2,1)S(1)} collective-permute-done((bf16[1472,192]{0,1:T(8,128)(2,1)S(1)}, bf16[1472,192]{0,1:T(8,128)(2,1)S(1)}, u32[]{:S(2)}, u32[]{:S(2)}) %collective-permute-start.2) | collective-permute-done | bytes 565280 | tf_op jit(solution)/shard_map/ppermute | solution.py:779
  113.5 1.9 pad.15.x_ref
  115.5 2.9 copy.157.xt_ref
  118.3 2.2 copy.159.wof_ref
  120.6 20.4 %collective-permute-done.3 = bf16[512,1472]{0,1:T(8,128)(2,1)} collective-permute-done((bf16[512,1472]{0,1:T(8,128)(2,1)}, bf16[512,1472]{0,1:T(8,128)(2,1)}, u32[]{:S(2)}, u32[]{:S(2)}) %collective-permute-start.3) | collective-permute-done | bytes 1507360 | tf_op jit(solution)/shard_map/ppermute | solution.py:779
  140.9 5.3 %fusion.17 = (bf16[1472,1024]{1,0:T(8,128)(2,1)}, bf16[1024,1472]{0,1:T(8,128)(2,1)}) fusion(bf16[512,1472]{0,1:T(8,128)(2,1)} %collective-permute-done.3, bf16[512,1472]{0,1:T(8,128)(2,1)} %convert_element_type.53), kind=kLoop, calls=%fused_computation.54 | loop fusion | flops 6029312 | bytes 9043968 | tf_op jit(solution)/shard_map/transpose | solution.py:805
  146.2 3.2 copy.178
  149.4 2.0 pad.16.clone.c_ref
  151.3 125.6 %shard_map.197 = (f32[3,96,1792]{2,1,0:T(8,128)}, f32[512,1536]{1,0:T(8,128)}, f32[512,1536]{1,0:T(8,128)}, bf16[512,1536]{1,0:T(8,128)(2,1)}) custom-call(bf16[1024,1536]{1,0:T(8,128)(2,1)} %pad.15.x_ref, bf16[1024,1536]{1,0:T(8,128)(2,1)} %pad.16.clone.c_ref, bf16[1472,1024]{1,0:T(8,128)(2,1)} %copy.157.xt_ref, ...), custom_call_target="tpu_custom_call" | custom-call | flops 48620371968 | bytes 39944192 | tf_op jit(solution)/shard_map/pallas_call | solution.py:361
  276.9 113.7 %shard_map.198 = (f32[512,1472]{1,0:T(8,128)}, f32[96,768]{1,0:T(8,128)}, f32[56,128]{1,0:T(8,128)}, bf16[512,1536]{1,0:T(8,128)(2,1)}) custom-call(s32[1,1536]{1,0:T(1,128)} %constant.38.clone.bid_ref, bf16[1024,192]{1,0:T(8,128)(2,1)} %convolution_convert_fusion.2.q_ref, bf16[1024,192]{1,0:T(8,128)(2,1)} %convolution_convert_fusion.1.k_ref, ...), custom_call_target="tpu_custom_call" | custom-call | flops 13388218368 | bytes 28901376 | tf_op jit(solution)/shard_map/pallas_call | solution.py:664
  395.4 2.6 slice_bitcast_fusion
  398.1 2.1 copy.167
  401.6 2.3 copy.163
  403.9 3.5 copy.164
  (79 shorter events, 31.0 us)
Async XLA Ops:
  5.0 47.3 %collective-permute-start = (bf16[512,1472]{0,1:T(8,128)(2,1)}, bf16[512,1472]{0,1:T(8,128)(2,1)}, u32[]{:S(2)}, u32[]{:S(2)}) collective-permute-start(bf16[512,1472]{0,1:T(8,128)(2,1)} %get-tuple-element.85), channel_id=1, source_target_pairs={{0,1},{1,0},{2,3},{3,2},{4,5},{5,4},{6,7},{7,6},{8,9},{9,8},{10,11... | collective-permute-start | bytes 4521992 | tf_op jit(solution)/shard_map/ppermute | solution.py:779
  10.3 99.7 %copy-start = (f32[512,1472]{1,0:T(8,128)}, f32[512,1472]{1,0:T(8,128)S(1)}, u32[]{:S(2)}) copy-start(f32[512,1472]{1,0:T(8,128)S(1)} %copy.152.tok_hbm) | copy-start | bytes 9043972
  14.6 3.6 copy-start.14
  14.7 3.9 copy-start.16
  14.7 5.2 %copy-start.15 = (f32[32,3]{0,1:T(4,128)S(1)}, f32[32,3]{0,1:T(4,128)}, u32[]{:S(2)}) copy-start(f32[32,3]{0,1:T(4,128)} %param.19) | copy-start | bytes 1156
  18.8 8.9 %copy-start.13 = (s32[1024]{0:T(1024)}, s32[1024]{0:T(1024)S(1)}, u32[]{:S(2)}) copy-start(s32[1024]{0:T(1024)S(1)} %convert_reduce_fusion) | copy-start | bytes 12292
  20.5 12.1 %slice-start = ((s8[5275648]{0:T(1024)(128)(4,1)}), s8[4194304]{0:T(1024)(128)(4,1)S(1)}, s32[]{:S(2)}) async-start(s8[5275648]{0:T(1024)(128)(4,1)} %bitcast.46), calls=%async_computation | async-start | bytes 8388608
  27.7 4.9 %slice-start.1 = ((s8[5275648]{0:T(1024)(128)(4,1)}), s8[1081344]{0:T(1024)(128)(4,1)S(1)}, s32[]{:S(2)}) async-start(s8[5275648]{0:T(1024)(128)(4,1)} %bitcast.46), calls=%async_computation.1 | async-start | bytes 2162688
  32.6 2.8 copy-start.7
  36.7 8.9 %copy-start.11 = (f32[1472]{0:T(1024)S(1)}, f32[1472]{0:T(1024)}, u32[]{:S(2)}) copy-start(f32[1472]{0:T(1024)} %param.21) | copy-start | bytes 17668
  36.7 9.5 %copy-start.12 = (f32[1472]{0:T(1024)S(1)}, f32[1472]{0:T(1024)}, u32[]{:S(2)}) copy-start(f32[1472]{0:T(1024)} %param.17) | copy-start | bytes 17668
  56.7 2.3 copy-start.8
  64.4 16.5 %copy-start.5 = (bf16[1472,192]{0,1:T(8,128)(2,1)S(1)}, bf16[1472,192]{0,1:T(8,128)(2,1)}, u32[]{:S(2)}) copy-start(bf16[1472,192]{0,1:T(8,128)(2,1)} %param.20) | copy-start | bytes 1695748
  80.9 1.6 copy-start.10
  82.4 14.9 %collective-permute-start.1 = (bf16[1024,192]{1,0:T(8,128)(2,1)S(1)}, bf16[1024,192]{1,0:T(8,128)(2,1)S(1)}, u32[]{:S(2)}, u32[]{:S(2)}) collective-permute-start(bf16[1024,192]{1,0:T(8,128)(2,1)S(1)} %copy-done.10), channel_id=1, source_target_pairs={{0,1},{1,0},{2,3},{3,2},{4,5},{5,4},{6,7},{7,6},{8,9},{9,8},{10,11... | collective-permute-start | bytes 1179656 | tf_op jit(solution)/shard_map/ppermute | solution.py:779
  82.5 27.5 %collective-permute-start.2 = (bf16[1472,192]{0,1:T(8,128)(2,1)S(1)}, bf16[1472,192]{0,1:T(8,128)(2,1)S(1)}, u32[]{:S(2)}, u32[]{:S(2)}) collective-permute-start(bf16[1472,192]{0,1:T(8,128)(2,1)S(1)} %copy-done.5), channel_id=1, source_target_pairs={{0,1},{1,0},{2,3},{3,2},{4,5},{5,4},{6,7},{7,6},{8,9},{9,8},{10,11... | collective-permute-start | bytes 1695752 | tf_op jit(solution)/shard_map/ppermute | solution.py:779
  85.8 55.1 %collective-permute-start.3 = (bf16[512,1472]{0,1:T(8,128)(2,1)}, bf16[512,1472]{0,1:T(8,128)(2,1)}, u32[]{:S(2)}, u32[]{:S(2)}) collective-permute-start(bf16[512,1472]{0,1:T(8,128)(2,1)} %convert_element_type.53), channel_id=1, source_target_pairs={{0,1},{1,0},{2,3},{3,2},{4,5},{5,4},{6,7},{7,6},{8,9},{9,8},{10,11... | collective-permute-start | bytes 4521992 | tf_op jit(solution)/shard_map/ppermute | solution.py:779
  98.1 12.8 %copy-start.3 = (bf16[512,1472]{1,0:T(8,128)(2,1)S(1)}, bf16[512,1472]{1,0:T(8,128)(2,1)}, u32[]{:S(2)}) copy-start(bf16[512,1472]{1,0:T(8,128)(2,1)} %copy.142) | copy-start | bytes 4521988
  110.0 0.8 copy-start.4
  110.9 1.6 copy-start.1
  395.4 4.8 %copy-start.6 = (f32[512,1536]{1,0:T(8,128)S(1)}, f32[512,1536]{1,0:T(8,128)}, u32[]{:S(2)}) copy-start(f32[512,1536]{1,0:T(8,128)} %get-tuple-element.25) | copy-start | bytes 9437188
  398.0 2.2 copy-start.2
  398.0 2.8 copy-start.9
where the time goes:
time: 413 us; the launch traced here: 409 us
  Pallas kernels  256 us (62%)
  local copies, waits for them, and re-layouts  68.7 us (17%)
  waiting for transfers between devices  41.8 us (10%)
  other arithmetic  27.6 us (7%)
  matrix products  9.26 us (2%)
  starting transfers between devices  5.1 us (1%)
    pallas_call x1, Pallas kernels, ff_all(): pl.pallas_call(functools.partial(ff_kernel, steps, extra), grid=(steps,),...  126 us
    pallas_call x1, Pallas kernels, tail(): pl.pallas_call(functools.partial(tail_kernel, heads, dk, buckets, blocks,...  114 us
    ppermute x4, waiting for transfers between devices, swap(): return lax.ppermute(v, 'mp', [(0, 1), (1, 0)])  41.8 us
    unnamed x52, local copies, waits for them, and re-layouts  36.7 us
    pallas_call x1, Pallas kernels, attn_fwd(): pl.pallas_call(functools.partial(attn_fwd_kernel, heads, dk, buckets, blo...  16.4 us
  transfers between devices with their start and end apart: 4, of which 3 were waited for; matrix products, arithmetic and copies ran while one was open for 14% of the time, Pallas kernels for 0%

commit v1 on v0

v1 whole, which is shorter than its diff:
```python
import functools

import jax
import jax.numpy as jnp
import numpy as np
from jax import lax
from jax.experimental import pallas as pl
from jax.experimental.pallas import tpu as pltpu
from jax.sharding import PartitionSpec as P

MAXDIST = 128
norm_eps = 1e-06
BLK = 256
SPAN = 6 * BLK
REACH = 2
BF = jnp.bfloat16
F32 = jnp.float32
FF_VMEM = 63 << 20
FF_DONE = 3


def bucket_of(offsets, buckets, reach):
    half_range = buckets // 2
    upper_half = (offsets > 0).astype(np.int32) * half_range
    distance = np.abs(offsets)
    exact_range = half_range // 2
    safe_dist = np.maximum(distance, 1)
    log_bucket = exact_range + (
        np.log(safe_dist / exact_range) / np.log(reach / exact_range) * (half_range - exact_range)
    ).astype(np.int32)
    log_bucket = np.minimum(log_bucket, half_range - 1)
    return (upper_half + np.where(distance < exact_range, distance, log_bucket)).astype(np.int32)


def lane_buckets(buckets):
    lanes = np.arange(SPAN)
    shifted = np.where(lanes < 5 * BLK, lanes, lanes - SPAN)
    return bucket_of(REACH * BLK - shifted, buckets, MAXDIST).reshape(1, SPAN)


def dot(a, b, contract):
    return lax.dot_general(a, b, (contract, ((), ())), preferred_element_type=F32)


def flip(index, mask):
    out = index
    bit = 1
    while bit <= mask:
        if mask & bit:
            out = out + bit * (1 - 2 * (index // bit % 2))
        bit *= 2
    return out


GROUP_MASKS = (1, 2, 4, 12)


def group_coords(g):
    b = [g // (1 << i) % 2 for i in range(4)]
    return [b[0], b[1], (b[2] + b[3]) % 2, b[3]]


def block_position(k):
    b = [k >> i & 1 for i in range(4)]
    c = [b[0], b[1], b[2] ^ b[3], b[3]]
    return c[0] * 8 + c[1] * 4 + c[2] * 2 + c[3]


def column(line):
    return jnp.broadcast_to(line, (8, line.shape[1])).T[:, 0:1]


def norm_scale(v):
    return lax.rsqrt(jnp.mean(v * v, axis=0, keepdims=True) + norm_eps)


def lanes(block):
    return pl.ds(pl.multiple_of(block * BLK, BLK), BLK)


def remote(src, dst, send, recv, who):
    return pltpu.make_async_remote_copy(
        src_ref=src,
        dst_ref=dst,
        send_sem=send,
        recv_sem=recv,
        device_id=who,
        device_id_type=pl.DeviceIdType.MESH,
    )


def meet(devices):
    barrier = pltpu.get_barrier_semaphore()
    for who in devices:
        pl.semaphore_signal(barrier, inc=1, device_id=who, device_id_type=pl.DeviceIdType.MESH)
    pl.semaphore_wait(barrier, len(devices))


def front_kernel(
    heads, dk, buckets, blocks,
    rel_ref, len_ref, bid_ref, pad_ref, ag_ref, fg_ref, wq_ref, wo_ref,
    tok_hbm, far_hbm, cot_hbm,
    e_ref, inv_ref, qkv_ref, ctx_hbm, nrm_hbm, xt_hbm, mid_hbm, ct_hbm, wall_hbm,
    f1, fb, f3, cl, nrm, table, padc, mask, score, agc, fgc, wall, wn, call, xo,
    lsem, osem, wsend, wrecv, csend, crecv,
):
    qb, h = pl.program_id(0), pl.program_id(1)
    dp, x = lax.axis_index("dp"), lax.axis_index("mp")
    d, rows = f1.shape
    cols = heads * dk
    half = cols // 2
    core = dp % 2
    other = (dp, 1 - x)
    sibling = (dp + 1 - 2 * core, x)
    near_blocks = blocks // 2
    part = pl.ds(core * half, half)
    far_part = pl.ds(cols + core * half, half)

    def local(i):
        src, dst = ((tok_hbm, f1), (far_hbm, fb), (cot_hbm, f3))[i]
        return pltpu.make_async_copy(src, dst, lsem.at[i])

    def out(i):
        src, dst = (
            (call, ctx_hbm), (nrm, nrm_hbm), (f1, mid_hbm), (cl, ct_hbm.at[:, pl.ds(0, rows)]), (wall, wall_hbm)
        )[i]
        return pltpu.make_async_copy(src, dst, osem.at[i])

    def xt_out(b):
        return pltpu.make_async_copy(xo.at[:, lanes(b)], xt_hbm.at[:, lanes(b)], osem.at[5 + b])

    w_copy = remote(wo_ref.at[part], wall.at[far_part], wsend.at[0], wrecv.at[0], other)
    w_pass = remote(wall.at[far_part], wall.at[far_part], wsend.at[1], wrecv.at[1], sibling)
    c_copy = remote(cl.at[:, pl.ds(0, BLK)], ct_hbm.at[:, pl.ds(rows, BLK)], wsend.at[2], wrecv.at[2], other)

    def ctx_copy(b):
        there = (b + near_blocks) % blocks
        return remote(
            call.at[pl.ds(0, cols), lanes(b)], call.at[pl.ds(cols, cols), lanes(there)],
            csend.at[b], crecv.at[b], other,
        )

    @pl.when((qb == 0) & (h == 0))
    def _():
        for i in (2, 0, 1):
            local(i).start()
        meet([other, sibling])
        w_copy.start()
        wall[0:cols, :] = wo_ref[...]
        local(2).wait()
        cl[...] = f3[...].astype(BF)
        c_copy.start()
        out(3).start()
        agc[...] = column(ag_ref[...])
        fgc[...] = column(fg_ref[...])
        local(0).wait()
        local(1).wait()
        for b in range(blocks):
            ls = slice(b * BLK, (b + 1) * BLK)
            v = f1[:, ls] if b < near_blocks else fb[:, b * BLK - rows : (b + 1) * BLK - rows].astype(F32)
            nrm[:, ls] = (v * norm_scale(v) * agc[...]).astype(BF)
            qkv_ref[:, ls] = dot(wq_ref[...], nrm[:, ls], ((1,), (0,))).astype(BF)
        out(1).start()
        for i in range(2):
            start = (1 - x) * rows if i else x * rows
            line = pad_ref[:, pl.ds(pl.multiple_of(start, BLK), rows)].astype(F32)
            padc[i * rows : (i + 1) * rows, :] = jnp.broadcast_to(line, (8, rows)).T
        ids = bid_ref[...]
        for hh in range(heads):
            line = jnp.zeros((1, SPAN), F32)
            for b in range(buckets):
                line = jnp.where(ids == b, rel_ref[b, hh], line)
            turned = pltpu.roll(
                jnp.broadcast_to(line, (BLK, SPAN)), 0, 1, stride=1, stride_axis=0
            )
            for i in range(7):
                g = min(max(i - 1, 0), 4)
                table[hh, i] = turned[:, BLK * (4 - g) : BLK * (5 - g)]

    @pl.when((qb == 1) & (h == 0))
    def _():
        w_copy.wait()
        w_pass.start()

    q_true = (qb + near_blocks * x) % blocks

    @pl.when(h == 0)
    def _():
        q_pos = q_true * BLK + lax.broadcasted_iota(jnp.int32, (1, BLK), 1)
        k_iota = lax.broadcasted_iota(jnp.int32, (BLK, BLK), 0)
        for kb in range(blocks):
            k_pos = (kb + near_blocks * x) % blocks * BLK + k_iota
            bound = 0
            q_doc = jnp.zeros((1, BLK), jnp.int32)
            k_doc = jnp.zeros((BLK, BLK), jnp.int32)
            for i in range(len_ref.shape[1]):
                bound = bound + len_ref[0, i]
                q_doc = q_doc + (q_pos >= bound).astype(jnp.int32)
                k_doc = k_doc + (k_pos >= bound).astype(jnp.int32)
            krows = slice(kb * BLK, (kb + 1) * BLK)
            seen = (padc[krows, 0:1] > 0.5) | (k_pos == q_pos)
            mask[krows, :] = jnp.where((k_doc == q_doc) & seen, 0.0, -1000000000.0)

    def head_rows(group):
        return pl.ds(pl.multiple_of(group * cols + h * dk, dk), dk)

    qh = qkv_ref[head_rows(0), lanes(qb)]
    peak = None
    for kb in range(blocks):
        krows = slice(kb * BLK, (kb + 1) * BLK)
        s = dot(qkv_ref[head_rows(1), krows], qh, ((0,), (0,)))
        diag = (kb + near_blocks * x) % blocks - q_true + blocks - 1
        s = s + table[h, diag] + mask[krows, :]
        score[krows, :] = s
        top = jnp.max(s, axis=0, keepdims=True)
        peak = top if peak is None else jnp.maximum(peak, top)
    total = jnp.zeros((1, BLK), F32)
    ctx = jnp.zeros((dk, BLK), F32)
    for kb in range(blocks):
        krows = slice(kb * BLK, (kb + 1) * BLK)
        e = jnp.exp(score[krows, :] - peak)
        total = total + jnp.sum(e, axis=0, keepdims=True)
        e_low = e.astype(BF)
        e_ref[0, 0, krows, :] = e_low
        ctx = ctx + dot(qkv_ref[head_rows(2), krows], e_low, ((1,), (0,)))
    inv = 1.0 / total
    inv_ref[0, 0] = inv
    call[head_rows(0), lanes(qb)] = (ctx * inv).astype(BF)

    @pl.when(h == heads - 1)
    def _():
        ctx_copy(qb).start()

    @pl.when((h == heads - 1) & (qb == blocks - 1))
    def _():
        w_pass.wait()
        wn[...] = wall[...].astype(F32).T.astype(BF)
        out(4).start()
        for i in range(blocks):
            b = (i + near_blocks) % blocks
            ctx_copy(i).wait()
            ls = slice(b * BLK, (b + 1) * BLK)
            v = dot(wn[...], call[:, ls], ((1,), (0,)))
            if b < near_blocks:
                v = v + f1[:, ls]
                f1[:, ls] = v
            else:
                v = v + fb[:, b * BLK - rows : (b + 1) * BLK - rows].astype(F32)
            xo[:, ls] = (v * norm_scale(v) * fgc[...]).astype(BF)
            xt_out(b).start()
        out(0).start()
        out(2).start()
        c_copy.wait()
        for i in range(5):
            out(i).wait()
        for b in range(blocks):
            xt_out(b).wait()


def front(rel, lengths, pad, again, fgain, wq, wo, tok, far, cot, heads, dk):
    d, rows = tok.shape
    seq = 2 * rows
    cols = heads * dk
    blocks = seq // BLK
    buckets = rel.shape[0]
    bids = jnp.asarray(lane_buckets(buckets))
    one = pl.Buffered(1)
    dma = pltpu.SemaphoreType.DMA
    any_spec = pl.BlockSpec(memory_space=pl.ANY)
    smem = pl.BlockSpec(memory_space=pltpu.SMEM)

    def full(v):
        return pl.BlockSpec(v.shape, lambda i, h: (0, 0), pipeline_mode=one)

    return pl.pallas_call(
        functools.partial(front_kernel, heads, dk, buckets, blocks),
        grid=(blocks, heads),
        in_specs=[smem, smem, full(bids), full(pad), full(again), full(fgain), full(wq), full(wo)]
        + [any_spec] * 3,
        out_specs=[
            pl.BlockSpec((1, 1, seq, BLK), lambda i, h: (h, i, 0, 0)),
            pl.BlockSpec((1, 1, 1, BLK), lambda i, h: (h, i, 0, 0)),
            pl.BlockSpec((3 * cols, seq), lambda i, h: (0, 0)),
        ]
        + [any_spec] * 6,
        out_shape=[
            jax.ShapeDtypeStruct((heads, blocks, seq, BLK), BF),
            jax.ShapeDtypeStruct((heads, blocks, 1, BLK), F32),
            jax.ShapeDtypeStruct((3 * cols, seq), BF),
            jax.ShapeDtypeStruct((2 * cols, seq), BF),
            jax.ShapeDtypeStruct((d, seq), BF),
            jax.ShapeDtypeStruct((d, seq), BF),
            jax.ShapeDtypeStruct((d, rows), F32),
            jax.ShapeDtypeStruct((d, seq), BF),
            jax.ShapeDtypeStruct((2 * cols, d), BF),
        ],
        scratch_shapes=[
            pltpu.VMEM((d, rows), F32),
            pltpu.VMEM((d, rows), BF),
            pltpu.VMEM((d, rows), F32),
            pltpu.VMEM((d, rows), BF),
            pltpu.VMEM((d, seq), BF),
            pltpu.VMEM((heads, 7, BLK, BLK), F32),
            pltpu.VMEM((seq, 8), F32),
            pltpu.VMEM((seq, BLK), F32),
            pltpu.VMEM((seq, BLK), F32),
            pltpu.VMEM((d, 1), F32),
            pltpu.VMEM((d, 1), F32),
            pltpu.VMEM((2 * cols, d), BF),
            pltpu.VMEM((d, 2 * cols), BF),
            pltpu.VMEM((2 * cols, seq), BF),
            pltpu.VMEM((d, seq), BF),
            dma((3,)), dma((5 + blocks,)), dma((3,)), dma((3,)), dma((blocks,)), dma((blocks,)),
        ],
        compiler_params=pltpu.CompilerParams(
            vmem_limit_bytes=FF_VMEM, collective_id=2, has_side_effects=True
        ),
        cost_estimate=pl.CostEstimate(
            flops=16 * heads * seq * seq * dk + 10 * seq * d * cols,
            bytes_accessed=2 * heads * seq * seq + 30 * rows * d,
            transcendentals=heads * seq * seq,
        ),
    )(rel, lengths, bids, pad, again, fgain, wq, wo, tok, far, cot)


def ff_kernel(
    steps, done, extra,
    xt_ref, wg_ref, wu_ref, ct_hbm, wo_hbm,
    grads_ref, din_hbm, near_hbm, far_hbm, hand_hbm,
    ct, wo, hid, dg, du, din, stage, r1, r2, r3, r4, xs, xr, of, nf,
    csem, wo_sem, s1, s2, s3, s4, t1, t2, t3, t4, xsem, osem, hsem,
):
    i = pl.program_id(0)
    phase, j = i // steps, i % steps
    f, total = hid.shape
    rows = total // 2
    d = xt_ref.shape[0]
    shard = d // 16
    dp, mp = lax.axis_index("dp"), lax.axis_index("mp")
    a = group_coords(dp // extra)
    peers = [flip(dp, m * extra) for m in GROUP_MASKS]
    other = (dp, 1 - mp)
    bufs = (r1, r2, r3, r4)
    sends, recvs = (s1, s2, s3, s4), (t1, t2, t3, t4)
    end = steps - 1

    def wo_copy(n):
        return pltpu.make_async_copy(wo_hbm.at[:, lanes(n)], wo.at[:, lanes(n)], wo_sem.at[n])

    def c_local(n):
        size = (BLK, rows)[n]
        part = pl.ds((rows, 0)[n], size)
        return pltpu.make_async_copy(ct_hbm.at[:, part], ct.at[:, part], csem.at[n])

    c_far = remote(
        ct_hbm.at[:, pl.ds(BLK, BLK)], ct.at[:, pl.ds(rows + BLK, BLK)], csem.at[2], csem.at[3], other
    )

    def hop(level, s, w):
        half = 8 >> level
        away = pl.ds((1 - a[level]) * half, half)
        src = stage.at[w, away] if level == 0 else bufs[level - 1].at[s, away]
        return remote(src, bufs[level].at[s], sends[level].at[s], recvs[level].at[s], (peers[level], mp))

    def hand_copy(s):
        return pltpu.make_async_copy(r1.at[s], hand_hbm.at[s - 3 * done], hsem.at[s - 3 * done])

    def absorb(level, step, w):
        s = step * 3 + w
        half = 8 >> level
        copy = hop(level, s, w)
        copy.wait_recv()
        copy.wait_send()
        keep = pl.ds(a[level] * half, half)
        kept = stage[w, keep] if level == 0 else bufs[level - 1][s, keep]
        both = kept.astype(F32) + bufs[level][s].astype(F32)
        if level == 3:
            grads_ref[w, :, lanes(step)] = both[0]
            return
        bufs[level][s] = both.astype(BF)
        if level > 0:
            hop(level + 1, s, w).start()
            return
        if isinstance(step, int):
            hand_copy(s).start()
            return

        @pl.when(step < done)
        def _():
            hop(1, s, w).start()

        @pl.when(step >= done)
        def _():
            hand_copy(s).start()

    def absorb_step(level, step):
        def one(w, carry):
            absorb(level, step, w)
            return carry

        lax.fori_loop(0, 3, one, 0)

    @pl.when(i == 0)
    def _():
        meet([(p, mp) for p in peers] + [other])
        c_far.start()
        c_local(0).start()
        for n in range(steps):
            wo_copy(n).start()
        c_local(1).start()
        din[...] = jnp.zeros_like(din)
        stage[...] = jnp.zeros_like(stage)
        c_local(0).wait()

    @pl.when(phase == 0)
    def _():
        wo_copy(j).wait()

    @pl.when(i == steps)
    def _():
        c_far.wait()

    scale = np.float32(np.sqrt(2 / np.pi))
    frows = lanes(j)

    def block(tok, acc):
        gate = dot(wg_ref[...], xt_ref[:, tok], ((0,), (0,)))
        up = dot(wu_ref[...], xt_ref[:, tok], ((0,), (0,)))
        dh = dot(wo[:, frows], ct[:, tok], ((0,), (0,)))
        sq = gate * gate
        t = jnp.tanh(scale * gate * (1.0 + 0.044715 * sq))
        half = 0.5 * (1.0 + t)
        act = gate * half
        slope = half + 0.5 * gate * (1.0 - t * t) * (scale * (1.0 + (3 * 0.044715) * sq))
        hid[frows, tok] = (act * up).astype(BF)
        dgr = (dh * (up * slope)).astype(BF)
        dur = (dh * act).astype(BF)
        dg[frows, tok] = dgr
        du[frows, tok] = dur
        din[:, acc] += dot(wg_ref[...], dgr, ((1,), (0,))) + dot(wu_ref[...], dur, ((1,), (0,)))

    x_copy = remote(xs, xr, xsem.at[0], xsem.at[1], other)

    @pl.when(phase < 2)
    def _():
        block(lanes(phase + rows // BLK), lanes(phase))

    @pl.when(i == 2 * steps - 1)
    def _():
        xs[...] = din[...].astype(BF)
        x_copy.start()
        din[...] = jnp.zeros_like(din)
        c_local(1).wait()

    per = 4 * shard

    @pl.when(phase == 2)
    def _():
        for n in range(rows // BLK):
            block(pl.ds(n * BLK, BLK), pl.ds(n * BLK, BLK))

        @pl.when(j > 0)
        def _():
            absorb(0, j - 1, 2)

        for w in range(3):
            right = (hid, dg, du)[w][frows, :]
            for q in range(4):
                rs = slice(q * per, (q + 1) * per)
                left = ct[rs, :] if w == 0 else xt_ref[rs, :]
                part = dot(left, right, ((1,), (1,)))
                for k in range(4):
                    stage[w, block_position(4 * q + k), 0:shard, :] = part[
                        k * shard : (k + 1) * shard
                    ].astype(BF)
            hop(0, j * 3 + w, w).start()
            if w > 0:
                absorb(0, j, w - 1)

        for when, events in ((3, ((1, 0),)), (5, ((1, 1), (2, 0))), (6, ((3, 0),))):
            @pl.when(j == when)
            def _():
                for level, step in events:
                    absorb_step(level, step)

    @pl.when(i == 3 * steps - 1)
    def _():
        absorb(0, end, 2)

        def out_part(n):
            return dot(wo[...], hid[:, n * BLK : (n + 1) * BLK], ((1,), (0,)))

        half = rows // BLK
        for n in range(half):
            of[:, n * BLK : (n + 1) * BLK] = out_part(half + n).astype(BF)
        far_copy = pltpu.make_async_copy(of, far_hbm, osem.at[0])
        far_copy.start()
        absorb_step(1, 2)
        absorb_step(2, 1)
        x_copy.wait()
        din[...] += xr[...].astype(F32)
        din_copy = pltpu.make_async_copy(din, din_hbm, osem.at[2])
        din_copy.start()
        nf[:, 0:BLK] = out_part(0)
        absorb_step(2, 2)
        absorb_step(3, 1)
        for n in range(1, half):
            nf[:, n * BLK : (n + 1) * BLK] = out_part(n)
        near_copy = pltpu.make_async_copy(nf, near_hbm, osem.at[1])
        near_copy.start()
        absorb_step(3, 2)

        def flush(s, carry):
            hand_copy(s).wait()
            return carry

        lax.fori_loop(3 * done, 3 * steps, flush, 0)
        far_copy.wait()
        near_copy.wait()
        din_copy.wait()


def ff_all(xt, ct, w2, wo, extra):
    d, total = xt.shape
    f = wo.shape[1]
    rows = total // 2
    steps = f // BLK
    done = FF_DONE
    chunks = 3 * steps
    kept = 3 * done
    shard = d // 16
    spad = -(-shard // 16) * 16
    dma = pltpu.SemaphoreType.DMA
    any_spec = pl.BlockSpec(memory_space=pl.ANY)
    return pl.pallas_call(
        functools.partial(ff_kernel, steps, done, extra),
        grid=(3 * steps,),
        in_specs=[
            pl.BlockSpec((d, total), lambda i: (0, 0), pipeline_mode=pl.Buffered(1)),
            pl.BlockSpec((None, d, BLK), lambda i: (0, 0, i % steps)),
            pl.BlockSpec((None, d, BLK), lambda i: (1, 0, i % steps)),
            any_spec,
            any_spec,
        ],
        out_specs=[pl.BlockSpec((3, spad, done * BLK), lambda i: (0, 0, 0))] + [any_spec] * 4,
        out_shape=[
            jax.ShapeDtypeStruct((3, spad, done * BLK), F32),
            jax.ShapeDtypeStruct((d, rows), F32),
            jax.ShapeDtypeStruct((d, rows), F32),
            jax.ShapeDtypeStruct((d, rows), BF),
            jax.ShapeDtypeStruct((chunks - kept, 8, spad, BLK), BF),
        ],
        scratch_shapes=[
            pltpu.VMEM((d, total), BF),
            pltpu.VMEM((d, f), BF),
            pltpu.VMEM((f, total), BF),
            pltpu.VMEM((f, total), BF),
            pltpu.VMEM((f, total), BF),
            pltpu.VMEM((d, rows), F32),
            pltpu.VMEM((3, 16, spad, BLK), BF),
            pltpu.VMEM((chunks, 8, spad, BLK), BF),
            pltpu.VMEM((kept, 4, spad, BLK), BF),
            pltpu.VMEM((kept, 2, spad, BLK), BF),
            pltpu.VMEM((kept, 1, spad, BLK), BF),
            pltpu.VMEM((d, rows), BF),
            pltpu.VMEM((d, rows), BF),
            pltpu.VMEM((d, rows), BF),
            pltpu.VMEM((d, rows), F32),
            dma((4,)),
            dma((steps,)),
            dma((chunks,)), dma((kept,)), dma((kept,)), dma((kept,)),
            dma((chunks,)), dma((kept,)), dma((kept,)), dma((kept,)),
            dma((2,)),
            dma((3,)),
            dma((chunks - kept,)),
        ],
        compiler_params=pltpu.CompilerParams(
            vmem_limit_bytes=FF_VMEM, collective_id=0, has_side_effects=True
        ),
        cost_estimate=pl.CostEstimate(
            flops=18 * total * d * f,
            bytes_accessed=6 * d * f + 16 * total * d,
            transcendentals=total * f,
        ),
    )(xt, w2, w2, ct, wo)


def tail_kernel(
    heads, dk, buckets, blocks, extra, later,
    bid_ref, qkv_ref, e_ref, inv_ref, wall_ref, ctx_ref, wq_ref, ag_ref, fg_ref,
    din_hbm, mid_hbm, cot_hbm, tok_hbm, nrm_hbm, far_hbm, hand_hbm,
    ig_hbm, g_ref, small_ref, grads_ref, back_hbm,
    f1, f2, f3, nrm, wn, alow, dctx, dcs, osend, orecv, gsum, fsum, agc, fgc,
    dp_s, dkv, tally, dproj, grad, dns, dnr,
    stage, t1, t2, t3, t4, hk, h2, h3, h4, sb, rb,
    lsem, ksem, xs_sem, xr_sem, cs_sem, cr_sem, bs_sem, br_sem, hs2, hs3, hs4, hr2, hr3, hr4,
):
    qb, h = pl.program_id(0), pl.program_id(1)
    step_id = qb * heads + h
    dp, x = lax.axis_index("dp"), lax.axis_index("mp")
    d, rows = f2.shape
    seq = 2 * rows
    cols = heads * dk
    shard = d // 16
    a = group_coords(dp // extra)
    peers = [flip(dp, m * extra) for m in GROUP_MASKS]
    other = (dp, 1 - x)
    bufs = (stage, t1, t2, t3, t4)
    hbufs = (None, hk, h2, h3, h4)
    hsends, hrecvs = (None, hs2, hs3, hs4), (None, hr2, hr3, hr4)
    near_blocks = blocks // 2

    def local(i):
        src, dst = ((din_hbm, f1), (mid_hbm, f2), (cot_hbm, f3), (tok_hbm, f2), (nrm_hbm, nrm))[i]
        return pltpu.make_async_copy(src, dst, lsem.at[i])

    dctx_copy = remote(dcs, dctx.at[:, pl.ds(rows, rows)], xs_sem.at[0], xr_sem.at[0], other)
    o_copy = remote(osend, orecv, xs_sem.at[1], xr_sem.at[1], other)
    back_copy = remote(far_hbm, back_hbm, xs_sem.at[2], xr_sem.at[2], other)

    def dn_copy(r):
        return remote(dns.at[r], dnr.at[r], xs_sem.at[3 + r], xr_sem.at[3 + r], other)

    def hop(level):
        half = 8 >> level
        away = pl.ds((1 - a[level]) * half, half)
        return remote(
            bufs[level].at[away], bufs[level + 1], cs_sem.at[level], cr_sem.at[level], (peers[level], x)
        )

    def absorb(level):
        half = 8 >> level
        hop(level).wait()
        both = bufs[level][pl.ds(a[level] * half, half)].astype(F32) + bufs[level + 1][...].astype(F32)
        if level < 3:
            bufs[level + 1][...] = both.astype(BF)
            hop(level + 1).start()
        else:
            for i in range(4):
                g_ref[i] = both[0, :, i * cols : (i + 1) * cols]

    def keep_copy(s):
        return pltpu.make_async_copy(hand_hbm.at[s, pl.ds(a[1] * 4, 4)], hk.at[s], ksem.at[s])

    def hand_hop(level, s):
        half = 8 >> level
        away = pl.ds((1 - a[level]) * half, half)
        src = hand_hbm.at[s, away] if level == 1 else hbufs[level].at[s, away]
        return remote(src, hbufs[level + 1].at[s], hsends[level].at[s], hrecvs[level].at[s], (peers[level], x))

    def hand_start(block):
        def one(w, carry):
            keep_copy(block * 3 + w).start()
            hand_hop(1, block * 3 + w).start()
            return carry

        lax.fori_loop(0, 3, one, 0)

    def hand_absorb(level, block):
        def one(w, carry):
            s = block * 3 + w
            half = 8 >> level
            hand_hop(level, s).wait()
            if level == 1:
                keep_copy(s).wait()
                kept = hk[s]
            else:
                kept = hbufs[level][s, pl.ds(a[level] * half, half)]
            both = kept.astype(F32) + hbufs[level + 1][s].astype(F32)
            if level < 3:
                hbufs[level + 1][s] = both.astype(BF)
                hand_hop(level + 1, s).start()
            else:
                grads_ref[w, :, block * BLK : (block + 1) * BLK] = both[0]
            return carry

        lax.fori_loop(0, 3, one, 0)

    def round_copy(i):
        who = other if i == 4 else (peers[i], x)
        return remote(sb.at[i], rb.at[i], bs_sem.at[i], br_sem.at[i], who)

    def round_end(i):
        round_copy(i).wait()
        sb[i + 1] = sb[i] + rb[i]
        if i < 4:
            round_copy(i + 1).start()

    def out_copy(r):
        return pltpu.make_async_copy(f3.at[:, lanes(r)], ig_hbm.at[:, lanes(r)], lsem.at[5 + r])

    def lane_sum(v):
        total = v[:, 0:128]
        for i in range(1, v.shape[1] // 128):
            total = total + v[:, i * 128 : (i + 1) * 128]
        return total

    def dn_part(b):
        ls = slice(b * BLK, (b + 1) * BLK)
        part = dot(wn[...], dproj[:, ls], ((1,), (0,)))
        gsum[...] += lane_sum(nrm[:, ls].astype(F32) * part)
        return part

    @pl.when(step_id == 0)
    def _():
        for i in range(3):
            local(i).start()
        meet([(p, x) for p in peers] + [other])
        hand_start(0)
        if later > 1:
            hand_start(1)
        dkv[...] = jnp.zeros_like(dkv)
        tally[...] = jnp.zeros_like(tally)
        stage[...] = jnp.zeros_like(stage)
        fsum[...] = jnp.zeros_like(fsum)
        gsum[...] = jnp.zeros_like(gsum)
        agc[...] = column(ag_ref[...])
        fgc[...] = column(fg_ref[...])
        for i in range(3):
            local(i).wait()
        for r in range(near_blocks):
            ls = slice(r * BLK, (r + 1) * BLK)
            v = f2[:, ls]
            c = f1[:, ls]
            scale = norm_scale(v)
            n = v * scale
            cg = c * fgc[...]
            m = jnp.mean(cg * n, axis=0, keepdims=True)
            gm = f3[:, ls] + scale * (cg - n * m)
            fsum[...] += lane_sum(c * n)
            f1[:, ls] = gm
            alow[:, ls] = gm.astype(BF)
        for i in range(3, 5):
            local(i).start()
        dcs[...] = dot(wall_ref[cols : 2 * cols, :], alow[...], ((1,), (0,))).astype(BF)
        dctx_copy.start()
        dctx[:, :rows] = dot(wall_ref[0:cols, :], alow[...], ((1,), (0,))).astype(BF)
        osend[...] = dot(alow[...], ctx_ref[cols : 2 * cols, :rows], ((1,), (1,))).astype(BF)
        grad[:, 3 * cols : 4 * cols] = dot(alow[...], ctx_ref[0:cols, :rows], ((1,), (1,)))
        wn[...] = wq_ref[...].astype(F32).T.astype(BF)
        dctx_copy.wait()
        o_copy.start()
        back_copy.start()

    def head_rows(group):
        return pl.ds(pl.multiple_of(group * cols + h * dk, dk), dk)

    inv = inv_ref[0, 0]
    qh = qkv_ref[head_rows(0), lanes(qb)]
    scaled = (dctx[head_rows(0), lanes(qb)].astype(F32) * inv).astype(BF)
    inner = jnp.zeros((1, BLK), F32)
    for kb in range(blocks):
        krows = slice(kb * BLK, (kb + 1) * BLK)
        g = dot(qkv_ref[head_rows(2), krows], scaled, ((0,), (0,)))
        dp_s[krows, :] = g
        inner = inner + jnp.sum(e_ref[0, 0, krows, :].astype(F32) * g, axis=0, keepdims=True)
    inner = inner * inv
    dq = jnp.zeros((dk, BLK), F32)
    q_true = (qb + near_blocks * x) % blocks
    for kb in range(blocks):
        krows = slice(kb * BLK, (kb + 1) * BLK)
        e = e_ref[0, 0, krows, :]
        ds = (e.astype(F32) * (dp_s[krows, :] - inner)).astype(BF)
        dkv[head_rows(0), krows] += dot(qh, ds, ((1,), (1,)))
        dkv[head_rows(1), krows] += dot(scaled, e, ((1,), (1,)))
        dq = dq + dot(qkv_ref[head_rows(1), krows], ds, ((1,), (0,)))
        diag = (kb + near_blocks * x) % blocks - q_true + blocks - 1
        tally[h, diag] += ds.astype(F32)
    dproj[head_rows(0), lanes(qb)] = dq.astype(BF)

    @pl.when(step_id == 5)
    def _():
        hand_absorb(1, 0)
        if later > 2:
            hand_start(2)

    @pl.when(step_id == blocks * heads - 1)
    def _():
        dproj[cols : 3 * cols, :] = dkv[...].astype(BF)
        for i in range(3, 5):
            local(i).wait()
        for r in range(near_blocks):
            dns[r] = dn_part(near_blocks + r).astype(BF)
            dn_copy(r).start()
        if later > 1:
            hand_absorb(1, 1)
        if later > 3:
            hand_start(3)
        grad[:, 0 : 3 * cols] = dot(nrm[...], dproj[...], ((1,), (1,)))
        o_copy.wait()
        grad[:, 3 * cols : 4 * cols] += orecv[...].astype(F32)
        for k in range(16):
            stage[block_position(k), 0:shard, :] = grad[k * shard : (k + 1) * shard, :].astype(BF)
        hop(0).start()
        hand_absorb(2, 0)
        for r in range(near_blocks):
            f3[:, r * BLK : (r + 1) * BLK] = dn_part(r)
        absorb(0)
        if later > 1:
            hand_absorb(2, 1)
        hand_absorb(3, 0)
        ids = bid_ref[...]
        hot = ids == lax.broadcasted_iota(jnp.int32, (buckets, SPAN), 0)
        out_lane = lax.broadcasted_iota(jnp.int32, (buckets, 128), 1)
        sub = lax.broadcasted_iota(jnp.int32, (8, SPAN), 0)
        out = jnp.zeros((buckets, 128), F32)
        for hh in range(heads):
            line = jnp.zeros((8, SPAN), F32)
            for g in range(BLK // 8):
                group = slice(8 * g, 8 * g + 8)
                t = [tally[hh, i, group, :] for i in range(7)]
                parts = [t[5] + t[6], t[4], t[3], t[2], t[1] + t[0]]
                strip = jnp.concatenate(parts + [jnp.zeros((8, BLK), F32)], axis=1)
                line = line + (strip if g == 0 else pltpu.roll(strip, SPAN - 8 * g, 1))
            for bit in (1, 2, 4):
                line = jnp.where((sub // bit) % 2 == 1, pltpu.roll(line, SPAN - bit, 1), line)
            sums = jnp.sum(line, axis=0, keepdims=True)
            col = jnp.sum(jnp.where(hot, sums, 0.0), axis=1, keepdims=True)
            out = jnp.where(out_lane == x * heads + hh, col, out)
        sb[0] = jnp.zeros(sb.shape[1:], F32)
        sb[0, 0:buckets, :] = out
        again = jnp.sum(gsum[...].T, axis=0, keepdims=True) / ag_ref[...]
        fgain = jnp.sum(fsum[...].T, axis=0, keepdims=True)
        lines = -(-d // 128)
        for i in range(lines):
            n = min(128, d - 128 * i)
            sb[0, buckets + i : buckets + i + 1, 0:n] = again[:, 128 * i : 128 * i + n]
            sb[0, buckets + lines + i : buckets + lines + i + 1, 0:n] = fgain[:, 128 * i : 128 * i + n]
        round_copy(0).start()
        if later > 2:
            hand_absorb(1, 2)
        round_end(0)
        if later > 1:
            hand_absorb(3, 1)
        round_end(1)
        if later > 2:
            hand_absorb(2, 2)
        round_end(2)
        if later > 3:
            hand_absorb(1, 3)
        absorb(1)
        round_end(3)
        if later > 2:
            hand_absorb(3, 2)
        round_end(4)
        small_ref[...] = sb[5]
        if later > 3:
            hand_absorb(2, 3)
        for r in range(near_blocks):
            ls = slice(r * BLK, (r + 1) * BLK)
            dn_copy(r).wait()
            c = f3[:, ls] + dnr[r].astype(F32)
            v = f2[:, ls]
            scale = norm_scale(v)
            n = v * scale
            cg = c * agc[...]
            m = jnp.mean(cg * n, axis=0, keepdims=True)
            f3[:, ls] = f1[:, ls] + scale * (cg - n * m)
            out_copy(r).start()
            if r == 0:
                absorb(2)
                if later > 3:
                    hand_absorb(3, 3)
        absorb(3)
        back_copy.wait()
        for r in range(near_blocks):
            out_copy(r).wait()


def tail(qkv, e, inv, wall, ctx, wq, again, fgain, din, mid, cot, tok, nrm, far, hand,
         buckets, heads, dk, extra):
    d, rows = tok.shape
    seq = 2 * rows
    cols = heads * dk
    blocks = seq // BLK
    near = blocks // 2
    shard = d // 16
    spad = -(-shard // 16) * 16
    chunks = hand.shape[0]
    later = chunks // 3
    lines = -(-(buckets + 2 * -(-d // 128)) // 8) * 8
    bids = jnp.asarray(lane_buckets(buckets))
    one = pl.Buffered(1)
    dma = pltpu.SemaphoreType.DMA
    any_spec = pl.BlockSpec(memory_space=pl.ANY)

    def full(v):
        return pl.BlockSpec(v.shape, lambda i, h: (0, 0), pipeline_mode=one)

    return pl.pallas_call(
        functools.partial(tail_kernel, heads, dk, buckets, blocks, extra, later),
        grid=(blocks, heads),
        in_specs=[
            full(bids),
            full(qkv),
            pl.BlockSpec((1, 1, seq, BLK), lambda i, h: (h, i, 0, 0)),
            pl.BlockSpec((1, 1, 1, BLK), lambda i, h: (h, i, 0, 0)),
            full(wall),
            full(ctx),
            full(wq),
            full(again),
            full(fgain),
        ]
        + [any_spec] * 7,
        out_specs=[
            any_spec,
            pl.BlockSpec((4, spad, cols), lambda i, h: (0, 0, 0)),
            pl.BlockSpec((lines, 128), lambda i, h: (0, 0)),
            pl.BlockSpec((3, spad, later * BLK), lambda i, h: (0, 0, 0)),
            any_spec,
        ],
        out_shape=[
            jax.ShapeDtypeStruct((d, rows), F32),
            jax.ShapeDtypeStruct((4, spad, cols), F32),
            jax.ShapeDtypeStruct((lines, 128), F32),
            jax.ShapeDtypeStruct((3, spad, later * BLK), F32),
            jax.ShapeDtypeStruct(far.shape, BF),
        ],
        scratch_shapes=[
            pltpu.VMEM((d, rows), F32),
            pltpu.VMEM((d, rows), F32),
            pltpu.VMEM((d, rows), F32),
            pltpu.VMEM((d, seq), BF),
            pltpu.VMEM((d, 3 * cols), BF),
            pltpu.VMEM((d, rows), BF),
            pltpu.VMEM((cols, seq), BF),
            pltpu.VMEM((cols, rows), BF),
            pltpu.VMEM((d, cols), BF),
            pltpu.VMEM((d, cols), BF),
            pltpu.VMEM((d, 128), F32),
            pltpu.VMEM((d, 128), F32),
            pltpu.VMEM((d, 1), F32),
            pltpu.VMEM((d, 1), F32),
            pltpu.VMEM((seq, BLK), F32),
            pltpu.VMEM((2 * cols, seq), F32),
            pltpu.VMEM((heads, 7, BLK, BLK), F32),
            pltpu.VMEM((3 * cols, seq), BF),
            pltpu.VMEM((d, 4 * cols), F32),
            pltpu.VMEM((near, d, BLK), BF),
            pltpu.VMEM((near, d, BLK), BF),
            pltpu.VMEM((16, spad, 4 * cols), BF),
            pltpu.VMEM((8, spad, 4 * cols), BF),
            pltpu.VMEM((4, spad, 4 * cols), BF),
            pltpu.VMEM((2, spad, 4 * cols), BF),
            pltpu.VMEM((1, spad, 4 * cols), BF),
            pltpu.VMEM((chunks, 4, spad, BLK), BF),
            pltpu.VMEM((chunks, 4, spad, BLK), BF),
            pltpu.VMEM((chunks, 2, spad, BLK), BF),
            pltpu.VMEM((chunks, 1, spad, BLK), BF),
            pltpu.VMEM((6, lines, 128), F32),
            pltpu.VMEM((5, lines, 128), F32),
            dma((5 + near,)),
            dma((chunks,)),
            dma((3 + near,)), dma((3 + near,)),
            dma((4,)), dma((4,)),
            dma((5,)), dma((5,)),
            dma((chunks,)), dma((chunks,)), dma((chunks,)),
            dma((chunks,)), dma((chunks,)), dma((chunks,)),
        ],
        compiler_params=pltpu.CompilerParams(
            vmem_limit_bytes=FF_VMEM, collective_id=1, has_side_effects=True
        ),
        cost_estimate=pl.CostEstimate(
            flops=32 * heads * seq * seq * dk + 8 * seq * d * 3 * cols,
            bytes_accessed=2 * heads * seq * seq + 30 * rows * d,
            transcendentals=0,
        ),
    )(bids, qkv, e, inv, wall, ctx, wq, again, fgain, din, mid, cot, tok, nrm, far, hand)


def take(array, index):
    return lax.dynamic_index_in_dim(array, index, 0, keepdims=False)


def per_device(
    tokens,
    cotangent,
    doc_lengths,
    pad_mask,
    attn_gain,
    qkv_weight,
    rel_table,
    out_weight,
    ff_gain,
    ff_in_weight,
    ff_out_weight,
):
    rows, d = tokens.shape
    n_dp = lax.axis_size("dp")
    n_mp = lax.axis_size("mp")
    cols = qkv_weight.shape[2]
    buckets, heads = rel_table.shape
    dk = cols // heads
    me = lax.axis_index("dp")
    shard = d // n_dp
    extra = n_dp // 16

    def hop(v, mask):
        return lax.ppermute(v, "dp", [(i, i ^ mask) for i in range(n_dp)])

    def bit(b):
        return (me >> b) & 1

    def reduce_rest(parts, low_bits):
        for b in reversed(range(low_bits)):
            halves = [p.reshape((2, p.shape[0] // 2) + p.shape[1:]) for p in parts]
            away = sum(take(p, 1 - bit(b)).astype(F32) for p in halves).astype(BF)
            parts = [take(p, bit(b)) for p in halves] + [hop(away, 1 << b)]
        return sum(p.astype(F32) for p in parts)[0]

    def finish(g):
        g = g[: d // 16]
        if extra == 1:
            return g
        return reduce_rest([g.reshape(extra, shard, g.shape[1])], extra.bit_length() - 1)

    tok = tokens.T
    cot = cotangent.T
    far = lax.ppermute(tok.astype(BF), "mp", [(0, 1), (1, 0)])
    w2 = jnp.transpose(ff_in_weight, (1, 0, 2))
    wq = jnp.transpose(qkv_weight, (1, 2, 0)).reshape(3 * cols, d)
    again, fgain = attn_gain.reshape(1, d), ff_gain.reshape(1, d)

    e, inv, qkv, ctx, nrm, xt, mid, ct, wall = front(
        rel_table, doc_lengths, pad_mask, again, fgain, wq, out_weight.T, tok, far, cot, heads, dk
    )
    early, din, near_out, far_out, hand = ff_all(xt, ct, w2, ff_out_weight, extra)
    input_grad, last, small, late, back = tail(
        qkv, e, inv, wall, ctx, wq, again, fgain, din, mid, cot, tok, nrm, far_out, hand,
        buckets, heads, dk, extra,
    )
    result = (mid + near_out + back.astype(F32)).T

    ffo, ffg, ffu = (finish(jnp.concatenate([early[i], late[i]], axis=1)) for i in range(3))
    grad_qkv = jnp.stack([finish(last[i]) for i in range(3)], axis=1)
    for b in range(extra.bit_length() - 1):
        small = small + hop(small, 1 << b)
    lines = -(-d // 128)
    return (
        result,
        input_grad.T,
        small[buckets : buckets + lines].reshape(-1)[:d],
        grad_qkv,
        small[:buckets, : heads * n_mp],
        finish(last[3]),
        small[buckets + lines : buckets + 2 * lines].reshape(-1)[:d],
        jnp.stack([ffg, ffu], axis=1),
        ffo,
    )


def solution(mesh):
    return jax.shard_map(
        per_device,
        mesh=mesh,
        in_specs=(
            P(("dp", "mp"), None),
            P(("dp", "mp"), None),
            P("dp", None),
            P("dp", None),
            P(),
            P(None, None, "mp"),
            P(None, "mp"),
            P(None, "mp"),
            P(),
            P(None, None, "mp"),
            P(None, "mp"),
        ),
        out_specs=(
            P(("dp", "mp"), None),
            P(("dp", "mp"), None),
            P(),
            P("dp", None, "mp"),
            P(),
            P("dp", "mp"),
            P(),
            P("dp", None, "mp"),
            P("dp", "mp"),
        ),
        check_vma=False,
    )
```

time: 413 us -> 333 us (0.81)
  local copies, waits for them, and re-layouts: 68.7 us -> 24 us
  waiting for transfers between devices: 41.8 us -> 19.9 us
  other arithmetic: 27.6 us -> 6.36 us
  Pallas kernels: 256 us -> 274 us
  matrix products: 9.26 us -> 0 us
    ppermute x4 -> x1, waiting for transfers between devices: 41.8 us -> 19.9 us  [per_device(): far = lax.ppermute(tok.astype(BF), 'mp', [(0, 1), (1, 0)])]
    unnamed x52 -> x25, local copies, waits for them, and re-layouts: 36.7 us -> 18.8 us
    pallas_call x2, Pallas kernels: 142 us -> 157 us  [the longest x1 116 us: ff_all(): pl.pallas_call(functools.partial(ff_kernel, steps, done, extra), grid=(3...]
    pad x4 -> x0, local copies, waits for them, and re-layouts: 11.6 us -> none  [the longest x1 4.9 us: per_device(): jnp.pad(jnp.transpose(ff_in_weight, (1, 0, 2)), ((0, 0), (0, pad_d), (0,...]
    dot_general x7 -> x0, matrix products: 9.26 us -> none  [the longest x3 5.44 us: project(): return jnp.dot(normed, w, preferred_element_type=F32).astype(BF)]
    reduce_sum x3 -> x0, other arithmetic: 6.28 us -> none  [the longest x2 6.19 us: rms_scale(): jnp.mean(v * v, axis=-1, keepdims=True) + norm_eps]
    slice x7 -> x1, local copies, waits for them, and re-layouts: 6.16 us -> 0.81 us  [per_device(): small[:buckets, :heads * n_mp]]
    convert_element_type x3 -> x1, other arithmetic: 7.13 us -> 2.06 us  [per_device(): far = lax.ppermute(tok.astype(BF), 'mp', [(0, 1), (1, 0)])]
  transfers between devices with their start and end apart: 4 -> 1, of which waited for: 3 -> 1; matrix products, arithmetic and copies ran while one was open for 14% -> 4% of each run, Pallas kernels for 0% -> 0%
where the time goes in v1:
time: 333 us; the launch traced here: 329 us
  Pallas kernels  274 us (82%)
  local copies, waits for them, and re-layouts  24 us (7%)
  waiting for transfers between devices  19.9 us (6%)
  other arithmetic  6.36 us (2%)
    pallas_call x1, Pallas kernels, tail(): pl.pallas_call(functools.partial(tail_kernel, heads, dk, buckets, blocks,...  117 us
    pallas_call x1, Pallas kernels, ff_all(): pl.pallas_call(functools.partial(ff_kernel, steps, done, extra), grid=(3...  116 us
    pallas_call x1, Pallas kernels, front(): pl.pallas_call(functools.partial(front_kernel, heads, dk, buckets, blocks...  40.7 us
    ppermute x1, waiting for transfers between devices, per_device(): far = lax.ppermute(tok.astype(BF), 'mp', [(0, 1), (1, 0)])  19.9 us
    unnamed x25, local copies, waits for them, and re-layouts  18.8 us
  transfers between devices with their start and end apart: 1, of which 1 were waited for; matrix products, arithmetic and copies ran while one was open for 4% of the time, Pallas kernels for 0%

profile of v1, /device:TPU:0, one launch (start us, length us, event | category | flops | bytes accessed | tf_op | source)
XLA Modules:
  0.0 328.7 jit_solution(16794780014804696014)
XLA Ops:
  0.6 0.0 copy-start.6
  0.7 0.0 copy-start.7
  0.7 0.0 copy-start.8
  0.7 2.1 bitcast_convert_fusion
  2.7 3.0 collective-permute-start
  5.7 0.6 reshape.40.ag_ref
  6.3 0.6 reshape.41.fg_ref
  6.9 0.0 copy-done.8
  6.9 0.7 copy.22.rel_ref
  7.6 11.2 %copy.27 = bf16[1472,2,1792]{2,0,1:T(8,128)(2,1)} copy(bf16[1472,2,1792]{2,1,0:T(2,128)(2,1)} %param.22) | data formatting | bytes 21102592 | tf_op args[9]
  18.9 19.9 %collective-permute-done.far_hbm = bf16[1472,512]{1,0:T(8,128)(2,1)S(1)} collective-permute-done((bf16[1472,512]{1,0:T(8,128)(2,1)S(1)}, bf16[1472,512]{1,0:T(8,128)(2,1)S(1)}, u32[]{:S(2)}, u32[]{:S(2)}) %collective-permute-start) | collective-permute-done | bytes 1507360 | tf_op jit(solution)/shard_map/ppermute | solution.py:1019
  38.7 1.1 copy-done.9
  39.9 40.7 %shard_map.196 = (bf16[3,4,1024,256]{3,2,1,0:T(8,128)(2,1)}, f32[3,4,1,256]{3,2,1,0:T(1,128)}, bf16[576,1024]{1,0:T(8,128)(2,1)}, bf16[384,1024]{1,0:T(8,128)(2,...) custom-call(f32[32,3]{1,0:T(8,128)} %copy.22.rel_ref, ...), custom_call_target="tpu_custom_call" | custom-call | flops 6115295232 | bytes 28901376 | tf_op jit(solution)/shard_map/pallas_call | solution.py:275
  80.5 116.3 %shard_map.197 = (f32[3,96,768]{2,1,0:T(8,128)}, f32[1472,512]{1,0:T(8,128)}, f32[1472,512]{1,0:T(8,128)}, bf16[1472,512]{1,0:T(8,128)(2,1)}, bf16[12,8,96,256]{3,2,1,0:T(8,128)(2,1)}) custom-call(bf16[1472,1024]{1,0:T(8,128)(2,1)} %get-tuple-element.29.xt_ref, bf16[2,1472,1792]{2,1,0:T(8,128)(2,1)} %bitcast.43, bf16[2,1472,1792]{2,1,0:T(8,128)(2,1)} %bitcast.44, ...), custom_call_target="tpu_custom_call" | custom-call | flops 48620371968 | bytes 39944192 | tf_op jit(solution)/shard_map/pallas_call | solution.py:535
  196.9 0.0 copy-start.5
  196.9 117.5 %shard_map.198 = (f32[1472,512]{1,0:T(8,128)}, f32[4,96,192]{2,1,0:T(8,128)}, f32[56,128]{1,0:T(8,128)}, f32[3,96,1024]{2,1,0:T(8,128)}, bf16[1472,512]{1,0:T(8,128)(2,1)}) custom-call(s32[1,1536]{1,0:T(1,128)} %constant.2.clone.bid_ref, bf16[576,1024]{1,0:T(8,128)(2,1)} %get-tuple-element.32.qkv_ref, bf16[3,4,1024,256]{3,2,1,0:T(8,128)(2,1)} %get-tuple-element.33.e_ref, ...), custom_call_target="tpu_custom_call" | custom-call | flops 13388218368 | bytes 28901376 | tf_op jit(solution)/shard_map/pallas_call | solution.py:890
  314.4 0.8 slice.73
  315.2 1.4 slice_bitcast_fusion.10
  316.6 0.7 copy.24
  317.2 1.7 slice_bitcast_fusion.6
  318.9 0.1 slice_bitcast_fusion.3
  319.0 0.1 slice_bitcast_fusion
  319.1 0.1 fusion
  319.2 0.1 pad_maximum_fusion
  319.3 2.1 copy.25
  321.4 0.0 copy-done.2
  321.4 1.0 copy-done
  322.4 0.4 copy-done.3
  322.8 2.5 add_bitcast_fusion
  325.2 0.9 pad_maximum_fusion.1
  326.1 0.7 pad_maximum_fusion.4
  326.9 1.6 copy.29
  (11 shorter events, 0.0 us)
Async XLA Ops:
  0.6 5.1 %copy-start.6 = (f32[1472]{0:T(1024)S(1)}, f32[1472]{0:T(1024)}, u32[]{:S(2)}) copy-start(f32[1472]{0:T(1024)} %param.17) | copy-start | bytes 17668
  0.7 5.7 %copy-start.7 = (f32[1472]{0:T(1024)S(1)}, f32[1472]{0:T(1024)}, u32[]{:S(2)}) copy-start(f32[1472]{0:T(1024)} %param.21) | copy-start | bytes 17668
  0.7 6.3 %copy-start.8 = (f32[32,3]{0,1:T(4,128)S(1)}, f32[32,3]{0,1:T(4,128)}, u32[]{:S(2)}) copy-start(f32[32,3]{0,1:T(4,128)} %param.19) | copy-start | bytes 1156
  2.7 36.0 %collective-permute-start = (bf16[1472,512]{1,0:T(8,128)(2,1)S(1)}, bf16[1472,512]{1,0:T(8,128)(2,1)S(1)}, u32[]{:S(2)}, u32[]{:S(2)}) collective-permute-start(bf16[1472,512]{1,0:T(8,128)(2,1)S(1)} %bitcast_convert_fusion), channel_id=1, source_target_pairs={{0,1},{1,0},{2,3},{3,2},{4,5},{5,4},{6,7},{7,6},{8,9},{9,8},{10,11... | collective-permute-start | bytes 4521992 | tf_op jit(solution)/shard_map/ppermute | solution.py:1019
  38.7 1.1 copy-start.9
  196.9 122.1 %copy-start.5 = (f32[3,96,768]{2,1,0:T(8,128)S(1)}, f32[3,96,768]{2,1,0:T(8,128)}, u32[]{:S(2)}) copy-start(f32[3,96,768]{2,1,0:T(8,128)} %get-tuple-element.45) | copy-start | bytes 2654212
  314.4 4.6 %copy-start.4 = (f32[3,96,1024]{2,1,0:T(8,128)S(1)}, f32[3,96,1024]{2,1,0:T(8,128)}, u32[]{:S(2)}) copy-start(f32[3,96,1024]{2,1,0:T(8,128)} %get-tuple-element.46) | copy-start | bytes 3538948
  319.1 2.3 copy-start.2
  319.2 3.2 copy-start
  319.2 3.6 %copy-start.3 = (bf16[1472,512]{1,0:T(8,128)(2,1)S(1)}, bf16[1472,512]{1,0:T(8,128)(2,1)}, u32[]{:S(2)}) copy-start(bf16[1472,512]{1,0:T(8,128)(2,1)} %get-tuple-element.41) | copy-start | bytes 4521988
  322.8 4.1 %copy-start.1 = (f32[1472,512]{1,0:T(8,128)S(1)}, f32[1472,512]{1,0:T(8,128)}, u32[]{:S(2)}) copy-start(f32[1472,512]{1,0:T(8,128)} %get-tuple-element.42) | copy-start | bytes 9043972

commit v2 on v1

--- a/solution.py
+++ b/solution.py
@@ -16,7 +16,7 @@
 BF = jnp.bfloat16
 F32 = jnp.float32
 FF_VMEM = 63 << 20
-FF_DONE = 3
+FF_DONE = 2
 
 
 def bucket_of(offsets, buckets, reach):
@@ -60,10 +60,14 @@
     return [b[0], b[1], (b[2] + b[3]) % 2, b[3]]
 
 
-def block_position(k):
+Y_FIRST = (0, 1, 2, 3)
+Z_FIRST = (0, 2, 3, 1)
+
+
+def block_position(k, order):
     b = [k >> i & 1 for i in range(4)]
     c = [b[0], b[1], b[2] ^ b[3], b[3]]
-    return c[0] * 8 + c[1] * 4 + c[2] * 2 + c[3]
+    return sum(c[order[i]] << (3 - i) for i in range(4))
 
 
 def column(line):
@@ -325,16 +329,15 @@
 
 def ff_kernel(
     steps, done, extra,
-    xt_ref, wg_ref, wu_ref, ct_hbm, wo_hbm,
-    grads_ref, din_hbm, near_hbm, far_hbm, hand_hbm,
-    ct, wo, hid, dg, du, din, stage, r1, r2, r3, r4, xs, xr, of, nf,
-    csem, wo_sem, s1, s2, s3, s4, t1, t2, t3, t4, xsem, osem, hsem,
+    xt_hbm, w_hbm, ct_hbm, wo_hbm,
+    grads_ref, din_hbm, near_hbm, far_hbm, back_hbm, mid_hbm, hand_hbm,
+    xt, ct, wg, wu, wo, hid, dg, du, din, stage, r1, r2, r3, r4, xs, xr, of,
+    csem, wsem, s1, s2, s3, s4, t1, t2, t3, t4, xsem, osem, hsem,
 ):
-    i = pl.program_id(0)
-    phase, j = i // steps, i % steps
     f, total = hid.shape
     rows = total // 2
-    d = xt_ref.shape[0]
+    chunks = rows // BLK
+    d = xt.shape[0]
     shard = d // 16
     dp, mp = lax.axis_index("dp"), lax.axis_index("mp")
     a = group_coords(dp // extra)
@@ -344,17 +347,23 @@
     sends, recvs = (s1, s2, s3, s4), (t1, t2, t3, t4)
     end = steps - 1
 
-    def wo_copy(n):
-        return pltpu.make_async_copy(wo_hbm.at[:, lanes(n)], wo.at[:, lanes(n)], wo_sem.at[n])
-
-    def c_local(n):
-        size = (BLK, rows)[n]
-        part = pl.ds((rows, 0)[n], size)
-        return pltpu.make_async_copy(ct_hbm.at[:, part], ct.at[:, part], csem.at[n])
+    def weight_copy(kind, n):
+        src, dst = ((w_hbm.at[0], wg), (w_hbm.at[1], wu), (wo_hbm, wo))[kind]
+        return pltpu.make_async_copy(src.at[:, lanes(n)], dst.at[:, lanes(n)], wsem.at[kind, n])
+
+    def tok_copy(n):
+        src, dst, start, size = (
+            (xt_hbm, xt, rows, BLK), (ct_hbm, ct, rows, BLK),
+            (xt_hbm, xt, rows + BLK, BLK), (xt_hbm, xt, 0, rows), (ct_hbm, ct, 0, rows),
+        )[n]
+        part = pl.ds(start, size)
+        return pltpu.make_async_copy(src.at[:, part], dst.at[:, part], csem.at[n])
 
     c_far = remote(
-        ct_hbm.at[:, pl.ds(BLK, BLK)], ct.at[:, pl.ds(rows + BLK, BLK)], csem.at[2], csem.at[3], other
+        ct_hbm.at[:, pl.ds(BLK, BLK)], ct.at[:, pl.ds(rows + BLK, BLK)], csem.at[5], csem.at[6], other
     )
+    x_copy = remote(xs, xr, xsem.at[0], xsem.at[1], other)
+    back_copy = remote(of, back_hbm, xsem.at[2], xsem.at[3], other)
 
     def hop(level, s, w):
         half = 8 >> level
@@ -363,161 +372,215 @@
         return remote(src, bufs[level].at[s], sends[level].at[s], recvs[level].at[s], (peers[level], mp))
 
     def hand_copy(s):
-        return pltpu.make_async_copy(r1.at[s], hand_hbm.at[s - 3 * done], hsem.at[s - 3 * done])
-
-    def absorb(level, step, w):
-        s = step * 3 + w
-        half = 8 >> level
-        copy = hop(level, s, w)
-        copy.wait_recv()
-        copy.wait_send()
-        keep = pl.ds(a[level] * half, half)
-        kept = stage[w, keep] if level == 0 else bufs[level - 1][s, keep]
-        both = kept.astype(F32) + bufs[level][s].astype(F32)
-        if level == 3:
-            grads_ref[w, :, lanes(step)] = both[0]
-            return
-        bufs[level][s] = both.astype(BF)
-        if level > 0:
-            hop(level + 1, s, w).start()
-            return
+        if isinstance(s, int) and s < 3 * done + 3:
+            return pltpu.make_async_copy(r2.at[s], mid_hbm.at[s - 3 * done], hsem.at[s - 3 * done])
+        return pltpu.make_async_copy(r1.at[s], hand_hbm.at[s - 3 * done - 3], hsem.at[s - 3 * done])
+
+    def absorb_first(step):
+        for w in range(3):
+            s = step * 3 + w
+            copy = hop(0, s, w)
+            copy.wait_recv()
+            copy.wait_send()
+        keep = pl.ds(a[0] * 8, 8)
+        for w in range(3):
+            s = step * 3 + w
+            r1[s] = stage[w, keep] + r1[s]
+
+        def onward():
+            for w in range(3):
+                hop(1, step * 3 + w, w).start()
+
+        def aside():
+            for w in range(3):
+                hand_copy(step * 3 + w).start()
+
         if isinstance(step, int):
-            hand_copy(s).start()
-            return
-
-        @pl.when(step < done)
-        def _():
-            hop(1, s, w).start()
-
-        @pl.when(step >= done)
-        def _():
-            hand_copy(s).start()
-
-    def absorb_step(level, step):
+            onward() if step <= done else aside()
+        else:
+            pl.when(step <= done)(onward)
+            pl.when(step > done)(aside)
+
+    def absorb(level, step):
         def one(w, carry):
-            absorb(level, step, w)
+            s = step * 3 + w
+            half = 8 >> level
+            copy = hop(level, s, w)
+            copy.wait_recv()
+            copy.wait_send()
+            kept = bufs[level - 1][s, pl.ds(a[level] * half, half)]
+            if level < 3:
+                bufs[level][s] = kept + bufs[level][s]
+                if step < done:
+                    hop(level + 1, s, w).start()
+            else:
+                both = kept.astype(F32) + bufs[level][s].astype(F32)
+                grads_ref[w, :, lanes(step)] = both[0]
             return carry
 
         lax.fori_loop(0, 3, one, 0)
 
-    @pl.when(i == 0)
-    def _():
-        meet([(p, mp) for p in peers] + [other])
-        c_far.start()
-        c_local(0).start()
-        for n in range(steps):
-            wo_copy(n).start()
-        c_local(1).start()
-        din[...] = jnp.zeros_like(din)
-        stage[...] = jnp.zeros_like(stage)
-        c_local(0).wait()
-
-    @pl.when(phase == 0)
-    def _():
-        wo_copy(j).wait()
-
-    @pl.when(i == steps)
-    def _():
-        c_far.wait()
-
     scale = np.float32(np.sqrt(2 / np.pi))
-    frows = lanes(j)
-
-    def block(tok, acc):
-        gate = dot(wg_ref[...], xt_ref[:, tok], ((0,), (0,)))
-        up = dot(wu_ref[...], xt_ref[:, tok], ((0,), (0,)))
-        dh = dot(wo[:, frows], ct[:, tok], ((0,), (0,)))
+
+    def forward(j, tok):
+        fcols = lanes(j)
+        gate = dot(wg[:, fcols], xt[:, tok], ((0,), (0,)))
+        up = dot(wu[:, fcols], xt[:, tok], ((0,), (0,)))
+        dh = dot(wo[:, fcols], ct[:, tok], ((0,), (0,)))
+        return gate, up, dh
+
+    def pointwise(j, tok, values):
+        gate, up, dh = values
+        frows = lanes(j)
         sq = gate * gate
         t = jnp.tanh(scale * gate * (1.0 + 0.044715 * sq))
         half = 0.5 * (1.0 + t)
         act = gate * half
         slope = half + 0.5 * gate * (1.0 - t * t) * (scale * (1.0 + (3 * 0.044715) * sq))
         hid[frows, tok] = (act * up).astype(BF)
-        dgr = (dh * (up * slope)).astype(BF)
-        dur = (dh * act).astype(BF)
-        dg[frows, tok] = dgr
-        du[frows, tok] = dur
-        din[:, acc] += dot(wg_ref[...], dgr, ((1,), (0,))) + dot(wu_ref[...], dur, ((1,), (0,)))
-
-    x_copy = remote(xs, xr, xsem.at[0], xsem.at[1], other)
-
-    @pl.when(phase < 2)
-    def _():
-        block(lanes(phase + rows // BLK), lanes(phase))
-
-    @pl.when(i == 2 * steps - 1)
-    def _():
-        xs[...] = din[...].astype(BF)
-        x_copy.start()
-        din[...] = jnp.zeros_like(din)
-        c_local(1).wait()
+        dg[frows, tok] = (dh * (up * slope)).astype(BF)
+        du[frows, tok] = (dh * act).astype(BF)
+
+    def backward(j, tok, acc):
+        rs = lanes(j)
+        din[:, acc] += dot(wg[:, rs], dg[rs, tok], ((1,), (0,))) + dot(wu[:, rs], du[rs, tok], ((1,), (0,)))
+
+    def far_lanes(t):
+        return lanes(t // steps + chunks), lanes(t // steps)
+
+    def near(j):
+        parts = [pl.ds(n * BLK, BLK) for n in range(chunks)]
+        values = [forward(j, p) for p in parts]
+        for p, v in zip(parts, values):
+            pointwise(j, p, v)
+        for p in parts:
+            backward(j, p, p)
 
     per = 4 * shard
 
-    @pl.when(phase == 2)
-    def _():
-        for n in range(rows // BLK):
-            block(pl.ds(n * BLK, BLK), pl.ds(n * BLK, BLK))
-
-        @pl.when(j > 0)
-        def _():
-            absorb(0, j - 1, 2)
-
+    def grads(j, order):
         for w in range(3):
-            right = (hid, dg, du)[w][frows, :]
+            right = (hid, dg, du)[w][lanes(j), :]
             for q in range(4):
                 rs = slice(q * per, (q + 1) * per)
-                left = ct[rs, :] if w == 0 else xt_ref[rs, :]
+                left = ct[rs, :] if w == 0 else xt[rs, :]
                 part = dot(left, right, ((1,), (1,)))
                 for k in range(4):
-                    stage[w, block_position(4 * q + k), 0:shard, :] = part[
+                    stage[w, block_position(4 * q + k, order), 0:shard, :] = part[
                         k * shard : (k + 1) * shard
                     ].astype(BF)
+        for w in range(3):
             hop(0, j * 3 + w, w).start()
-            if w > 0:
-                absorb(0, j, w - 1)
-
-        for when, events in ((3, ((1, 0),)), (5, ((1, 1), (2, 0))), (6, ((3, 0),))):
-            @pl.when(j == when)
-            def _():
-                for level, step in events:
-                    absorb_step(level, step)
-
-    @pl.when(i == 3 * steps - 1)
-    def _():
-        absorb(0, end, 2)
-
-        def out_part(n):
-            return dot(wo[...], hid[:, n * BLK : (n + 1) * BLK], ((1,), (0,)))
-
-        half = rows // BLK
-        for n in range(half):
-            of[:, n * BLK : (n + 1) * BLK] = out_part(half + n).astype(BF)
-        far_copy = pltpu.make_async_copy(of, far_hbm, osem.at[0])
-        far_copy.start()
-        absorb_step(1, 2)
-        absorb_step(2, 1)
-        x_copy.wait()
-        din[...] += xr[...].astype(F32)
-        din_copy = pltpu.make_async_copy(din, din_hbm, osem.at[2])
-        din_copy.start()
-        nf[:, 0:BLK] = out_part(0)
-        absorb_step(2, 2)
-        absorb_step(3, 1)
-        for n in range(1, half):
-            nf[:, n * BLK : (n + 1) * BLK] = out_part(n)
-        near_copy = pltpu.make_async_copy(nf, near_hbm, osem.at[1])
-        near_copy.start()
-        absorb_step(3, 2)
-
-        def flush(s, carry):
-            hand_copy(s).wait()
-            return carry
-
-        lax.fori_loop(3 * done, 3 * steps, flush, 0)
-        far_copy.wait()
-        near_copy.wait()
-        din_copy.wait()
+
+    def out_part(n):
+        return dot(wo[...], hid[:, n * BLK : (n + 1) * BLK], ((1,), (0,)))
+
+    def weights_wait(j):
+        for kind in range(3):
+            weight_copy(kind, j).wait()
+
+    meet([(p, mp) for p in peers] + [other])
+    c_far.start()
+    tok_copy(0).start()
+    tok_copy(1).start()
+    for n in range(steps):
+        for kind in range(3):
+            weight_copy(kind, n).start()
+        if n == 0:
+            tok_copy(2).start()
+    tok_copy(3).start()
+    tok_copy(4).start()
+    din[...] = jnp.zeros_like(din)
+    stage[...] = jnp.zeros_like(stage)
+    tok_copy(0).wait()
+    tok_copy(1).wait()
+    weights_wait(0)
+    tok0, acc0 = far_lanes(0)
+    pointwise(0, tok0, forward(0, tok0))
+
+    def far_step(t, carry):
+        j = t % steps
+
+        @pl.when(t < steps)
+        def _():
+            weights_wait(j)
+
+        @pl.when(t == steps)
+        def _():
+            tok_copy(2).wait()
+            c_far.wait()
+
+        tok, _ = far_lanes(t)
+        before, acc = far_lanes(t - 1)
+        values = forward(j, tok)
+        backward((t - 1) % steps, before, acc)
+        pointwise(j, tok, values)
+        return carry
+
+    lax.fori_loop(1, chunks * steps, far_step, 0)
+    tok_copy(3).wait()
+    tok_copy(4).wait()
+    last, acc = far_lanes(chunks * steps - 1)
+    backward(end, last, acc)
+    xs[...] = din[...].astype(BF)
+    x_copy.start()
+    din[...] = jnp.zeros_like(din)
+    near(0)
+
+    def near_step(j, carry):
+        grads(j, Y_FIRST)
+        near(j + 1)
+        absorb_first(j)
+
+        @pl.when(j == 3)
+        def _():
+            absorb(1, 0)
+            of[...] = out_part(chunks).astype(BF)
+
+        @pl.when(j == 4)
+        def _():
+            x_copy.wait()
+            back_copy.start()
+
+        @pl.when(j == 5)
+        def _():
+            absorb(1, 1)
+            absorb(2, 0)
+
+        return carry
+
+    lax.fori_loop(0, end, near_step, 0)
+    din[...] += xr[...].astype(F32)
+    din_copy = pltpu.make_async_copy(din, din_hbm, osem.at[2])
+    din_copy.start()
+    grads(end, Z_FIRST)
+    xs[:, 0:BLK] = out_part(chunks + 1).astype(BF)
+    far_copy = pltpu.make_async_copy(xs.at[:, pl.ds(0, BLK)], far_hbm, osem.at[0])
+    far_copy.start()
+    absorb_first(end)
+    din_copy.wait()
+    din[:, 0:BLK] = out_part(0)
+    absorb(2, 1)
+    absorb(3, 0)
+    for n in range(1, chunks):
+        din[:, n * BLK : (n + 1) * BLK] = out_part(n)
+    near_copy = pltpu.make_async_copy(din, near_hbm, osem.at[1])
+    near_copy.start()
+    absorb(1, done)
+    for w in range(3):
+        hand_copy(3 * done + w).start()
+    absorb(3, 1)
+    far_copy.wait()
+    near_copy.wait()
+
+    def flush(s, carry):
+        hand_copy(s).wait()
+        return carry
+
+    lax.fori_loop(3 * done + 3, 3 * steps, flush, 0)
+    for w in range(3):
+        hand_copy(3 * done + w).wait()
+    back_copy.wait()
 
 
 def ff_all(xt, ct, w2, wo, extra):
@@ -534,24 +597,22 @@
     any_spec = pl.BlockSpec(memory_space=pl.ANY)
     return pl.pallas_call(
         functools.partial(ff_kernel, steps, done, extra),
-        grid=(3 * steps,),
-        in_specs=[
-            pl.BlockSpec((d, total), lambda i: (0, 0), pipeline_mode=pl.Buffered(1)),
-            pl.BlockSpec((None, d, BLK), lambda i: (0, 0, i % steps)),
-            pl.BlockSpec((None, d, BLK), lambda i: (1, 0, i % steps)),
-            any_spec,
-            any_spec,
-        ],
-        out_specs=[pl.BlockSpec((3, spad, done * BLK), lambda i: (0, 0, 0))] + [any_spec] * 4,
+        in_specs=[any_spec] * 4,
+        out_specs=[pl.BlockSpec(memory_space=pltpu.VMEM)] + [any_spec] * 6,
         out_shape=[
             jax.ShapeDtypeStruct((3, spad, done * BLK), F32),
             jax.ShapeDtypeStruct((d, rows), F32),
             jax.ShapeDtypeStruct((d, rows), F32),
-            jax.ShapeDtypeStruct((d, rows), BF),
-            jax.ShapeDtypeStruct((chunks - kept, 8, spad, BLK), BF),
+            jax.ShapeDtypeStruct((d, BLK), BF),
+            jax.ShapeDtypeStruct((d, BLK), BF),
+            jax.ShapeDtypeStruct((3, 4, spad, BLK), BF),
+            jax.ShapeDtypeStruct((chunks - kept - 3, 8, spad, BLK), BF),
         ],
         scratch_shapes=[
             pltpu.VMEM((d, total), BF),
+            pltpu.VMEM((d, total), BF),
+            pltpu.VMEM((d, f), BF),
+            pltpu.VMEM((d, f), BF),
             pltpu.VMEM((d, f), BF),
             pltpu.VMEM((f, total), BF),
             pltpu.VMEM((f, total), BF),
@@ -559,18 +620,17 @@
             pltpu.VMEM((d, rows), F32),
             pltpu.VMEM((3, 16, spad, BLK), BF),
             pltpu.VMEM((chunks, 8, spad, BLK), BF),
-            pltpu.VMEM((kept, 4, spad, BLK), BF),
+            pltpu.VMEM((kept + 3, 4, spad, BLK), BF),
             pltpu.VMEM((kept, 2, spad, BLK), BF),
             pltpu.VMEM((kept, 1, spad, BLK), BF),
             pltpu.VMEM((d, rows), BF),
             pltpu.VMEM((d, rows), BF),
-            pltpu.VMEM((d, rows), BF),
-            pltpu.VMEM((d, rows), F32),
+            pltpu.VMEM((d, BLK), BF),
+            dma((7,)),
+            dma((3, steps)),
+            dma((chunks,)), dma((kept + 3,)), dma((kept,)), dma((kept,)),
+            dma((chunks,)), dma((kept + 3,)), dma((kept,)), dma((kept,)),
             dma((4,)),
-            dma((steps,)),
-            dma((chunks,)), dma((kept,)), dma((kept,)), dma((kept,)),
-            dma((chunks,)), dma((kept,)), dma((kept,)), dma((kept,)),
-            dma((2,)),
             dma((3,)),
             dma((chunks - kept,)),
         ],
@@ -582,17 +642,17 @@
             bytes_accessed=6 * d * f + 16 * total * d,
             transcendentals=total * f,
         ),
-    )(xt, w2, w2, ct, wo)
+    )(xt, w2, ct, wo)
 
 
 def tail_kernel(
-    heads, dk, buckets, blocks, extra, later,
+    heads, dk, buckets, blocks, extra,
     bid_ref, qkv_ref, e_ref, inv_ref, wall_ref, ctx_ref, wq_ref, ag_ref, fg_ref,
-    din_hbm, mid_hbm, cot_hbm, tok_hbm, nrm_hbm, far_hbm, hand_hbm,
+    din_hbm, mid_hbm, cot_hbm, tok_hbm, nrm_hbm, far_hbm, part_hbm, hand_hbm,
     ig_hbm, g_ref, small_ref, grads_ref, back_hbm,
     f1, f2, f3, nrm, wn, alow, dctx, dcs, osend, orecv, gsum, fsum, agc, fgc,
     dp_s, dkv, tally, dproj, grad, dns, dnr,
-    stage, t1, t2, t3, t4, hk, h2, h3, h4, sb, rb,
+    stage, t1, t2, t3, t4, hk, hm, h2, h3, h4, sb, rb,
     lsem, ksem, xs_sem, xr_sem, cs_sem, cr_sem, bs_sem, br_sem, hs2, hs3, hs4, hr2, hr3, hr4,
 ):
     qb, h = pl.program_id(0), pl.program_id(1)
@@ -606,7 +666,6 @@
     peers = [flip(dp, m * extra) for m in GROUP_MASKS]
     other = (dp, 1 - x)
     bufs = (stage, t1, t2, t3, t4)
-    hbufs = (None, hk, h2, h3, h4)
     hsends, hrecvs = (None, hs2, hs3, hs4), (None, hr2, hr3, hr4)
     near_blocks = blocks // 2
 
@@ -616,10 +675,13 @@
 
     dctx_copy = remote(dcs, dctx.at[:, pl.ds(rows, rows)], xs_sem.at[0], xr_sem.at[0], other)
     o_copy = remote(osend, orecv, xs_sem.at[1], xr_sem.at[1], other)
-    back_copy = remote(far_hbm, back_hbm, xs_sem.at[2], xr_sem.at[2], other)
+
+    def back_copy(i):
+        part = pl.ds(i * 128, 128)
+        return remote(far_hbm.at[:, part], back_hbm.at[:, part], xs_sem.at[2 + i], xr_sem.at[2 + i], other)
 
     def dn_copy(r):
-        return remote(dns.at[r], dnr.at[r], xs_sem.at[3 + r], xr_sem.at[3 + r], other)
+        return remote(dns.at[r], dnr.at[r], xs_sem.at[4 + r], xr_sem.at[4 + r], other)
 
     def hop(level):
         half = 8 >> level
@@ -631,27 +693,42 @@
     def absorb(level):
         half = 8 >> level
         hop(level).wait()
-        both = bufs[level][pl.ds(a[level] * half, half)].astype(F32) + bufs[level + 1][...].astype(F32)
+        kept = bufs[level][pl.ds(a[level] * half, half)]
         if level < 3:
-            bufs[level + 1][...] = both.astype(BF)
+            bufs[level + 1][...] = kept + bufs[level + 1][...]
             hop(level + 1).start()
         else:
+            both = kept.astype(F32) + bufs[level + 1][...].astype(F32)
             for i in range(4):
                 g_ref[i] = both[0, :, i * cols : (i + 1) * cols]
 
-    def keep_copy(s):
-        return pltpu.make_async_copy(hand_hbm.at[s, pl.ds(a[1] * 4, 4)], hk.at[s], ksem.at[s])
-
-    def hand_hop(level, s):
+    def order_of(block):
+        return Z_FIRST if block == 4 else Y_FIRST
+
+    def keep_copy(block, w):
+        s = block * 3 + w
+        if block == 0:
+            return pltpu.make_async_copy(part_hbm.at[w, pl.ds(a[2] * 2, 2)], hm.at[w], ksem.at[s])
+        keep = pl.ds(a[order_of(block)[1]] * 4, 4)
+        return pltpu.make_async_copy(hand_hbm.at[s - 3, keep], hk.at[s - 3], ksem.at[s])
+
+    def hand_hop(level, block, w):
+        s = block * 3 + w
         half = 8 >> level
-        away = pl.ds((1 - a[level]) * half, half)
-        src = hand_hbm.at[s, away] if level == 1 else hbufs[level].at[s, away]
-        return remote(src, hbufs[level + 1].at[s], hsends[level].at[s], hrecvs[level].at[s], (peers[level], x))
+        c = order_of(block)[level]
+        away = pl.ds((1 - a[c]) * half, half)
+        if level == 1:
+            src, dst = hand_hbm.at[s - 3, away], h2.at[s - 3]
+        elif level == 2:
+            src, dst = part_hbm.at[w, away] if block == 0 else h2.at[s - 3, away], h3.at[s]
+        else:
+            src, dst = h3.at[s, away], h4.at[s]
+        return remote(src, dst, hsends[level].at[s], hrecvs[level].at[s], (peers[c], x))
 
     def hand_start(block):
         def one(w, carry):
-            keep_copy(block * 3 + w).start()
-            hand_hop(1, block * 3 + w).start()
+            keep_copy(block, w).start()
+            hand_hop(2 if block == 0 else 1, block, w).start()
             return carry
 
         lax.fori_loop(0, 3, one, 0)
@@ -660,24 +737,28 @@
         def one(w, carry):
             s = block * 3 + w
             half = 8 >> level
-            hand_hop(level, s).wait()
+            keep = pl.ds(a[order_of(block)[level]] * half, half)
+            hand_hop(level, block, w).wait()
+            if level == (2 if block == 0 else 1):
+                keep_copy(block, w).wait()
+                kept = hm[w] if block == 0 else hk[s - 3]
+            else:
+                kept = h2[s - 3, keep] if level == 2 else h3[s, keep]
             if level == 1:
-                keep_copy(s).wait()
-                kept = hk[s]
+                h2[s - 3] = kept + h2[s - 3]
+            elif level == 2:
+                h3[s] = kept + h3[s]
             else:
-                kept = hbufs[level][s, pl.ds(a[level] * half, half)]
-            both = kept.astype(F32) + hbufs[level + 1][s].astype(F32)
+                both = kept.astype(F32) + h4[s].astype(F32)
+                grads_ref[w, :, block * BLK : (block + 1) * BLK] = both[0]
             if level < 3:
-                hbufs[level + 1][s] = both.astype(BF)
-                hand_hop(level + 1, s).start()
-            else:
-                grads_ref[w, :, block * BLK : (block + 1) * BLK] = both[0]
+                hand_hop(level + 1, block, w).start()
             return carry
 
         lax.fori_loop(0, 3, one, 0)
 
     def round_copy(i):
-        who = other if i == 4 else (peers[i], x)
+        who = other if i == 4 else (peers[(0, 2, 3, 1)[i]], x)
         return remote(sb.at[i], rb.at[i], bs_sem.at[i], br_sem.at[i], who)
 
     def round_end(i):
@@ -706,9 +787,9 @@
         for i in range(3):
             local(i).start()
         meet([(p, x) for p in peers] + [other])
-        hand_start(0)
-        if later > 1:
-            hand_start(1)
+        back_copy(0).start()
+        for block in (0, 4, 1, 2, 3):
+            hand_start(block)
         dkv[...] = jnp.zeros_like(dkv)
         tally[...] = jnp.zeros_like(tally)
         stage[...] = jnp.zeros_like(stage)
@@ -740,7 +821,7 @@
         wn[...] = wq_ref[...].astype(F32).T.astype(BF)
         dctx_copy.wait()
         o_copy.start()
-        back_copy.start()
+        back_copy(1).start()
 
     def head_rows(group):
         return pl.ds(pl.multiple_of(group * cols + h * dk, dk), dk)
@@ -768,11 +849,13 @@
         tally[h, diag] += ds.astype(F32)
     dproj[head_rows(0), lanes(qb)] = dq.astype(BF)
 
-    @pl.when(step_id == 5)
-    def _():
-        hand_absorb(1, 0)
-        if later > 2:
-            hand_start(2)
+    for when, events in (
+        (2, ((2, 0),)), (5, ((1, 1),)), (7, ((1, 4),)), (9, ((3, 0),)), (10, ((2, 1), (1, 2))),
+    ):
+        @pl.when(step_id == when)
+        def _():
+            for level, block in events:
+                hand_absorb(level, block)
 
     @pl.when(step_id == blocks * heads - 1)
     def _():
@@ -782,23 +865,18 @@
         for r in range(near_blocks):
             dns[r] = dn_part(near_blocks + r).astype(BF)
             dn_copy(r).start()
-        if later > 1:
-            hand_absorb(1, 1)
-        if later > 3:
-            hand_start(3)
         grad[:, 0 : 3 * cols] = dot(nrm[...], dproj[...], ((1,), (1,)))
         o_copy.wait()
         grad[:, 3 * cols : 4 * cols] += orecv[...].astype(F32)
         for k in range(16):
-            stage[block_position(k), 0:shard, :] = grad[k * shard : (k + 1) * shard, :].astype(BF)
+            stage[block_position(k, Y_FIRST), 0:shard, :] = grad[k * shard : (k + 1) * shard, :].astype(BF)
         hop(0).start()
-        hand_absorb(2, 0)
+        hand_absorb(2, 4)
         for r in range(near_blocks):
             f3[:, r * BLK : (r + 1) * BLK] = dn_part(r)
         absorb(0)
-        if later > 1:
-            hand_absorb(2, 1)
-        hand_absorb(3, 0)
+        hand_absorb(3, 1)
+        hand_absorb(2, 2)
         ids = bid_ref[...]
         hot = ids == lax.broadcasted_iota(jnp.int32, (buckets, SPAN), 0)
         out_lane = lax.broadcasted_iota(jnp.int32, (buckets, 128), 1)
@@ -827,26 +905,14 @@
             sb[0, buckets + i : buckets + i + 1, 0:n] = again[:, 128 * i : 128 * i + n]
             sb[0, buckets + lines + i : buckets + lines + i + 1, 0:n] = fgain[:, 128 * i : 128 * i + n]
         round_copy(0).start()
-        if later > 2:
-            hand_absorb(1, 2)
+        hand_absorb(1, 3)
         round_end(0)
-        if later > 1:
-            hand_absorb(3, 1)
+        hand_absorb(3, 2)
         round_end(1)
-        if later > 2:
-            hand_absorb(2, 2)
+        hand_absorb(2, 3)
         round_end(2)
-        if later > 3:
-            hand_absorb(1, 3)
-        absorb(1)
-        round_end(3)
-        if later > 2:
-            hand_absorb(3, 2)
-        round_end(4)
-        small_ref[...] = sb[5]
-        if later > 3:
-            hand_absorb(2, 3)
-        for r in range(near_blocks):
+
+        def last_norm(r):
             ls = slice(r * BLK, (r + 1) * BLK)
             dn_copy(r).wait()
             c = f3[:, ls] + dnr[r].astype(F32)
@@ -857,17 +923,25 @@
             m = jnp.mean(cg * n, axis=0, keepdims=True)
             f3[:, ls] = f1[:, ls] + scale * (cg - n * m)
             out_copy(r).start()
-            if r == 0:
-                absorb(2)
-                if later > 3:
-                    hand_absorb(3, 3)
+
+        absorb(1)
+        last_norm(0)
+        round_end(3)
+        hand_absorb(3, 4)
+        hand_absorb(3, 3)
+        absorb(2)
+        for r in range(1, near_blocks):
+            last_norm(r)
+        round_end(4)
+        small_ref[...] = sb[5]
         absorb(3)
-        back_copy.wait()
+        for i in range(2):
+            back_copy(i).wait()
         for r in range(near_blocks):
             out_copy(r).wait()
 
 
-def tail(qkv, e, inv, wall, ctx, wq, again, fgain, din, mid, cot, tok, nrm, far, hand,
+def tail(qkv, e, inv, wall, ctx, wq, again, fgain, din, mid, cot, tok, nrm, far, half_way, hand,
          buckets, heads, dk, extra):
     d, rows = tok.shape
     seq = 2 * rows
@@ -877,7 +951,7 @@
     shard = d // 16
     spad = -(-shard // 16) * 16
     chunks = hand.shape[0]
-    later = chunks // 3
+    later = chunks // 3 + 1
     lines = -(-(buckets + 2 * -(-d // 128)) // 8) * 8
     bids = jnp.asarray(lane_buckets(buckets))
     one = pl.Buffered(1)
@@ -888,7 +962,7 @@
         return pl.BlockSpec(v.shape, lambda i, h: (0, 0), pipeline_mode=one)
 
     return pl.pallas_call(
-        functools.partial(tail_kernel, heads, dk, buckets, blocks, extra, later),
+        functools.partial(tail_kernel, heads, dk, buckets, blocks, extra),
         grid=(blocks, heads),
         in_specs=[
             full(bids),
@@ -901,7 +975,7 @@
             full(again),
             full(fgain),
         ]
-        + [any_spec] * 7,
+        + [any_spec] * 8,
         out_specs=[
             any_spec,
             pl.BlockSpec((4, spad, cols), lambda i, h: (0, 0, 0)),
@@ -944,18 +1018,19 @@
             pltpu.VMEM((2, spad, 4 * cols), BF),
             pltpu.VMEM((1, spad, 4 * cols), BF),
             pltpu.VMEM((chunks, 4, spad, BLK), BF),
+            pltpu.VMEM((3, 2, spad, BLK), BF),
             pltpu.VMEM((chunks, 4, spad, BLK), BF),
-            pltpu.VMEM((chunks, 2, spad, BLK), BF),
-            pltpu.VMEM((chunks, 1, spad, BLK), BF),
+            pltpu.VMEM((3 * later, 2, spad, BLK), BF),
+            pltpu.VMEM((3 * later, 1, spad, BLK), BF),
             pltpu.VMEM((6, lines, 128), F32),
             pltpu.VMEM((5, lines, 128), F32),
             dma((5 + near,)),
-            dma((chunks,)),
-            dma((3 + near,)), dma((3 + near,)),
+            dma((3 * later,)),
+            dma((4 + near,)), dma((4 + near,)),
             dma((4,)), dma((4,)),
             dma((5,)), dma((5,)),
-            dma((chunks,)), dma((chunks,)), dma((chunks,)),
-            dma((chunks,)), dma((chunks,)), dma((chunks,)),
+            dma((3 * later,)), dma((3 * later,)), dma((3 * later,)),
+            dma((3 * later,)), dma((3 * later,)), dma((3 * later,)),
         ],
         compiler_params=pltpu.CompilerParams(
             vmem_limit_bytes=FF_VMEM, collective_id=1, has_side_effects=True
@@ -965,7 +1040,7 @@
             bytes_accessed=2 * heads * seq * seq + 30 * rows * d,
             transcendentals=0,
         ),
-    )(bids, qkv, e, inv, wall, ctx, wq, again, fgain, din, mid, cot, tok, nrm, far, hand)
+    )(bids, qkv, e, inv, wall, ctx, wq, again, fgain, din, mid, cot, tok, nrm, far, half_way, hand)
 
 
 def take(array, index):
@@ -1024,11 +1099,12 @@
     e, inv, qkv, ctx, nrm, xt, mid, ct, wall = front(
         rel_table, doc_lengths, pad_mask, again, fgain, wq, out_weight.T, tok, far, cot, heads, dk
     )
-    early, din, near_out, far_out, hand = ff_all(xt, ct, w2, ff_out_weight, extra)
-    input_grad, last, small, late, back = tail(
-        qkv, e, inv, wall, ctx, wq, again, fgain, din, mid, cot, tok, nrm, far_out, hand,
+    early, din, near_out, far_out, back0, half_way, hand = ff_all(xt, ct, w2, ff_out_weight, extra)
+    input_grad, last, small, late, back1 = tail(
+        qkv, e, inv, wall, ctx, wq, again, fgain, din, mid, cot, tok, nrm, far_out, half_way, hand,
         buckets, heads, dk, extra,
     )
+    back = jnp.concatenate([back0, back1], axis=1)
     result = (mid + near_out + back.astype(F32)).T
 
     ffo, ffg, ffu = (finish(jnp.concatenate([early[i], late[i]], axis=1)) for i in range(3))

time: 333 us -> 284 us (0.85)
  Pallas kernels: 274 us -> 228 us
    pallas_call x1, Pallas kernels: 116 us -> 88.8 us  [ff_all(): pl.pallas_call(functools.partial(ff_kernel, steps, done, extra), in_specs...]
    pallas_call x1, Pallas kernels: 117 us -> 98.3 us  [tail(): pl.pallas_call(functools.partial(tail_kernel, heads, dk, buckets, blocks,...]
    unnamed x25 -> x27, local copies, waits for them, and re-layouts: 18.8 us -> 18.1 us
  transfers between devices with their start and end apart: 1 -> 1, of which waited for: 1 -> 1; matrix products, arithmetic and copies ran while one was open for 4% -> 5% of each run, Pallas kernels for 0% -> 0%
where the time goes in v2:
time: 284 us; the launch traced here: 281 us
  Pallas kernels  228 us (80%)
  local copies, waits for them, and re-layouts  23.4 us (8%)
  waiting for transfers between devices  19.8 us (7%)
  other arithmetic  6.33 us (2%)
  starting transfers between devices  3 us (1%)
    pallas_call x1, Pallas kernels, tail(): pl.pallas_call(functools.partial(tail_kernel, heads, dk, buckets, blocks,...  98.3 us
    pallas_call x1, Pallas kernels, ff_all(): pl.pallas_call(functools.partial(ff_kernel, steps, done, extra), in_specs...  88.8 us
    pallas_call x1, Pallas kernels, front(): pl.pallas_call(functools.partial(front_kernel, heads, dk, buckets, blocks...  40.6 us
    ppermute x1, waiting for transfers between devices, per_device(): far = lax.ppermute(tok.astype(BF), 'mp', [(0, 1), (1, 0)])  19.8 us
    unnamed x27, local copies, waits for them, and re-layouts  18.1 us
  transfers between devices with their start and end apart: 1, of which 1 were waited for; matrix products, arithmetic and copies ran while one was open for 5% of the time, Pallas kernels for 0%

profile of v2, /device:TPU:0, one launch (start us, length us, event | category | flops | bytes accessed | tf_op | source)
XLA Modules:
  0.0 281.3 jit_solution(16535497399867649779)
XLA Ops:
  0.6 0.0 copy-start.7
  0.7 0.0 copy-start.8
  0.7 0.0 copy-start.9
  0.7 2.1 bitcast_convert_fusion
  2.7 3.0 %collective-permute-start = (bf16[1472,512]{1,0:T(8,128)(2,1)S(1)}, bf16[1472,512]{1,0:T(8,128)(2,1)S(1)}, u32[]{:S(2)}, u32[]{:S(2)}) collective-permute-start(bf16[1472,512]{1,0:T(8,128)(2,1)S(1)} %bitcast_convert_fusion), channel_id=1, source_target_pairs={{0,1},{1,0},{2,3},{3,2},{4,5},{5,4},{6,7},{7,6},{8,9},{9,8},{10,11... | collective-permute-start | bytes 4521992 | tf_op jit(solution)/shard_map/ppermute | solution.py:1094
  5.7 0.6 reshape.40.ag_ref
  6.3 0.6 reshape.41.fg_ref
  6.9 0.0 copy-done.9
  6.9 0.7 copy.22.rel_ref
  7.6 11.2 %copy.27 = bf16[1472,2,1792]{2,0,1:T(8,128)(2,1)} copy(bf16[1472,2,1792]{2,1,0:T(2,128)(2,1)} %param.22) | data formatting | bytes 21102592 | tf_op args[9]
  18.9 19.8 %collective-permute-done.far_hbm = bf16[1472,512]{1,0:T(8,128)(2,1)S(1)} collective-permute-done((bf16[1472,512]{1,0:T(8,128)(2,1)S(1)}, bf16[1472,512]{1,0:T(8,128)(2,1)S(1)}, u32[]{:S(2)}, u32[]{:S(2)}) %collective-permute-start) | collective-permute-done | bytes 1507360 | tf_op jit(solution)/shard_map/ppermute | solution.py:1094
  38.7 1.1 copy-done.10
  39.9 40.6 %shard_map.196 = (bf16[3,4,1024,256]{3,2,1,0:T(8,128)(2,1)}, f32[3,4,1,256]{3,2,1,0:T(1,128)}, bf16[576,1024]{1,0:T(8,128)(2,1)}, bf16[384,1024]{1,0:T(8,128)(2,...) custom-call(f32[32,3]{1,0:T(8,128)} %copy.22.rel_ref, ...), custom_call_target="tpu_custom_call" | custom-call | flops 6115295232 | bytes 28901376 | tf_op jit(solution)/shard_map/pallas_call | solution.py:279
  80.5 88.8 %shard_map.197 = (f32[3,96,512]{2,1,0:T(8,128)}, f32[1472,512]{1,0:T(8,128)}, f32[1472,512]{1,0:T(8,128)}, bf16[1472,256]{1,0:T(8,128)(2,1)}, bf16[1472,256]{1,0...) custom-call(bf16[1472,1024]{1,0:T(8,128)(2,1)} %get-tuple-element.31.xt_hbm, ...), custom_call_target="tpu_custom_call" | custom-call | flops 48620371968 | bytes 39944192 | tf_op jit(solution)/shard_map/pallas_call | solution.py:598
  169.2 0.0 copy-start.6
  169.3 98.3 %shard_map.198 = (f32[1472,512]{1,0:T(8,128)}, f32[4,96,192]{2,1,0:T(8,128)}, f32[56,128]{1,0:T(8,128)}, f32[3,96,1280]{2,1,0:T(8,128)}, bf16[1472,256]{1,0:T(8,128)(2,1)}) custom-call(s32[1,1536]{1,0:T(1,128)} %constant.2.clone.bid_ref, bf16[576,1024]{1,0:T(8,128)(2,1)} %get-tuple-element.35.qkv_ref, bf16[3,4,1024,256]{3,2,1,0:T(8,128)(2,1)} %get-tuple-element.36.e_ref, ...), custom_call_target="tpu_custom_call" | custom-call | flops 13388218368 | bytes 28901376 | tf_op jit(solution)/shard_map/pallas_call | solution.py:964
  267.6 0.8 slice.73
  268.4 1.4 slice_bitcast_fusion.10
  269.8 0.7 copy.24
  270.5 1.7 slice_bitcast_fusion.6
  272.2 0.0 copy-done.6
  272.2 0.1 slice_bitcast_fusion
  272.4 0.1 fusion
  272.5 0.1 pad_maximum_fusion
  272.6 2.1 copy.25
  274.7 0.9 pad_maximum_fusion.1
  275.6 0.0 copy-done.5
  275.6 0.5 copy-done.1
  276.1 0.1 copy-done.4
  276.2 2.5 add_bitcast_fusion
  278.7 0.7 pad_maximum_fusion.4
  279.4 1.6 copy.29
  (13 shorter events, 0.1 us)
Async XLA Ops:
  0.6 5.1 %copy-start.7 = (f32[1472]{0:T(1024)S(1)}, f32[1472]{0:T(1024)}, u32[]{:S(2)}) copy-start(f32[1472]{0:T(1024)} %param.17) | copy-start | bytes 17668
  0.7 5.7 %copy-start.8 = (f32[1472]{0:T(1024)S(1)}, f32[1472]{0:T(1024)}, u32[]{:S(2)}) copy-start(f32[1472]{0:T(1024)} %param.21) | copy-start | bytes 17668
  0.7 6.3 %copy-start.9 = (f32[32,3]{0,1:T(4,128)S(1)}, f32[32,3]{0,1:T(4,128)}, u32[]{:S(2)}) copy-start(f32[32,3]{0,1:T(4,128)} %param.19) | copy-start | bytes 1156
  2.7 36.0 %collective-permute-start = (bf16[1472,512]{1,0:T(8,128)(2,1)S(1)}, bf16[1472,512]{1,0:T(8,128)(2,1)S(1)}, u32[]{:S(2)}, u32[]{:S(2)}) collective-permute-start(bf16[1472,512]{1,0:T(8,128)(2,1)S(1)} %bitcast_convert_fusion), channel_id=1, source_target_pairs={{0,1},{1,0},{2,3},{3,2},{4,5},{5,4},{6,7},{7,6},{8,9},{9,8},{10,11... | collective-permute-start | bytes 4521992 | tf_op jit(solution)/shard_map/ppermute | solution.py:1094
  38.7 1.1 copy-start.10
  169.2 102.9 %copy-start.6 = (f32[3,96,512]{2,1,0:T(8,128)S(1)}, f32[3,96,512]{2,1,0:T(8,128)}, u32[]{:S(2)}) copy-start(f32[3,96,512]{2,1,0:T(8,128)} %get-tuple-element.49) | copy-start | bytes 1769476
  267.6 4.6 %copy-start.3 = (f32[3,96,1280]{2,1,0:T(8,128)S(1)}, f32[3,96,1280]{2,1,0:T(8,128)}, u32[]{:S(2)}) copy-start(f32[3,96,1280]{2,1,0:T(8,128)} %get-tuple-element.50) | copy-start | bytes 4423684
  272.3 3.2 %copy-start.5 = (bf16[1472,256]{1,0:T(8,128)(2,1)S(1)}, bf16[1472,256]{1,0:T(8,128)(2,1)}, u32[]{:S(2)}) copy-start(bf16[1472,256]{1,0:T(8,128)(2,1)} %get-tuple-element.45) | copy-start | bytes 2260996
  272.5 3.1 %copy-start = (f32[1472,512]{1,0:T(8,128)S(1)}, f32[1472,512]{1,0:T(8,128)}, u32[]{:S(2)}) copy-start(f32[1472,512]{1,0:T(8,128)} %get-tuple-element.30.mid_hbm) | copy-start | bytes 9043972
  272.5 3.6 %copy-start.1 = (f32[1472,512]{1,0:T(8,128)S(1)}, f32[1472,512]{1,0:T(8,128)}, u32[]{:S(2)}) copy-start(f32[1472,512]{1,0:T(8,128)} %get-tuple-element.33) | copy-start | bytes 9043972
  272.5 3.7 %copy-start.4 = (bf16[1472,256]{1,0:T(8,128)(2,1)S(1)}, bf16[1472,256]{1,0:T(8,128)(2,1)}, u32[]{:S(2)}) copy-start(bf16[1472,256]{1,0:T(8,128)(2,1)} %get-tuple-element.34) | copy-start | bytes 2260996
  276.2 3.2 %copy-start.2 = (f32[1472,512]{1,0:T(8,128)S(1)}, f32[1472,512]{1,0:T(8,128)}, u32[]{:S(2)}) copy-start(f32[1472,512]{1,0:T(8,128)} %get-tuple-element.46) | copy-start | bytes 9043972

commit v3 on v2

v3 whole, which is shorter than its diff:
```python
import functools

import jax
import jax.numpy as jnp
import numpy as np
from jax import lax
from jax.experimental import pallas as pl
from jax.experimental.pallas import tpu as pltpu
from jax.sharding import PartitionSpec as P

MAXDIST = 128
norm_eps = 1e-06
BLK = 256
SPAN = 6 * BLK
REACH = 2
BF = jnp.bfloat16
F32 = jnp.float32
FF_VMEM = 63 << 20
FF_DONE = 2


def bucket_of(offsets, buckets, reach):
    half_range = buckets // 2
    upper_half = (offsets > 0).astype(np.int32) * half_range
    distance = np.abs(offsets)
    exact_range = half_range // 2
    safe_dist = np.maximum(distance, 1)
    log_bucket = exact_range + (
        np.log(safe_dist / exact_range) / np.log(reach / exact_range) * (half_range - exact_range)
    ).astype(np.int32)
    log_bucket = np.minimum(log_bucket, half_range - 1)
    return (upper_half + np.where(distance < exact_range, distance, log_bucket)).astype(np.int32)


def lane_buckets(buckets):
    lanes = np.arange(SPAN)
    shifted = np.where(lanes < 5 * BLK, lanes, lanes - SPAN)
    return bucket_of(REACH * BLK - shifted, buckets, MAXDIST).reshape(1, SPAN)


def dot(a, b, contract):
    return lax.dot_general(a, b, (contract, ((), ())), preferred_element_type=F32)


def flip(index, mask):
    out = index
    bit = 1
    while bit <= mask:
        if mask & bit:
            out = out + bit * (1 - 2 * (index // bit % 2))
        bit *= 2
    return out


GROUP_MASKS = (1, 2, 4, 12)


def group_coords(g):
    b = [g // (1 << i) % 2 for i in range(4)]
    return [b[0], b[1], (b[2] + b[3]) % 2, b[3]]


Y_FIRST = (0, 1, 2, 3)
Z_FIRST = (0, 2, 3, 1)


def block_position(k, order):
    b = [k >> i & 1 for i in range(4)]
    c = [b[0], b[1], b[2] ^ b[3], b[3]]
    return sum(c[order[i]] << (3 - i) for i in range(4))


def column(line):
    return jnp.broadcast_to(line, (8, line.shape[1])).T[:, 0:1]


def norm_scale(v):
    return lax.rsqrt(jnp.mean(v * v, axis=0, keepdims=True) + norm_eps)


def lanes(block):
    return pl.ds(pl.multiple_of(block * BLK, BLK), BLK)


def remote(src, dst, send, recv, who):
    return pltpu.make_async_remote_copy(
        src_ref=src,
        dst_ref=dst,
        send_sem=send,
        recv_sem=recv,
        device_id=who,
        device_id_type=pl.DeviceIdType.MESH,
    )


def meet(devices):
    barrier = pltpu.get_barrier_semaphore()
    for who in devices:
        pl.semaphore_signal(barrier, inc=1, device_id=who, device_id_type=pl.DeviceIdType.MESH)
    pl.semaphore_wait(barrier, len(devices))


def near_diagonal(offset):
    i = offset + 3
    return i + (6 - i) // 6 - i // 6 - 1


def front_kernel(
    heads, dk, buckets, blocks,
    rel_ref, len_ref, bid_ref, pad_ref, ag_ref, fg_ref, wq_ref, wo_ref,
    tok_hbm, far_hbm, cot_hbm,
    e_ref, inv_ref, qkv_ref, ctx_hbm, nrm_hbm, xt_hbm, mid_hbm, ct_hbm, wall_hbm,
    f1, fb, f3, cl, nrm, table, padc, mask, score, agc, fgc, wall, wn, call, xo,
    lsem, osem, wsend, wrecv, csend, crecv,
):
    qb = pl.program_id(0)
    dp, x = lax.axis_index("dp"), lax.axis_index("mp")
    d, rows = f1.shape
    cols = heads * dk
    half = cols // 2
    core = dp % 2
    other = (dp, 1 - x)
    sibling = (dp + 1 - 2 * core, x)
    near_blocks = blocks // 2
    part = pl.ds(core * half, half)
    far_part = pl.ds(cols + core * half, half)

    def local(i):
        src, dst = ((tok_hbm, f1), (far_hbm, fb), (cot_hbm, f3))[i]
        return pltpu.make_async_copy(src, dst, lsem.at[i])

    def out(i):
        src, dst = (
            (call, ctx_hbm), (nrm, nrm_hbm), (f1, mid_hbm), (cl, ct_hbm.at[:, pl.ds(0, rows)]), (wall, wall_hbm)
        )[i]
        return pltpu.make_async_copy(src, dst, osem.at[i])

    def xt_out(b):
        return pltpu.make_async_copy(xo.at[:, lanes(b)], xt_hbm.at[:, lanes(b)], osem.at[5 + b])

    w_copy = remote(wo_ref.at[part], wall.at[far_part], wsend.at[0], wrecv.at[0], other)
    w_pass = remote(wall.at[far_part], wall.at[far_part], wsend.at[1], wrecv.at[1], sibling)
    c_copy = remote(cl.at[:, pl.ds(0, BLK)], ct_hbm.at[:, pl.ds(rows, BLK)], wsend.at[2], wrecv.at[2], other)

    def ctx_copy(b):
        there = (b + near_blocks) % blocks
        return remote(
            call.at[pl.ds(0, cols), lanes(b)], call.at[pl.ds(cols, cols), lanes(there)],
            csend.at[b], crecv.at[b], other,
        )

    @pl.when(qb == 0)
    def _():
        for i in (2, 0, 1):
            local(i).start()
        meet([other, sibling])
        w_copy.start()
        wall[0:cols, :] = wo_ref[...]
        local(2).wait()
        cl[...] = f3[...].astype(BF)
        c_copy.start()
        out(3).start()
        agc[...] = column(ag_ref[...])
        fgc[...] = column(fg_ref[...])
        local(0).wait()
        local(1).wait()
        for b in range(blocks):
            ls = slice(b * BLK, (b + 1) * BLK)
            v = f1[:, ls] if b < near_blocks else fb[:, b * BLK - rows : (b + 1) * BLK - rows].astype(F32)
            nrm[:, ls] = (v * norm_scale(v) * agc[...]).astype(BF)
            qkv_ref[:, ls] = dot(wq_ref[...], nrm[:, ls], ((1,), (0,))).astype(BF)
        out(1).start()
        for i in range(2):
            start = (1 - x) * rows if i else x * rows
            line = pad_ref[:, pl.ds(pl.multiple_of(start, BLK), rows)].astype(F32)
            padc[i * rows : (i + 1) * rows, :] = jnp.broadcast_to(line, (8, rows)).T
        ids = bid_ref[...]
        for hh in range(heads):
            line = jnp.zeros((1, SPAN), F32)
            for b in range(buckets):
                line = jnp.where(ids == b, rel_ref[b, hh], line)
            turned = pltpu.roll(
                jnp.broadcast_to(line, (BLK, SPAN)), 0, 1, stride=1, stride_axis=0
            )
            for g in range(5):
                table[hh, g] = turned[:, BLK * (4 - g) : BLK * (5 - g)]

    @pl.when(qb == 1)
    def _():
        w_copy.wait()
        w_pass.start()

    q_true = (qb + near_blocks * x) % blocks

    q_pos = q_true * BLK + lax.broadcasted_iota(jnp.int32, (1, BLK), 1)
    k_iota = lax.broadcasted_iota(jnp.int32, (BLK, BLK), 0)
    for kb in range(blocks):
        k_pos = (kb + near_blocks * x) % blocks * BLK + k_iota
        bound = 0
        q_doc = jnp.zeros((1, BLK), jnp.int32)
        k_doc = jnp.zeros((BLK, BLK), jnp.int32)
        for i in range(len_ref.shape[1]):
            bound = bound + len_ref[0, i]
            q_doc = q_doc + (q_pos >= bound).astype(jnp.int32)
            k_doc = k_doc + (k_pos >= bound).astype(jnp.int32)
        krows = slice(kb * BLK, (kb + 1) * BLK)
        seen = (padc[krows, 0:1] > 0.5) | (k_pos == q_pos)
        mask[krows, :] = jnp.where((k_doc == q_doc) & seen, 0.0, -1000000000.0)

    def head_rows(h, group):
        return pl.ds(pl.multiple_of(group * cols + h * dk, dk), dk)

    def diagonal(kb):
        return near_diagonal((kb + near_blocks * x) % blocks - q_true)

    def head(h, carry):
        qh = qkv_ref[head_rows(h, 0), lanes(qb)]
        peak = None
        for kb in range(blocks):
            krows = slice(kb * BLK, (kb + 1) * BLK)
            s = dot(qkv_ref[head_rows(h, 1), krows], qh, ((0,), (0,)))
            diag = diagonal(kb)
            s = s + table[h, diag] + mask[krows, :]
            score[krows, :] = s
            top = jnp.max(s, axis=0, keepdims=True)
            peak = top if peak is None else jnp.maximum(peak, top)
        total = jnp.zeros((1, BLK), F32)
        ctx = jnp.zeros((dk, BLK), F32)
        for kb in range(blocks):
            krows = slice(kb * BLK, (kb + 1) * BLK)
            e = jnp.exp(score[krows, :] - peak)
            total = total + jnp.sum(e, axis=0, keepdims=True)
            e_low = e.astype(BF)
            e_ref[h, 0, krows, :] = e_low
            ctx = ctx + dot(qkv_ref[head_rows(h, 2), krows], e_low, ((1,), (0,)))
        inv = 1.0 / total
        inv_ref[h, 0] = inv
        call[head_rows(h, 0), lanes(qb)] = (ctx * inv).astype(BF)
        return carry

    lax.fori_loop(0, heads, head, 0)
    ctx_copy(qb).start()

    @pl.when(qb == blocks - 1)
    def _():
        w_pass.wait()
        wn[...] = wall[...].astype(F32).T.astype(BF)
        out(4).start()
        for i in range(blocks):
            b = (i + near_blocks) % blocks
            ctx_copy(i).wait()
            ls = slice(b * BLK, (b + 1) * BLK)
            v = dot(wn[...], call[:, ls], ((1,), (0,)))
            if b < near_blocks:
                v = v + f1[:, ls]
                f1[:, ls] = v
            else:
                v = v + fb[:, b * BLK - rows : (b + 1) * BLK - rows].astype(F32)
            xo[:, ls] = (v * norm_scale(v) * fgc[...]).astype(BF)
            xt_out(b).start()
        out(0).start()
        out(2).start()
        c_copy.wait()
        for i in range(5):
            out(i).wait()
        for b in range(blocks):
            xt_out(b).wait()


def front(rel, lengths, pad, again, fgain, wq, wo, tok, far, cot, heads, dk):
    d, rows = tok.shape
    seq = 2 * rows
    cols = heads * dk
    blocks = seq // BLK
    buckets = rel.shape[0]
    bids = jnp.asarray(lane_buckets(buckets))
    one = pl.Buffered(1)
    dma = pltpu.SemaphoreType.DMA
    any_spec = pl.BlockSpec(memory_space=pl.ANY)
    smem = pl.BlockSpec(memory_space=pltpu.SMEM)

    def full(v):
        return pl.BlockSpec(v.shape, lambda i: (0, 0), pipeline_mode=one)

    return pl.pallas_call(
        functools.partial(front_kernel, heads, dk, buckets, blocks),
        grid=(blocks,),
        in_specs=[smem, smem, full(bids), full(pad), full(again), full(fgain), full(wq), full(wo)]
        + [any_spec] * 3,
        out_specs=[
            pl.BlockSpec((heads, 1, seq, BLK), lambda i: (0, i, 0, 0)),
            pl.BlockSpec((heads, 1, 1, BLK), lambda i: (0, i, 0, 0)),
            pl.BlockSpec((3 * cols, seq), lambda i: (0, 0)),
        ]
        + [any_spec] * 6,
        out_shape=[
            jax.ShapeDtypeStruct((heads, blocks, seq, BLK), BF),
            jax.ShapeDtypeStruct((heads, blocks, 1, BLK), F32),
            jax.ShapeDtypeStruct((3 * cols, seq), BF),
            jax.ShapeDtypeStruct((2 * cols, seq), BF),
            jax.ShapeDtypeStruct((d, seq), BF),
            jax.ShapeDtypeStruct((d, seq), BF),
            jax.ShapeDtypeStruct((d, rows), F32),
            jax.ShapeDtypeStruct((d, seq), BF),
            jax.ShapeDtypeStruct((2 * cols, d), BF),
        ],
        scratch_shapes=[
            pltpu.VMEM((d, rows), F32),
            pltpu.VMEM((d, rows), BF),
            pltpu.VMEM((d, rows), F32),
            pltpu.VMEM((d, rows), BF),
            pltpu.VMEM((d, seq), BF),
            pltpu.VMEM((heads, 5, BLK, BLK), F32),
            pltpu.VMEM((seq, 8), F32),
            pltpu.VMEM((seq, BLK), F32),
            pltpu.VMEM((seq, BLK), F32),
            pltpu.VMEM((d, 1), F32),
            pltpu.VMEM((d, 1), F32),
            pltpu.VMEM((2 * cols, d), BF),
            pltpu.VMEM((d, 2 * cols), BF),
            pltpu.VMEM((2 * cols, seq), BF),
            pltpu.VMEM((d, seq), BF),
            dma((3,)), dma((5 + blocks,)), dma((3,)), dma((3,)), dma((blocks,)), dma((blocks,)),
        ],
        compiler_params=pltpu.CompilerParams(
            vmem_limit_bytes=FF_VMEM, collective_id=2, has_side_effects=True
        ),
        cost_estimate=pl.CostEstimate(
            flops=16 * heads * seq * seq * dk + 10 * seq * d * cols,
            bytes_accessed=2 * heads * seq * seq + 30 * rows * d,
            transcendentals=heads * seq * seq,
        ),
    )(rel, lengths, bids, pad, again, fgain, wq, wo, tok, far, cot)


def ff_kernel(
    steps, done, extra,
    xt_hbm, w_hbm, ct_hbm, wo_hbm, mid_hbm, wq_hbm,
    grads_ref, din_hbm, near_hbm, far_hbm, back_hbm, half_hbm, hand_hbm, wfar_hbm,
    xt, ct, wg, wu, wo, hid, dg, du, din, stage, r1, r2, r3, r4, xs, xr, of,
    csem, wsem, s1, s2, s3, s4, t1, t2, t3, t4, xsem, osem, hsem,
):
    f, total = hid.shape
    rows = total // 2
    chunks = rows // BLK
    d = xt.shape[0]
    shard = d // 16
    dp, mp = lax.axis_index("dp"), lax.axis_index("mp")
    a = group_coords(dp // extra)
    peers = [flip(dp, m * extra) for m in GROUP_MASKS]
    other = (dp, 1 - mp)
    core = dp % 2
    sibling = dp + 1 - 2 * core
    bufs = (r1, r2, r3, r4)
    sends, recvs = (s1, s2, s3, s4), (t1, t2, t3, t4)
    end = steps - 1

    def weight_copy(kind, n):
        src, dst = ((w_hbm.at[0], wg), (w_hbm.at[1], wu), (wo_hbm, wo))[kind]
        return pltpu.make_async_copy(src.at[:, lanes(n)], dst.at[:, lanes(n)], wsem.at[kind, n])

    def tok_copy(n):
        src, dst, start, size = (
            (xt_hbm, xt, rows, BLK), (ct_hbm, ct, rows, BLK),
            (xt_hbm, xt, 0, rows), (ct_hbm, ct, 0, rows), (xt_hbm, xt, rows + BLK, BLK),
        )[n]
        part = pl.ds(start, size)
        return pltpu.make_async_copy(src.at[:, part], dst.at[:, part], csem.at[n])

    near_part, far_part = pl.ds(0, rows), pl.ds(rows, rows)
    c_far = remote(
        ct_hbm.at[:, pl.ds(BLK, BLK)], ct.at[:, pl.ds(rows + BLK, BLK)], csem.at[5], csem.at[6], other
    )
    x_copy = remote(xs, xr, xsem.at[0], xsem.at[1], other)
    back_copy = remote(of.at[:, pl.ds(0, 128)], back_hbm, xsem.at[2], xsem.at[3], other)
    wq_rows = wq_hbm.shape[0] // 2
    wq_part = pl.ds(core * wq_rows, wq_rows)
    w_copy = remote(wq_hbm.at[wq_part], wfar_hbm.at[wq_part], xsem.at[4], xsem.at[5], other)
    w_pass = remote(wfar_hbm.at[wq_part], wfar_hbm.at[wq_part], xsem.at[6], xsem.at[7], (sibling, mp))
    mid_copy = pltpu.make_async_copy(mid_hbm, din.at[:, far_part], osem.at[3])

    def hop(level, n):
        half = 8 >> level
        away = pl.ds((1 - a[level]) * half, half)
        src = stage.at[away] if level == 0 else bufs[level - 1].at[n, away]
        return remote(src, bufs[level].at[n], sends[level].at[n], recvs[level].at[n], (peers[level], mp))

    def hand_copy(n):
        if isinstance(n, int) and n == done:
            return pltpu.make_async_copy(r2.at[n], half_hbm, hsem.at[0])
        return pltpu.make_async_copy(r1.at[n], hand_hbm.at[n - done - 1], hsem.at[n - done])

    def absorb_first(n):
        hop(0, n).wait()
        r1[n] = stage[pl.ds(a[0] * 8, 8)] + r1[n]
        if isinstance(n, int):
            hand_copy(n).start()
            return

        @pl.when(n <= done)
        def _():
            hop(1, n).start()

        @pl.when(n > done)
        def _():
            hand_copy(n).start()

    def absorb(level, n):
        half = 8 >> level
        hop(level, n).wait()
        kept = bufs[level - 1][n, pl.ds(a[level] * half, half)]
        if level < 3:
            bufs[level][n] = kept + bufs[level][n]
            if n < done:
                hop(level + 1, n).start()
            else:
                hand_copy(n).start()
        else:
            both = kept.astype(F32) + bufs[level][n].astype(F32)
            for w in range(3):
                grads_ref[w, :, n * BLK : (n + 1) * BLK] = both[0, w]

    scale = np.float32(np.sqrt(2 / np.pi))

    def place(u):
        early, late = u // steps, (u - 4) // steps
        is_far0 = (early == 0) * 1
        is_far1 = (late == 1) * 1
        v = u - steps
        n = v - steps * (u // (2 * steps + 4))
        near_j, near_c = n // 2, n % 2
        j = is_far0 * u + is_far1 * (u - steps - 4) + (1 - is_far0 - is_far1) * near_j
        c = is_far0 * chunks + is_far1 * (chunks + 1) + (1 - is_far0 - is_far1) * near_c
        return j, c

    def substep(u):
        j, c = place(u)
        pj, pc = place(u - 1)
        pj = pj + (u == 0) * 1
        fcols, tok = lanes(j), lanes(c)
        pcols, ptok = lanes(pj), lanes(pc)
        gate = dot(wg[:, fcols], xt[:, tok], ((0,), (0,)))
        up = dot(wu[:, fcols], xt[:, tok], ((0,), (0,)))
        dh = dot(wo[:, fcols], ct[:, tok], ((0,), (0,)))
        backward(pcols, ptok)
        sq = gate * gate
        t = jnp.tanh(scale * gate * (1.0 + 0.044715 * sq))
        half = 0.5 * (1.0 + t)
        act = gate * half
        slope = half + 0.5 * gate * (1.0 - t * t) * (scale * (1.0 + (3 * 0.044715) * sq))
        hid[fcols, tok] = (act * up).astype(BF)
        dg[fcols, tok] = (dh * (up * slope)).astype(BF)
        du[fcols, tok] = (dh * act).astype(BF)

    def backward(rs, tok):
        din[:, tok] += dot(wg[:, rs], dg[rs, tok], ((1,), (0,))) + dot(wu[:, rs], du[rs, tok], ((1,), (0,)))

    per = 4 * shard

    def grads(j):
        z = j // end
        for w in range(3):
            right = (hid, dg, du)[w][lanes(j), :]
            for q in range(4):
                rs = slice(q * per, (q + 1) * per)
                left = ct[rs, :] if w == 0 else xt[rs, :]
                part = dot(left, right, ((1,), (1,)))
                for k in range(4):
                    at = block_position(4 * q + k, Y_FIRST)
                    at = at + z * (block_position(4 * q + k, Z_FIRST) - at)
                    stage[at, w, 0:shard, :] = part[k * shard : (k + 1) * shard].astype(BF)
        hop(0, j).start()

    def out_part(n):
        return dot(wo[...], hid[:, lanes(n)], ((1,), (0,)))

    meet([(p, mp) for p in peers] + [other] + ([(sibling, mp)] if extra > 1 else []))
    c_far.start()
    w_copy.start()
    tok_copy(0).start()
    tok_copy(1).start()
    for n in range(steps):
        for kind in range(3):
            weight_copy(kind, n).start()
    for n in range(2, 5):
        tok_copy(n).start()
    din[...] = jnp.zeros_like(din)
    stage[...] = jnp.zeros_like(stage)
    before = place(-1)[1]
    dg[0:BLK, before * BLK : (before + 1) * BLK] = jnp.zeros((BLK, BLK), BF)
    du[0:BLK, before * BLK : (before + 1) * BLK] = jnp.zeros((BLK, BLK), BF)
    tok_copy(0).wait()
    tok_copy(1).wait()
    count = 2 * chunks * steps
    far_end = 2 * steps + 4

    def step(u, carry):
        @pl.when(u < steps)
        def _():
            for kind in range(3):
                weight_copy(kind, u).wait()

        @pl.when(u == steps)
        def _():
            tok_copy(2).wait()
            tok_copy(3).wait()

        @pl.when(u == steps + 4)
        def _():
            tok_copy(4).wait()
            c_far.wait()

        @pl.when(u < count)
        def _():
            substep(u)

        @pl.when(u == far_end)
        def _():
            xs[...] = din[:, far_part].astype(BF)
            x_copy.start()
            mid_copy.start()

        @pl.when(u == count)
        def _():
            pj, pc = place(count - 1)
            backward(lanes(pj), lanes(pc))

            def one(n, carry):
                of[:, lanes(n)] = out_part(n + chunks).astype(BF)
                return carry

            lax.fori_loop(0, chunks, one, 0)

        n = (u - far_end + 1) // 2

        @pl.when((u >= far_end + 1) & (u % 2 == (far_end + 1) % 2))
        def _():
            absorb_first(n - 1)

        @pl.when((u >= far_end - 1) & (u % 2 == (far_end + 1) % 2))
        def _():
            for at, events in ((3, ((1, 0),)), (5, ((1, 1), (2, 0))), (6, ((2, 1), (3, 0)))):
                @pl.when(n == at)
                def _():
                    for level, block in events:
                        absorb(level, block)

            grads(n)

        @pl.when(u == far_end + 5)
        def _():
            w_copy.wait()
            w_pass.start()

        return carry

    lax.fori_loop(0, count + 2, step, 0)
    x_copy.wait()
    back_copy.start()
    rest = far_hbm.shape[1]
    far_copy = pltpu.make_async_copy(of.at[:, pl.ds(128, rest)], far_hbm, osem.at[0])
    far_copy.start()
    mid_copy.wait()

    def one(n, carry):
        at = lanes(n + chunks)
        din[:, at] = din[:, at] + out_part(n)
        return carry

    lax.fori_loop(0, chunks, one, 0)
    near_copy = pltpu.make_async_copy(din.at[:, far_part], near_hbm, osem.at[1])
    near_copy.start()
    absorb_first(end)
    absorb(1, done)
    din[:, near_part] += xr[...].astype(F32)
    din_copy = pltpu.make_async_copy(din.at[:, near_part], din_hbm, osem.at[2])
    din_copy.start()
    absorb(3, 1)
    w_pass.wait()

    for n in range(done, steps):
        hand_copy(n).wait()
    far_copy.wait()
    near_copy.wait()
    din_copy.wait()
    back_copy.wait()


def ff_all(xt, ct, w2, wo, mid, wq, extra):
    d, total = xt.shape
    f = wo.shape[1]
    rows = total // 2
    steps = f // BLK
    done = FF_DONE
    shard = d // 16
    spad = -(-shard // 16) * 16
    dma = pltpu.SemaphoreType.DMA
    any_spec = pl.BlockSpec(memory_space=pl.ANY)
    return pl.pallas_call(
        functools.partial(ff_kernel, steps, done, extra),
        in_specs=[any_spec] * 6,
        out_specs=[pl.BlockSpec(memory_space=pltpu.VMEM)] + [any_spec] * 7,
        out_shape=[
            jax.ShapeDtypeStruct((3, spad, done * BLK), F32),
            jax.ShapeDtypeStruct((d, rows), F32),
            jax.ShapeDtypeStruct((d, rows), F32),
            jax.ShapeDtypeStruct((d, rows - 128), BF),
            jax.ShapeDtypeStruct((d, 128), BF),
            jax.ShapeDtypeStruct((4, 3, spad, BLK), BF),
            jax.ShapeDtypeStruct((steps - done - 1, 8, 3, spad, BLK), BF),
            jax.ShapeDtypeStruct(wq.shape, BF),
        ],
        scratch_shapes=[
            pltpu.VMEM((d, total), BF),
            pltpu.VMEM((d, total), BF),
            pltpu.VMEM((d, f), BF),
            pltpu.VMEM((d, f), BF),
            pltpu.VMEM((d, f), BF),
            pltpu.VMEM((f, total), BF),
            pltpu.VMEM((f, total), BF),
            pltpu.VMEM((f, total), BF),
            pltpu.VMEM((d, total), F32),
            pltpu.VMEM((16, 3, spad, BLK), BF),
            pltpu.VMEM((steps, 8, 3, spad, BLK), BF),
            pltpu.VMEM((done + 1, 4, 3, spad, BLK), BF),
            pltpu.VMEM((done, 2, 3, spad, BLK), BF),
            pltpu.VMEM((done, 1, 3, spad, BLK), BF),
            pltpu.VMEM((d, rows), BF),
            pltpu.VMEM((d, rows), BF),
            pltpu.VMEM((d, rows), BF),
            dma((7,)),
            dma((3, steps)),
            dma((steps,)), dma((done + 1,)), dma((done,)), dma((done,)),
            dma((steps,)), dma((done + 1,)), dma((done,)), dma((done,)),
            dma((8,)),
            dma((4,)),
            dma((steps - done,)),
        ],
        compiler_params=pltpu.CompilerParams(
            vmem_limit_bytes=FF_VMEM, collective_id=0, has_side_effects=True
        ),
        cost_estimate=pl.CostEstimate(
            flops=18 * total * d * f,
            bytes_accessed=6 * d * f + 16 * total * d,
            transcendentals=total * f,
        ),
    )(xt, w2, ct, wo, mid, wq)


def tail_kernel(
    heads, dk, buckets, blocks, extra, first,
    bid_ref, qkv_ref, e_ref, inv_ref, wall_ref, ctx_ref, ag_ref, fg_ref, early_ref,
    din_hbm, mid_hbm, cot_hbm, tok_hbm, nrm_hbm, wq_hbm, wfar_hbm, near_hbm, back_hbm, far_hbm, part_hbm, hand_hbm,
    ig_hbm, res_hbm, gq_ref, go_ref, small_ref, ffo_ref, ffi_ref,
    f1, f2, f3, f4, nrm, wq, wn, wf, alow, dctx, dcs, osend, orecv, fsum, agc, fgc,
    dp_s, dkv, tally, dproj, dfar, grad, back0, back,
    sa, sb_, a1, a2, a3, a4, b1, b2, b3, b4, hk, hm, h2, h3, h4, sv, rv,
    lsem, ksem, xs_sem, xr_sem, cs_sem, cr_sem, bs_sem, br_sem, hs_sem, hr_sem,
):
    qb = pl.program_id(0)
    dp, x = lax.axis_index("dp"), lax.axis_index("mp")
    d, rows = f2.shape
    cols = heads * dk
    shard = d // 16
    a = group_coords(dp // extra)
    peers = [flip(dp, m * extra) for m in GROUP_MASKS]
    other = (dp, 1 - x)
    near_blocks = blocks // 2
    near_part, far_part = pl.ds(0, rows), pl.ds(rows, rows)
    halves = ((sa, a1, a2, a3, a4), (sb_, b1, b2, b3, b4))
    orders = (Y_FIRST, Z_FIRST)
    copies = (
        (din_hbm, f1), (mid_hbm, f2), (cot_hbm, f3), (tok_hbm, f2), (nrm_hbm, nrm), (wq_hbm, wq), (wfar_hbm, wq),
        (back_hbm, back0), (near_hbm.at[:, pl.ds(0, BLK)], f4), (near_hbm.at[:, pl.ds(BLK, BLK)], f4),
        (f4, res_hbm.at[:, pl.ds(0, BLK)]), (f4, res_hbm.at[:, pl.ds(BLK, BLK)]),
    )

    def local(i):
        return pltpu.make_async_copy(copies[i][0], copies[i][1], lsem.at[i])

    def x_copy(i, src, dst):
        return remote(src, dst, xs_sem.at[i], xr_sem.at[i], other)

    dctx_copy = x_copy(0, dcs, dctx.at[:, far_part])
    o_copy = x_copy(1, osend, orecv)
    dproj_copy = x_copy(2, dproj.at[:, far_part], dfar)

    def back_copy(i):
        part = pl.ds(i * 128, 128)
        return x_copy(3 + i, far_hbm.at[:, part], back.at[:, part])

    def hop(side, level):
        half = 8 >> level
        c = orders[side][level]
        away = pl.ds((1 - a[c]) * half, half)
        bufs = halves[side]
        return remote(
            bufs[level].at[away], bufs[level + 1], cs_sem.at[side, level], cr_sem.at[side, level], (peers[c], x)
        )

    def absorb(side, level):
        half = 8 >> level
        bufs = halves[side]
        hop(side, level).wait()
        kept = bufs[level][pl.ds(a[orders[side][level]] * half, half)]
        if level < 3:
            bufs[level + 1][...] = kept + bufs[level + 1][...]
            hop(side, level + 1).start()
            return
        both = (kept.astype(F32) + bufs[level + 1][...].astype(F32))[0, 0:shard]
        outs = (gq_ref.at[0], gq_ref.at[1]) if side == 0 else (gq_ref.at[2], go_ref)
        for i in range(2):
            outs[i][...] = both[:, i * cols : (i + 1) * cols]

    def order_of(block):
        return Z_FIRST if block == 4 else Y_FIRST

    def keep_copy(block):
        if block == 0:
            return pltpu.make_async_copy(part_hbm.at[pl.ds(a[2] * 2, 2)], hm, ksem.at[0])
        keep = pl.ds(a[order_of(block)[1]] * 4, 4)
        return pltpu.make_async_copy(hand_hbm.at[block - 1, keep], hk.at[block - 1], ksem.at[block])

    def hand_hop(level, block):
        half = 8 >> level
        c = order_of(block)[level]
        away = pl.ds((1 - a[c]) * half, half)
        if level == 1:
            src, dst = hand_hbm.at[block - 1, away], h2.at[block - 1]
        elif level == 2:
            src, dst = part_hbm.at[away] if block == 0 else h2.at[block - 1, away], h3.at[block]
        else:
            src, dst = h3.at[block, away], h4.at[block]
        return remote(src, dst, hs_sem.at[level, block], hr_sem.at[level, block], (peers[c], x))

    def put_grads(w, block, value):
        at = slice(block * BLK, (block + 1) * BLK)
        if w == 0:
            ffo_ref[:, at] = value
        else:
            ffi_ref[:, w - 1, at] = value

    def hand_absorb(level, block):
        half = 8 >> level
        keep = pl.ds(a[order_of(block)[level]] * half, half)
        hand_hop(level, block).wait()
        if level == (2 if block == 0 else 1):
            keep_copy(block).wait()
            kept = hm[...] if block == 0 else hk[block - 1]
        else:
            kept = h2[block - 1, keep] if level == 2 else h3[block, keep]
        if level == 1:
            h2[block - 1] = kept + h2[block - 1]
        elif level == 2:
            h3[block] = kept + h3[block]
        else:
            both = kept.astype(F32) + h4[block].astype(F32)
            for w in range(3):
                put_grads(w, first + block, both[0, w, 0:shard])
        if level < 3:
            hand_hop(level + 1, block).start()

    def round_copy(i):
        who = other if i == 4 else (peers[(0, 2, 3, 1)[i]], x)
        return remote(sv.at[i], rv.at[i], bs_sem.at[i], br_sem.at[i], who)

    def round_end(i):
        round_copy(i).wait()
        sv[i + 1] = sv[i] + rv[i]
        if i < 4:
            round_copy(i + 1).start()

    def out_copy(r):
        return pltpu.make_async_copy(f3.at[:, lanes(r)], ig_hbm.at[:, lanes(r)], lsem.at[len(copies) + r])

    def lane_sum(v):
        total = v[:, 0:128]
        for i in range(1, v.shape[1] // 128):
            total = total + v[:, i * 128 : (i + 1) * 128]
        return total

    @pl.when(qb == 0)
    def _():
        for i in range(3):
            local(i).start()
        meet([(p, x) for p in peers] + [other])
        back_copy(0).start()
        for block in (0, 4, 1, 2, 3):
            hand_hop(2 if block == 0 else 1, block).start()
        agc[...] = column(ag_ref[...])
        fgc[...] = column(fg_ref[...])
        dkv[...] = jnp.zeros_like(dkv)
        tally[...] = jnp.zeros_like(tally)
        sa[...] = jnp.zeros_like(sa)
        sb_[...] = jnp.zeros_like(sb_)
        fsum[...] = jnp.zeros_like(fsum)
        for i in range(3):
            local(i).wait()

        def norm_rows(r, carry):
            ls = lanes(r)
            v = f2[:, ls]
            c = f1[:, ls]
            scale = norm_scale(v)
            n = v * scale
            cg = c * fgc[...]
            m = jnp.mean(cg * n, axis=0, keepdims=True)
            gm = f3[:, ls] + scale * (cg - n * m)
            fsum[...] += lane_sum(c * n)
            f1[:, ls] = gm
            alow[:, ls] = gm.astype(BF)
            return carry

        lax.fori_loop(0, near_blocks, norm_rows, 0)
        dcs[...] = dot(wall_ref[cols : 2 * cols, :], alow[...], ((1,), (0,))).astype(BF)
        dctx_copy.start()
        for i in (3, 4, 5, 7, 8):
            local(i).start()
        for block in (0, 4, 1, 2, 3):
            keep_copy(block).start()
        dctx[:, near_part] = dot(wall_ref[0:cols, :], alow[...], ((1,), (0,))).astype(BF)
        osend[...] = dot(alow[...], ctx_ref[cols : 2 * cols, near_part], ((1,), (1,))).astype(BF)
        o_copy.start()
        grad[:, 3 * cols : 4 * cols] = dot(alow[...], ctx_ref[0:cols, near_part], ((1,), (1,)))
        for w in range(3):
            for block in range(first):
                put_grads(w, block, early_ref[w, 0:shard, block * BLK : (block + 1) * BLK])
        dctx_copy.wait()
        back_copy(1).start()

    @pl.when(qb == 1)
    def _():
        local(5).wait()
        wn[...] = wq[...].astype(F32).T.astype(BF)
        local(6).start()
        hand_absorb(2, 0)

    @pl.when(qb == 2)
    def _():
        local(6).wait()
        wf[...] = wq[...].astype(F32).T.astype(BF)
        hand_absorb(1, 1)
        hand_absorb(1, 4)
        local(7).wait()
        local(8).wait()
        back_copy(0).wait()
        f4[:, 0:128] += back0[...].astype(F32)
        f4[:, 128:BLK] += back[:, 0:128].astype(F32)
        local(10).start()

    @pl.when(qb == 3)
    def _():
        hand_absorb(3, 0)
        hand_absorb(2, 1)

    q_true = (qb + near_blocks * x) % blocks

    def head(h, carry):
        def head_rows(group):
            return pl.ds(pl.multiple_of(group * cols + h * dk, dk), dk)

        inv = inv_ref[h, 0]
        qh = qkv_ref[head_rows(0), lanes(qb)]
        scaled = (dctx[head_rows(0), lanes(qb)].astype(F32) * inv).astype(BF)
        inner = jnp.zeros((1, BLK), F32)
        for kb in range(blocks):
            krows = slice(kb * BLK, (kb + 1) * BLK)
            g = dot(qkv_ref[head_rows(2), krows], scaled, ((0,), (0,)))
            dp_s[krows, :] = g
            inner = inner + jnp.sum(e_ref[h, 0, krows, :].astype(F32) * g, axis=0, keepdims=True)
        inner = inner * inv
        dq = jnp.zeros((dk, BLK), F32)
        for kb in range(blocks):
            krows = slice(kb * BLK, (kb + 1) * BLK)
            e = e_ref[h, 0, krows, :]
            ds = (e.astype(F32) * (dp_s[krows, :] - inner)).astype(BF)
            dkv[head_rows(0), krows] += dot(qh, ds, ((1,), (1,)))
            dkv[head_rows(1), krows] += dot(scaled, e, ((1,), (1,)))
            dq = dq + dot(qkv_ref[head_rows(1), krows], ds, ((1,), (0,)))
            tally[h, near_diagonal((kb + near_blocks * x) % blocks - q_true)] += ds.astype(F32)
        dproj[head_rows(0), lanes(qb)] = dq.astype(BF)
        return carry

    lax.fori_loop(0, heads, head, 0)

    @pl.when(qb == blocks - 1)
    def _():
        dproj[cols : 3 * cols, :] = dkv[...].astype(BF)
        dproj_copy.start()
        back_copy(2).start()
        local(3).wait()
        local(4).wait()
        per = 4 * shard

        def grad_rows(q, carry):
            rs = pl.ds(pl.multiple_of(q * per, 16), per)
            grad[rs, 0 : 3 * cols] = dot(nrm[rs, :], dproj[...], ((1,), (1,)))
            return carry

        lax.fori_loop(0, 4, grad_rows, 0)
        o_copy.wait()
        grad[:, 3 * cols : 4 * cols] += orecv[...].astype(F32)
        for side in range(2):
            for k in range(16):
                halves[side][0][block_position(k, orders[side]), 0:shard, :] = grad[
                    k * shard : (k + 1) * shard, 2 * side * cols : 2 * (side + 1) * cols
                ].astype(BF)
            hop(side, 0).start()
        hand_absorb(1, 2)
        hand_absorb(2, 4)

        def near_rows(r, carry):
            f3[:, lanes(r)] = dot(wn[...], dproj[:, lanes(r)], ((1,), (0,)))
            return carry

        lax.fori_loop(0, near_blocks, near_rows, 0)
        absorb(0, 0)
        absorb(1, 0)
        hand_absorb(1, 3)
        hand_absorb(3, 1)
        hand_absorb(2, 2)
        ids = bid_ref[...]
        hot = ids == lax.broadcasted_iota(jnp.int32, (buckets, SPAN), 0)
        out_lane = lax.broadcasted_iota(jnp.int32, (buckets, 128), 1)
        sub = lax.broadcasted_iota(jnp.int32, (8, SPAN), 0)
        sv[0] = jnp.zeros(sv.shape[1:], F32)

        def bias_sums(hh, carry):
            line = jnp.zeros((8, SPAN), F32)
            for g in range(BLK // 8):
                group = slice(8 * g, 8 * g + 8)
                parts = [tally[hh, i, group, :] for i in (4, 3, 2, 1, 0)]
                strip = jnp.concatenate(parts + [jnp.zeros((8, BLK), F32)], axis=1)
                line = line + (strip if g == 0 else pltpu.roll(strip, SPAN - 8 * g, 1))
            for bit in (1, 2, 4):
                line = jnp.where((sub // bit) % 2 == 1, pltpu.roll(line, SPAN - bit, 1), line)
            sums = jnp.sum(line, axis=0, keepdims=True)
            col = jnp.sum(jnp.where(hot, sums, 0.0), axis=1, keepdims=True)
            sv[0, 0:buckets, :] = jnp.where(out_lane == x * heads + hh, col, sv[0, 0:buckets, :])
            return carry

        lax.fori_loop(0, heads, bias_sums, 0)
        product = wn[...].astype(F32) * grad[:, 0 : 3 * cols]
        again = lane_sum(product[:, 0:512]).T
        rest = product[:, 512 : 3 * cols]
        again = jnp.sum(again, axis=0, keepdims=True) + jnp.sum(rest.T, axis=0, keepdims=True)
        again = again / ag_ref[...]
        fgain = jnp.sum(fsum[...].T, axis=0, keepdims=True)
        lines = -(-d // 128)
        for i in range(lines):
            n = min(128, d - 128 * i)
            sv[0, buckets + i : buckets + i + 1, 0:n] = again[:, 128 * i : 128 * i + n]
            sv[0, buckets + lines + i : buckets + lines + i + 1, 0:n] = fgain[:, 128 * i : 128 * i + n]
        round_copy(0).start()
        absorb(0, 1)
        absorb(1, 1)
        round_end(0)
        hand_absorb(3, 4)
        hand_absorb(2, 3)
        local(10).wait()
        local(9).start()
        round_end(1)
        dproj_copy.wait()

        def last_norm(r, carry):
            ls = lanes(r)
            c = f3[:, ls] + dot(wf[...], dfar[:, ls], ((1,), (0,)))
            v = f2[:, ls]
            scale = norm_scale(v)
            n = v * scale
            cg = c * agc[...]
            m = jnp.mean(cg * n, axis=0, keepdims=True)
            f3[:, ls] = f1[:, ls] + scale * (cg - n * m)
            out_copy(r).start()
            return carry

        lax.fori_loop(0, near_blocks, last_norm, 0)
        absorb(0, 2)
        absorb(1, 2)
        hand_absorb(3, 2)
        round_end(2)
        back_copy(1).wait()
        back_copy(2).wait()
        local(9).wait()
        f4[...] += back[:, 128 : 128 + BLK].astype(F32)
        local(11).start()
        hand_absorb(3, 3)
        round_end(3)
        absorb(0, 3)
        absorb(1, 3)
        round_end(4)
        small_ref[...] = sv[5]
        local(11).wait()
        for r in range(near_blocks):
            out_copy(r).wait()


def tail(qkv, e, inv, wall, ctx, again, fgain, early, din, mid, cot, tok, nrm, wq, wfar, near_out, back, far,
         half_way, hand, buckets, heads, dk, extra, f):
    d, rows = tok.shape
    seq = 2 * rows
    cols = heads * dk
    blocks = seq // BLK
    near = blocks // 2
    shard = d // 16
    spad = -(-shard // 16) * 16
    later = hand.shape[0] + 1
    first = early.shape[2] // BLK
    lines = -(-(buckets + 2 * -(-d // 128)) // 8) * 8
    bids = jnp.asarray(lane_buckets(buckets))
    one = pl.Buffered(1)
    dma = pltpu.SemaphoreType.DMA
    any_spec = pl.BlockSpec(memory_space=pl.ANY)

    def full(v):
        return pl.BlockSpec(v.shape, lambda i: (0,) * len(v.shape), pipeline_mode=one)

    def chain(width):
        return [pltpu.VMEM((n, spad, width), BF) for n in (16, 8, 4, 2, 1)]

    outs = [
        jax.ShapeDtypeStruct((3, shard, cols), F32),
        jax.ShapeDtypeStruct((shard, cols), F32),
        jax.ShapeDtypeStruct((lines, 128), F32),
        jax.ShapeDtypeStruct((shard, f), F32),
        jax.ShapeDtypeStruct((shard, 2, f), F32),
    ]
    a_chain, b_chain = chain(2 * cols), chain(2 * cols)
    return pl.pallas_call(
        functools.partial(tail_kernel, heads, dk, buckets, blocks, extra, first),
        grid=(blocks,),
        in_specs=[
            full(bids),
            full(qkv),
            pl.BlockSpec((heads, 1, seq, BLK), lambda i: (0, i, 0, 0)),
            pl.BlockSpec((heads, 1, 1, BLK), lambda i: (0, i, 0, 0)),
            full(wall),
            full(ctx),
            full(again),
            full(fgain),
            full(early),
        ]
        + [any_spec] * 12,
        out_specs=[any_spec, any_spec] + [full(v) for v in outs],
        out_shape=[jax.ShapeDtypeStruct((d, rows), F32), jax.ShapeDtypeStruct((d, rows), F32)] + outs,
        scratch_shapes=[
            pltpu.VMEM((d, rows), F32),
            pltpu.VMEM((d, rows), F32),
            pltpu.VMEM((d, rows), F32),
            pltpu.VMEM((d, BLK), F32),
            pltpu.VMEM((d, seq), BF),
            pltpu.VMEM((3 * cols, d), BF),
            pltpu.VMEM((d, 3 * cols), BF),
            pltpu.VMEM((d, 3 * cols), BF),
            pltpu.VMEM((d, rows), BF),
            pltpu.VMEM((cols, seq), BF),
            pltpu.VMEM((cols, rows), BF),
            pltpu.VMEM((d, cols), BF),
            pltpu.VMEM((d, cols), BF),
            pltpu.VMEM((d, 128), F32),
            pltpu.VMEM((d, 1), F32),
            pltpu.VMEM((d, 1), F32),
            pltpu.VMEM((seq, BLK), F32),
            pltpu.VMEM((2 * cols, seq), F32),
            pltpu.VMEM((heads, 5, BLK, BLK), F32),
            pltpu.VMEM((3 * cols, seq), BF),
            pltpu.VMEM((3 * cols, rows), BF),
            pltpu.VMEM((d, 4 * cols), F32),
            pltpu.VMEM((d, 128), BF),
            pltpu.VMEM((d, rows - 128), BF),
            a_chain[0],
            b_chain[0],
        ]
        + a_chain[1:]
        + b_chain[1:]
        + [
            pltpu.VMEM((later - 1, 4, 3, spad, BLK), BF),
            pltpu.VMEM((2, 3, spad, BLK), BF),
            pltpu.VMEM((later - 1, 4, 3, spad, BLK), BF),
            pltpu.VMEM((later, 2, 3, spad, BLK), BF),
            pltpu.VMEM((later, 1, 3, spad, BLK), BF),
            pltpu.VMEM((6, lines, 128), F32),
            pltpu.VMEM((5, lines, 128), F32),
            dma((12 + near,)),
            dma((later,)),
            dma((6,)), dma((6,)),
            dma((2, 4)), dma((2, 4)),
            dma((5,)), dma((5,)),
            dma((4, later)), dma((4, later)),
        ],
        compiler_params=pltpu.CompilerParams(
            vmem_limit_bytes=FF_VMEM, collective_id=1, has_side_effects=True
        ),
        cost_estimate=pl.CostEstimate(
            flops=32 * heads * seq * seq * dk + 8 * seq * d * 3 * cols,
            bytes_accessed=2 * heads * seq * seq + 30 * rows * d,
            transcendentals=0,
        ),
    )(bids, qkv, e, inv, wall, ctx, again, fgain, early, din, mid, cot, tok, nrm, wq, wfar, near_out, back, far,
      half_way, hand)


def take(array, index):
    return lax.dynamic_index_in_dim(array, index, 0, keepdims=False)


def per_device(
    tokens,
    cotangent,
    doc_lengths,
    pad_mask,
    attn_gain,
    qkv_weight,
    rel_table,
    out_weight,
    ff_gain,
    ff_in_weight,
    ff_out_weight,
):
    rows, d = tokens.shape
    n_dp = lax.axis_size("dp")
    n_mp = lax.axis_size("mp")
    cols = qkv_weight.shape[2]
    buckets, heads = rel_table.shape
    dk = cols // heads
    me = lax.axis_index("dp")
    shard = d // n_dp
    extra = n_dp // 16

    def hop(v, mask):
        return lax.ppermute(v, "dp", [(i, i ^ mask) for i in range(n_dp)])

    def bit(b):
        return (me >> b) & 1

    def finish(g):
        parts = [g.reshape((extra, shard) + g.shape[1:])]
        for b in reversed(range(extra.bit_length() - 1)):
            halves = [p.reshape((2, p.shape[0] // 2) + p.shape[1:]) for p in parts]
            away = sum(take(p, 1 - bit(b)).astype(F32) for p in halves).astype(BF)
            parts = [take(p, bit(b)) for p in halves] + [hop(away, 1 << b)]
        return sum(p.astype(F32) for p in parts)[0]

    tok = tokens.T
    cot = cotangent.T
    far = lax.ppermute(tok.astype(BF), "mp", [(0, 1), (1, 0)])
    w2 = jnp.transpose(ff_in_weight, (1, 0, 2))
    wq = jnp.transpose(qkv_weight, (1, 2, 0)).reshape(3 * cols, d)
    again, fgain = attn_gain.reshape(1, d), ff_gain.reshape(1, d)

    e, inv, qkv, ctx, nrm, xt, mid, ct, wall = front(
        rel_table, doc_lengths, pad_mask, again, fgain, wq, out_weight.T, tok, far, cot, heads, dk
    )
    early, din, near_out, far_out, back, half_way, hand, wfar = ff_all(
        xt, ct, w2, ff_out_weight, mid, wq, extra
    )
    input_grad, result, grad_qkv, grad_out, small, ffo, ffi = tail(
        qkv, e, inv, wall, ctx, again, fgain, early, din, mid, cot, tok, nrm, wq, wfar, near_out, back, far_out,
        half_way, hand, buckets, heads, dk, extra, ff_out_weight.shape[1],
    )
    grad_qkv = jnp.transpose(grad_qkv, (1, 0, 2))
    if extra > 1:
        grad_qkv, grad_out, ffo, ffi = (finish(g) for g in (grad_qkv, grad_out, ffo, ffi))
    for b in range(extra.bit_length() - 1):
        small = small + hop(small, 1 << b)
    lines = -(-d // 128)
    return (
        result.T,
        input_grad.T,
        small[buckets : buckets + lines].reshape(-1)[:d],
        grad_qkv,
        small[:buckets, : heads * n_mp],
        grad_out,
        small[buckets + lines : buckets + 2 * lines].reshape(-1)[:d],
        ffi,
        ffo,
    )


def solution(mesh):
    return jax.shard_map(
        per_device,
        mesh=mesh,
        in_specs=(
            P(("dp", "mp"), None),
            P(("dp", "mp"), None),
            P("dp", None),
            P("dp", None),
            P(),
            P(None, None, "mp"),
            P(None, "mp"),
            P(None, "mp"),
            P(),
            P(None, None, "mp"),
            P(None, "mp"),
        ),
        out_specs=(
            P(("dp", "mp"), None),
            P(("dp", "mp"), None),
            P(),
            P("dp", None, "mp"),
            P(),
            P("dp", "mp"),
            P(),
            P("dp", None, "mp"),
            P("dp", "mp"),
        ),
        check_vma=False,
    )
```

time: 284 us -> 274 us (0.965)
  Pallas kernels: 228 us -> 222 us
  other arithmetic: 6.33 us -> 2.06 us
    pallas_call x1, Pallas kernels: 98.3 us -> 88.7 us  [tail(): pl.pallas_call(functools.partial(tail_kernel, heads, dk, buckets, blocks,...]
    unnamed x27, local copies, waits for them, and re-layouts: 18.1 us -> 22.5 us
    pallas_call x1, Pallas kernels: 88.8 us -> 92.4 us  [ff_all(): pl.pallas_call(functools.partial(ff_kernel, steps, done, extra), in_specs...]
where the time goes in v3:
time: 274 us
  Pallas kernels  222 us (81%)
  local copies, waits for them, and re-layouts  25.8 us (9%)
  waiting for transfers between devices  19.9 us (7%)
  starting transfers between devices  3 us (1%)
    pallas_call x1, Pallas kernels, ff_all(): pl.pallas_call(functools.partial(ff_kernel, steps, done, extra), in_specs...  92.4 us
    pallas_call x1, Pallas kernels, tail(): pl.pallas_call(functools.partial(tail_kernel, heads, dk, buckets, blocks,...  88.7 us
    pallas_call x1, Pallas kernels, front(): pl.pallas_call(functools.partial(front_kernel, heads, dk, buckets, blocks...  41.1 us
    unnamed x27, local copies, waits for them, and re-layouts  22.5 us
    ppermute x1, waiting for transfers between devices, per_device(): far = lax.ppermute(tok.astype(BF), 'mp', [(0, 1), (1, 0)])  19.9 us
  transfers between devices with their start and end apart: 1, of which 1 were waited for; matrix products, arithmetic and copies ran while one was open for 5% of the time, Pallas kernels for 0%

profile of v3, /device:TPU:0, one launch (start us, length us, event | category | flops | bytes accessed | tf_op | source)
XLA Modules:
  0.0 273.7 jit_solution(8271351976979319377)
XLA Ops:
  0.6 0.0 copy-start.5
  0.7 0.0 copy-start.6
  0.7 0.0 copy-start.7
  0.7 2.1 bitcast_convert_fusion
  2.7 3.0 %collective-permute-start = (bf16[1472,512]{1,0:T(8,128)(2,1)S(1)}, bf16[1472,512]{1,0:T(8,128)(2,1)S(1)}, u32[]{:S(2)}, u32[]{:S(2)}) collective-permute-start(bf16[1472,512]{1,0:T(8,128)(2,1)S(1)} %bitcast_convert_fusion), channel_id=1, source_target_pairs={{0,1},{1,0},{2,3},{3,2},{4,5},{5,4},{6,7},{7,6},{8,9},{9,8},{10,11... | collective-permute-start | bytes 4521992 | tf_op jit(solution)/shard_map/ppermute | solution.py:1146
  5.7 0.0 copy-done.5
  5.7 0.6 reshape.33.ag_ref
  6.3 0.0 copy-done.6
  6.3 0.6 reshape.34.fg_ref
  6.9 0.0 copy-done.7
  6.9 0.7 copy.22.rel_ref
  7.6 11.2 %copy.26 = bf16[1472,2,1792]{2,0,1:T(8,128)(2,1)} copy(bf16[1472,2,1792]{2,1,0:T(2,128)(2,1)} %param.22) | data formatting | bytes 21102592 | tf_op args[9]
  18.9 19.9 %collective-permute-done.far_hbm = bf16[1472,512]{1,0:T(8,128)(2,1)S(1)} collective-permute-done((bf16[1472,512]{1,0:T(8,128)(2,1)S(1)}, bf16[1472,512]{1,0:T(8,128)(2,1)S(1)}, u32[]{:S(2)}, u32[]{:S(2)}) %collective-permute-start) | collective-permute-done | bytes 1507360 | tf_op jit(solution)/shard_map/ppermute | solution.py:1146
  38.7 0.0 copy-start.8
  38.7 1.1 copy-done.8
  39.9 41.1 %shard_map.196 = (bf16[3,4,1024,256]{3,2,1,0:T(8,128)(2,1)}, f32[3,4,1,256]{3,2,1,0:T(1,128)}, bf16[576,1024]{1,0:T(8,128)(2,1)}, bf16[384,1024]{1,0:T(8,128)(2,...) custom-call(f32[32,3]{1,0:T(8,128)} %copy.22.rel_ref, ...), custom_call_target="tpu_custom_call" | custom-call | flops 6115295232 | bytes 28901376 | tf_op jit(solution)/shard_map/pallas_call | solution.py:285
  80.9 92.4 %shard_map.197 = (f32[3,96,512]{2,1,0:T(8,128)}, f32[1472,512]{1,0:T(8,128)}, f32[1472,512]{1,0:T(8,128)}, bf16[1472,384]{1,0:T(8,128)(2,1)}, bf16[1472,128]{1,0...) custom-call(bf16[1472,1024]{1,0:T(8,128)(2,1)} %get-tuple-element.38, ...), custom_call_target="tpu_custom_call" | custom-call | flops 48620371968 | bytes 39944192 | tf_op jit(solution)/shard_map/pallas_call | solution.py:599
  173.3 88.7 %shard_map.198 = (f32[1472,512]{1,0:T(8,128)}, f32[1472,512]{1,0:T(8,128)}, f32[3,92,192]{2,1,0:T(8,128)}, f32[92,192]{1,0:T(8,128)}, f32[56,128]{1,0:T(8,128)},...) custom-call(s32[1,1536]{1,0:T(1,128)} %constant.2.clone.bid_ref, bf16[576,1024]{1,0:T(8,128)(2,1)} %get-tuple-element.33.qkv_ref, ...), custom_call_target="tpu_custom_call" | custom-call | flops 13388218368 | bytes 28901376 | tf_op jit(solution)/shard_map/pallas_call | solution.py:1029
  262.1 0.7 slice.17
  262.8 1.4 slice_bitcast_fusion
  264.2 0.7 copy.24
  264.8 3.9 %copy.33 = f32[512,1472]{0,1:T(8,128)} copy(f32[512,1472]{0,1:T(8,128)} %bitcast.23) | data formatting | bytes 6029312
  268.8 0.0 copy-done
  268.8 1.6 copy.34
  270.4 0.0 copy-done.3
  270.4 0.7 copy.35
  271.1 0.0 copy-done.4
  271.1 0.6 copy.36
  271.8 0.0 copy-done.1
  271.8 1.1 copy.37
  272.8 0.0 copy-done.2
  272.8 0.8 copy.38
  (5 shorter events, 0.0 us)
Async XLA Ops:
  0.6 5.1 %copy-start.5 = (f32[1472]{0:T(1024)S(1)}, f32[1472]{0:T(1024)}, u32[]{:S(2)}) copy-start(f32[1472]{0:T(1024)} %param.17) | copy-start | bytes 17668
  0.7 5.7 %copy-start.6 = (f32[1472]{0:T(1024)S(1)}, f32[1472]{0:T(1024)}, u32[]{:S(2)}) copy-start(f32[1472]{0:T(1024)} %param.21) | copy-start | bytes 17668
  0.7 6.3 %copy-start.7 = (f32[32,3]{0,1:T(4,128)S(1)}, f32[32,3]{0,1:T(4,128)}, u32[]{:S(2)}) copy-start(f32[32,3]{0,1:T(4,128)} %param.19) | copy-start | bytes 1156
  2.7 36.0 %collective-permute-start = (bf16[1472,512]{1,0:T(8,128)(2,1)S(1)}, bf16[1472,512]{1,0:T(8,128)(2,1)S(1)}, u32[]{:S(2)}, u32[]{:S(2)}) collective-permute-start(bf16[1472,512]{1,0:T(8,128)(2,1)S(1)} %bitcast_convert_fusion), channel_id=1, source_target_pairs={{0,1},{1,0},{2,3},{3,2},{4,5},{5,4},{6,7},{7,6},{8,9},{9,8},{10,11... | collective-permute-start | bytes 4521992 | tf_op jit(solution)/shard_map/ppermute | solution.py:1146
  38.7 1.1 copy-start.8
  264.8 3.9 %copy-start = (f32[1472,512]{1,0:T(8,128)S(1)}, f32[1472,512]{1,0:T(8,128)}, u32[]{:S(2)}) copy-start(f32[1472,512]{1,0:T(8,128)} %get-tuple-element.51) | copy-start | bytes 9043972
  268.8 1.6 copy-start.3
  268.8 2.4 copy-start.4
  268.8 3.0 %copy-start.1 = (f32[92,2,1792]{2,1,0:T(2,128)S(1)}, f32[92,2,1792]{2,1,0:T(2,128)}, u32[]{:S(2)}) copy-start(f32[92,2,1792]{2,1,0:T(2,128)} %get-tuple-element.84) | copy-start | bytes 3956740
  270.4 2.4 copy-start.2

commit v4 on v3

--- a/solution.py
+++ b/solution.py
@@ -16,7 +16,6 @@
 BF = jnp.bfloat16
 F32 = jnp.float32
 FF_VMEM = 63 << 20
-FF_DONE = 2
 
 
 def bucket_of(offsets, buckets, reach):
@@ -62,6 +61,16 @@
 
 Y_FIRST = (0, 1, 2, 3)
 Z_FIRST = (0, 2, 3, 1)
+Z_BLOCK = 1
+LEVELS = (4, 3, 3, 2)
+
+
+def order_of(block):
+    return Z_FIRST if block == Z_BLOCK else Y_FIRST
+
+
+def levels_of(block):
+    return LEVELS[block] if block < len(LEVELS) else 1
 
 
 def block_position(k, order):
@@ -334,9 +343,9 @@
 
 
 def ff_kernel(
-    steps, done, extra,
+    steps, extra,
     xt_hbm, w_hbm, ct_hbm, wo_hbm, mid_hbm, wq_hbm,
-    grads_ref, din_hbm, near_hbm, far_hbm, back_hbm, half_hbm, hand_hbm, wfar_hbm,
+    grads_ref, din_hbm, near_hbm, far_hbm, back_hbm, quarter_hbm, half_hbm, hand_hbm, wfar_hbm,
     xt, ct, wg, wu, wo, hid, dg, du, din, stage, r1, r2, r3, r4, xs, xr, of,
     csem, wsem, s1, s2, s3, s4, t1, t2, t3, t4, xsem, osem, hsem,
 ):
@@ -379,40 +388,48 @@
     w_pass = remote(wfar_hbm.at[wq_part], wfar_hbm.at[wq_part], xsem.at[6], xsem.at[7], (sibling, mp))
     mid_copy = pltpu.make_async_copy(mid_hbm, din.at[:, far_part], osem.at[3])
 
-    def hop(level, n):
+    deep = len(LEVELS)
+
+    def hop(level, n, order):
         half = 8 >> level
-        away = pl.ds((1 - a[level]) * half, half)
+        c = order[level]
+        away = pl.ds((1 - a[c]) * half, half)
         src = stage.at[away] if level == 0 else bufs[level - 1].at[n, away]
-        return remote(src, bufs[level].at[n], sends[level].at[n], recvs[level].at[n], (peers[level], mp))
+        return remote(src, bufs[level].at[n], sends[level].at[n], recvs[level].at[n], (peers[c], mp))
 
     def hand_copy(n):
-        if isinstance(n, int) and n == done:
-            return pltpu.make_async_copy(r2.at[n], half_hbm, hsem.at[0])
-        return pltpu.make_async_copy(r1.at[n], hand_hbm.at[n - done - 1], hsem.at[n - done])
+        level = levels_of(n) if isinstance(n, int) else 1
+        dst = (hand_hbm.at[n - deep], half_hbm, quarter_hbm.at[n - 1])[level - 1]
+        return pltpu.make_async_copy(bufs[level - 1].at[n], dst, hsem.at[n])
 
     def absorb_first(n):
-        hop(0, n).wait()
+        hop(0, n, Y_FIRST).wait()
         r1[n] = stage[pl.ds(a[0] * 8, 8)] + r1[n]
         if isinstance(n, int):
             hand_copy(n).start()
             return
 
-        @pl.when(n <= done)
+        @pl.when(n == Z_BLOCK)
         def _():
-            hop(1, n).start()
-
-        @pl.when(n > done)
+            hop(1, n, Z_FIRST).start()
+
+        @pl.when((n < deep) & (n != Z_BLOCK))
+        def _():
+            hop(1, n, Y_FIRST).start()
+
+        @pl.when(n >= deep)
         def _():
             hand_copy(n).start()
 
     def absorb(level, n):
         half = 8 >> level
-        hop(level, n).wait()
-        kept = bufs[level - 1][n, pl.ds(a[level] * half, half)]
+        order = order_of(n)
+        hop(level, n, order).wait()
+        kept = bufs[level - 1][n, pl.ds(a[order[level]] * half, half)]
         if level < 3:
             bufs[level][n] = kept + bufs[level][n]
-            if n < done:
-                hop(level + 1, n).start()
+            if level + 1 < levels_of(n):
+                hop(level + 1, n, order).start()
             else:
                 hand_copy(n).start()
         else:
@@ -458,7 +475,7 @@
     per = 4 * shard
 
     def grads(j):
-        z = j // end
+        z = (j == Z_BLOCK) * 1
         for w in range(3):
             right = (hid, dg, du)[w][lanes(j), :]
             for q in range(4):
@@ -469,7 +486,7 @@
                     at = block_position(4 * q + k, Y_FIRST)
                     at = at + z * (block_position(4 * q + k, Z_FIRST) - at)
                     stage[at, w, 0:shard, :] = part[k * shard : (k + 1) * shard].astype(BF)
-        hop(0, j).start()
+        hop(0, j, Y_FIRST).start()
 
     def out_part(n):
         return dot(wo[...], hid[:, lanes(n)], ((1,), (0,)))
@@ -520,31 +537,25 @@
             x_copy.start()
             mid_copy.start()
 
-        @pl.when(u == count)
+        odd = u % 2 == 1
+        late = (u >= 2 * steps + 5) * 1
+        m = (u - 13) // 2 - 2 * ((u >= 2 * steps + 7) * 1)
+        n = (u - 11) // 2 - 2 * late
+
+        @pl.when(odd & ((u == 13) | (u == 15) | (u >= 2 * steps + 7)))
         def _():
-            pj, pc = place(count - 1)
-            backward(lanes(pj), lanes(pc))
-
-            def one(n, carry):
-                of[:, lanes(n)] = out_part(n + chunks).astype(BF)
-                return carry
-
-            lax.fori_loop(0, chunks, one, 0)
-
-        n = (u - far_end + 1) // 2
-
-        @pl.when((u >= far_end + 1) & (u % 2 == (far_end + 1) % 2))
+            absorb_first(m)
+
+        for at, events in (
+            (21, ((1, 0),)), (23, ((1, 1),)), (25, ((2, 0),)), (27, ((1, 2), (2, 1))),
+        ):
+            @pl.when(u == at)
+            def _():
+                for level, block in events:
+                    absorb(level, block)
+
+        @pl.when(odd & ((u == 11) | (u == 13) | (u >= 2 * steps + 5)))
         def _():
-            absorb_first(n - 1)
-
-        @pl.when((u >= far_end - 1) & (u % 2 == (far_end + 1) % 2))
-        def _():
-            for at, events in ((3, ((1, 0),)), (5, ((1, 1), (2, 0))), (6, ((2, 1), (3, 0)))):
-                @pl.when(n == at)
-                def _():
-                    for level, block in events:
-                        absorb(level, block)
-
             grads(n)
 
         @pl.when(u == far_end + 5)
@@ -554,31 +565,39 @@
 
         return carry
 
-    lax.fori_loop(0, count + 2, step, 0)
+    lax.fori_loop(0, count, step, 0)
+    pj, pc = place(count - 1)
+    backward(lanes(pj), lanes(pc))
+
+    def far_out(n, carry):
+        of[:, lanes(n)] = out_part(n + chunks).astype(BF)
+        return carry
+
+    lax.fori_loop(0, chunks, far_out, 0)
     x_copy.wait()
     back_copy.start()
     rest = far_hbm.shape[1]
     far_copy = pltpu.make_async_copy(of.at[:, pl.ds(128, rest)], far_hbm, osem.at[0])
     far_copy.start()
+    din[:, near_part] += xr[...].astype(F32)
+    din_copy = pltpu.make_async_copy(din.at[:, near_part], din_hbm, osem.at[2])
+    din_copy.start()
     mid_copy.wait()
 
-    def one(n, carry):
+    def near_out(n, carry):
         at = lanes(n + chunks)
         din[:, at] = din[:, at] + out_part(n)
         return carry
 
-    lax.fori_loop(0, chunks, one, 0)
+    lax.fori_loop(0, chunks, near_out, 0)
     near_copy = pltpu.make_async_copy(din.at[:, far_part], near_hbm, osem.at[1])
     near_copy.start()
     absorb_first(end)
-    absorb(1, done)
-    din[:, near_part] += xr[...].astype(F32)
-    din_copy = pltpu.make_async_copy(din.at[:, near_part], din_hbm, osem.at[2])
-    din_copy.start()
-    absorb(3, 1)
+    absorb(3, 0)
+    absorb(2, 2)
+    absorb(1, 3)
     w_pass.wait()
-
-    for n in range(done, steps):
+    for n in range(1, steps):
         hand_copy(n).wait()
     far_copy.wait()
     near_copy.wait()
@@ -591,23 +610,24 @@
     f = wo.shape[1]
     rows = total // 2
     steps = f // BLK
-    done = FF_DONE
+    deep = len(LEVELS)
     shard = d // 16
     spad = -(-shard // 16) * 16
     dma = pltpu.SemaphoreType.DMA
     any_spec = pl.BlockSpec(memory_space=pl.ANY)
     return pl.pallas_call(
-        functools.partial(ff_kernel, steps, done, extra),
+        functools.partial(ff_kernel, steps, extra),
         in_specs=[any_spec] * 6,
-        out_specs=[pl.BlockSpec(memory_space=pltpu.VMEM)] + [any_spec] * 7,
+        out_specs=[pl.BlockSpec(memory_space=pltpu.VMEM)] + [any_spec] * 8,
         out_shape=[
-            jax.ShapeDtypeStruct((3, spad, done * BLK), F32),
+            jax.ShapeDtypeStruct((3, spad, BLK), F32),
             jax.ShapeDtypeStruct((d, rows), F32),
             jax.ShapeDtypeStruct((d, rows), F32),
             jax.ShapeDtypeStruct((d, rows - 128), BF),
             jax.ShapeDtypeStruct((d, 128), BF),
+            jax.ShapeDtypeStruct((2, 2, 3, spad, BLK), BF),
             jax.ShapeDtypeStruct((4, 3, spad, BLK), BF),
-            jax.ShapeDtypeStruct((steps - done - 1, 8, 3, spad, BLK), BF),
+            jax.ShapeDtypeStruct((steps - deep, 8, 3, spad, BLK), BF),
             jax.ShapeDtypeStruct(wq.shape, BF),
         ],
         scratch_shapes=[
@@ -622,19 +642,19 @@
             pltpu.VMEM((d, total), F32),
             pltpu.VMEM((16, 3, spad, BLK), BF),
             pltpu.VMEM((steps, 8, 3, spad, BLK), BF),
-            pltpu.VMEM((done + 1, 4, 3, spad, BLK), BF),
-            pltpu.VMEM((done, 2, 3, spad, BLK), BF),
-            pltpu.VMEM((done, 1, 3, spad, BLK), BF),
+            pltpu.VMEM((4, 4, 3, spad, BLK), BF),
+            pltpu.VMEM((3, 2, 3, spad, BLK), BF),
+            pltpu.VMEM((1, 1, 3, spad, BLK), BF),
             pltpu.VMEM((d, rows), BF),
             pltpu.VMEM((d, rows), BF),
             pltpu.VMEM((d, rows), BF),
             dma((7,)),
             dma((3, steps)),
-            dma((steps,)), dma((done + 1,)), dma((done,)), dma((done,)),
-            dma((steps,)), dma((done + 1,)), dma((done,)), dma((done,)),
+            dma((steps,)), dma((4,)), dma((3,)), dma((1,)),
+            dma((steps,)), dma((4,)), dma((3,)), dma((1,)),
             dma((8,)),
             dma((4,)),
-            dma((steps - done,)),
+            dma((steps,)),
         ],
         compiler_params=pltpu.CompilerParams(
             vmem_limit_bytes=FF_VMEM, collective_id=0, has_side_effects=True
@@ -648,13 +668,14 @@
 
 
 def tail_kernel(
-    heads, dk, buckets, blocks, extra, first,
+    heads, dk, buckets, blocks, extra,
     bid_ref, qkv_ref, e_ref, inv_ref, wall_ref, ctx_ref, ag_ref, fg_ref, early_ref,
-    din_hbm, mid_hbm, cot_hbm, tok_hbm, nrm_hbm, wq_hbm, wfar_hbm, near_hbm, back_hbm, far_hbm, part_hbm, hand_hbm,
+    din_hbm, mid_hbm, cot_hbm, tok_hbm, nrm_hbm, wq_hbm, wfar_hbm, near_hbm, back_hbm, far_hbm,
+    quarter_hbm, half_hbm, hand_hbm,
     ig_hbm, res_hbm, gq_ref, go_ref, small_ref, ffo_ref, ffi_ref,
     f1, f2, f3, f4, nrm, wq, wn, wf, alow, dctx, dcs, osend, orecv, fsum, agc, fgc,
     dp_s, dkv, tally, dproj, dfar, grad, back0, back,
-    sa, sb_, a1, a2, a3, a4, b1, b2, b3, b4, hk, hm, h2, h3, h4, sv, rv,
+    sa, sb_, a1, a2, a3, a4, b1, b2, b3, b4, hk, hm, hq, h2, h3, h4, sv, rv,
     lsem, ksem, xs_sem, xr_sem, cs_sem, cr_sem, bs_sem, br_sem, hs_sem, hr_sem,
 ):
     qb = pl.program_id(0)
@@ -712,25 +733,32 @@
         for i in range(2):
             outs[i][...] = both[:, i * cols : (i + 1) * cols]
 
-    def order_of(block):
-        return Z_FIRST if block == 4 else Y_FIRST
+    deep = len(LEVELS)
+    handed = (1, 2, 3, 4, 5, 6)
 
     def keep_copy(block):
-        if block == 0:
-            return pltpu.make_async_copy(part_hbm.at[pl.ds(a[2] * 2, 2)], hm, ksem.at[0])
-        keep = pl.ds(a[order_of(block)[1]] * 4, 4)
-        return pltpu.make_async_copy(hand_hbm.at[block - 1, keep], hk.at[block - 1], ksem.at[block])
+        level = levels_of(block)
+        half = 8 >> level
+        keep = pl.ds(a[order_of(block)[level]] * half, half)
+        if level == 3:
+            src, dst = quarter_hbm.at[block - 1, keep], hq.at[block - 1]
+        elif level == 2:
+            src, dst = half_hbm.at[keep], hm
+        else:
+            src, dst = hand_hbm.at[block - deep, keep], hk.at[block - deep]
+        return pltpu.make_async_copy(src, dst, ksem.at[block])
 
     def hand_hop(level, block):
         half = 8 >> level
         c = order_of(block)[level]
         away = pl.ds((1 - a[c]) * half, half)
+        fresh = level == levels_of(block)
         if level == 1:
-            src, dst = hand_hbm.at[block - 1, away], h2.at[block - 1]
+            src, dst = hand_hbm.at[block - deep, away], h2.at[block - deep]
         elif level == 2:
-            src, dst = part_hbm.at[away] if block == 0 else h2.at[block - 1, away], h3.at[block]
+            src, dst = half_hbm.at[away] if fresh else h2.at[block - deep, away], h3.at[block - 3]
         else:
-            src, dst = h3.at[block, away], h4.at[block]
+            src, dst = quarter_hbm.at[block - 1, away] if fresh else h3.at[block - 3, away], h4.at[block - 1]
         return remote(src, dst, hs_sem.at[level, block], hr_sem.at[level, block], (peers[c], x))
 
     def put_grads(w, block, value):
@@ -744,19 +772,19 @@
         half = 8 >> level
         keep = pl.ds(a[order_of(block)[level]] * half, half)
         hand_hop(level, block).wait()
-        if level == (2 if block == 0 else 1):
+        if level == levels_of(block):
             keep_copy(block).wait()
-            kept = hm[...] if block == 0 else hk[block - 1]
+            kept = hk[block - deep] if level == 1 else (hm[...] if level == 2 else hq[block - 1])
         else:
-            kept = h2[block - 1, keep] if level == 2 else h3[block, keep]
+            kept = h2[block - deep, keep] if level == 2 else h3[block - 3, keep]
         if level == 1:
-            h2[block - 1] = kept + h2[block - 1]
+            h2[block - deep] = kept + h2[block - deep]
         elif level == 2:
-            h3[block] = kept + h3[block]
+            h3[block - 3] = kept + h3[block - 3]
         else:
-            both = kept.astype(F32) + h4[block].astype(F32)
+            both = kept.astype(F32) + h4[block - 1].astype(F32)
             for w in range(3):
-                put_grads(w, first + block, both[0, w, 0:shard])
+                put_grads(w, block, both[0, w, 0:shard])
         if level < 3:
             hand_hop(level + 1, block).start()
 
@@ -785,8 +813,8 @@
             local(i).start()
         meet([(p, x) for p in peers] + [other])
         back_copy(0).start()
-        for block in (0, 4, 1, 2, 3):
-            hand_hop(2 if block == 0 else 1, block).start()
+        for block in handed:
+            hand_hop(levels_of(block), block).start()
         agc[...] = column(ag_ref[...])
         fgc[...] = column(fg_ref[...])
         dkv[...] = jnp.zeros_like(dkv)
@@ -816,15 +844,14 @@
         dctx_copy.start()
         for i in (3, 4, 5, 7, 8):
             local(i).start()
-        for block in (0, 4, 1, 2, 3):
+        for block in handed:
             keep_copy(block).start()
         dctx[:, near_part] = dot(wall_ref[0:cols, :], alow[...], ((1,), (0,))).astype(BF)
         osend[...] = dot(alow[...], ctx_ref[cols : 2 * cols, near_part], ((1,), (1,))).astype(BF)
         o_copy.start()
         grad[:, 3 * cols : 4 * cols] = dot(alow[...], ctx_ref[0:cols, near_part], ((1,), (1,)))
         for w in range(3):
-            for block in range(first):
-                put_grads(w, block, early_ref[w, 0:shard, block * BLK : (block + 1) * BLK])
+            put_grads(w, 0, early_ref[w, 0:shard, :])
         dctx_copy.wait()
         back_copy(1).start()
 
@@ -833,25 +860,25 @@
         local(5).wait()
         wn[...] = wq[...].astype(F32).T.astype(BF)
         local(6).start()
-        hand_absorb(2, 0)
+        hand_absorb(3, 1)
+        hand_absorb(3, 2)
+        hand_absorb(2, 3)
 
     @pl.when(qb == 2)
     def _():
         local(6).wait()
         wf[...] = wq[...].astype(F32).T.astype(BF)
-        hand_absorb(1, 1)
-        hand_absorb(1, 4)
         local(7).wait()
         local(8).wait()
         back_copy(0).wait()
         f4[:, 0:128] += back0[...].astype(F32)
         f4[:, 128:BLK] += back[:, 0:128].astype(F32)
         local(10).start()
+        hand_absorb(1, 4)
 
     @pl.when(qb == 3)
     def _():
-        hand_absorb(3, 0)
-        hand_absorb(2, 1)
+        hand_absorb(3, 3)
 
     q_true = (qb + near_blocks * x) % blocks
 
@@ -906,7 +933,7 @@
                     k * shard : (k + 1) * shard, 2 * side * cols : 2 * (side + 1) * cols
                 ].astype(BF)
             hop(side, 0).start()
-        hand_absorb(1, 2)
+        hand_absorb(1, 5)
         hand_absorb(2, 4)
 
         def near_rows(r, carry):
@@ -916,9 +943,6 @@
         lax.fori_loop(0, near_blocks, near_rows, 0)
         absorb(0, 0)
         absorb(1, 0)
-        hand_absorb(1, 3)
-        hand_absorb(3, 1)
-        hand_absorb(2, 2)
         ids = bid_ref[...]
         hot = ids == lax.broadcasted_iota(jnp.int32, (buckets, SPAN), 0)
         out_lane = lax.broadcasted_iota(jnp.int32, (buckets, 128), 1)
@@ -952,14 +976,13 @@
             sv[0, buckets + i : buckets + i + 1, 0:n] = again[:, 128 * i : 128 * i + n]
             sv[0, buckets + lines + i : buckets + lines + i + 1, 0:n] = fgain[:, 128 * i : 128 * i + n]
         round_copy(0).start()
-        absorb(0, 1)
-        absorb(1, 1)
+        hand_absorb(3, 4)
+        hand_absorb(2, 5)
+        hand_absorb(1, 6)
         round_end(0)
-        hand_absorb(3, 4)
-        hand_absorb(2, 3)
         local(10).wait()
         local(9).start()
-        round_end(1)
+        absorb(1, 1)
         dproj_copy.wait()
 
         def last_norm(r, carry):
@@ -975,19 +998,22 @@
             return carry
 
         lax.fori_loop(0, near_blocks, last_norm, 0)
-        absorb(0, 2)
+        absorb(0, 1)
+        hand_absorb(3, 5)
+        round_end(1)
+        hand_absorb(2, 6)
         absorb(1, 2)
-        hand_absorb(3, 2)
         round_end(2)
         back_copy(1).wait()
         back_copy(2).wait()
         local(9).wait()
         f4[...] += back[:, 128 : 128 + BLK].astype(F32)
         local(11).start()
-        hand_absorb(3, 3)
+        absorb(0, 2)
+        hand_absorb(3, 6)
+        absorb(1, 3)
         round_end(3)
         absorb(0, 3)
-        absorb(1, 3)
         round_end(4)
         small_ref[...] = sv[5]
         local(11).wait()
@@ -996,7 +1022,7 @@
 
 
 def tail(qkv, e, inv, wall, ctx, again, fgain, early, din, mid, cot, tok, nrm, wq, wfar, near_out, back, far,
-         half_way, hand, buckets, heads, dk, extra, f):
+         quarter, half_way, hand, buckets, heads, dk, extra, f):
     d, rows = tok.shape
     seq = 2 * rows
     cols = heads * dk
@@ -1004,8 +1030,8 @@
     near = blocks // 2
     shard = d // 16
     spad = -(-shard // 16) * 16
-    later = hand.shape[0] + 1
-    first = early.shape[2] // BLK
+    deep = hand.shape[0]
+    later = deep + len(LEVELS)
     lines = -(-(buckets + 2 * -(-d // 128)) // 8) * 8
     bids = jnp.asarray(lane_buckets(buckets))
     one = pl.Buffered(1)
@@ -1027,7 +1053,7 @@
     ]
     a_chain, b_chain = chain(2 * cols), chain(2 * cols)
     return pl.pallas_call(
-        functools.partial(tail_kernel, heads, dk, buckets, blocks, extra, first),
+        functools.partial(tail_kernel, heads, dk, buckets, blocks, extra),
         grid=(blocks,),
         in_specs=[
             full(bids),
@@ -1040,7 +1066,7 @@
             full(fgain),
             full(early),
         ]
-        + [any_spec] * 12,
+        + [any_spec] * 13,
         out_specs=[any_spec, any_spec] + [full(v) for v in outs],
         out_shape=[jax.ShapeDtypeStruct((d, rows), F32), jax.ShapeDtypeStruct((d, rows), F32)] + outs,
         scratch_shapes=[
@@ -1074,11 +1100,12 @@
         + a_chain[1:]
         + b_chain[1:]
         + [
-            pltpu.VMEM((later - 1, 4, 3, spad, BLK), BF),
+            pltpu.VMEM((deep, 4, 3, spad, BLK), BF),
             pltpu.VMEM((2, 3, spad, BLK), BF),
-            pltpu.VMEM((later - 1, 4, 3, spad, BLK), BF),
-            pltpu.VMEM((later, 2, 3, spad, BLK), BF),
-            pltpu.VMEM((later, 1, 3, spad, BLK), BF),
+            pltpu.VMEM((2, 1, 3, spad, BLK), BF),
+            pltpu.VMEM((deep, 4, 3, spad, BLK), BF),
+            pltpu.VMEM((deep + 1, 2, 3, spad, BLK), BF),
+            pltpu.VMEM((later - 1, 1, 3, spad, BLK), BF),
             pltpu.VMEM((6, lines, 128), F32),
             pltpu.VMEM((5, lines, 128), F32),
             dma((12 + near,)),
@@ -1097,7 +1124,7 @@
             transcendentals=0,
         ),
     )(bids, qkv, e, inv, wall, ctx, again, fgain, early, din, mid, cot, tok, nrm, wq, wfar, near_out, back, far,
-      half_way, hand)
+      quarter, half_way, hand)
 
 
 def take(array, index):
@@ -1151,12 +1178,12 @@
     e, inv, qkv, ctx, nrm, xt, mid, ct, wall = front(
         rel_table, doc_lengths, pad_mask, again, fgain, wq, out_weight.T, tok, far, cot, heads, dk
     )
-    early, din, near_out, far_out, back, half_way, hand, wfar = ff_all(
+    early, din, near_out, far_out, back, quarter, half_way, hand, wfar = ff_all(
         xt, ct, w2, ff_out_weight, mid, wq, extra
     )
     input_grad, result, grad_qkv, grad_out, small, ffo, ffi = tail(
         qkv, e, inv, wall, ctx, again, fgain, early, din, mid, cot, tok, nrm, wq, wfar, near_out, back, far_out,
-        half_way, hand, buckets, heads, dk, extra, ff_out_weight.shape[1],
+        quarter, half_way, hand, buckets, heads, dk, extra, ff_out_weight.shape[1],
     )
     grad_qkv = jnp.transpose(grad_qkv, (1, 0, 2))
     if extra > 1:

time: 274 us -> 260 us (0.949)
  Pallas kernels: 222 us -> 209 us
    pallas_call x1, Pallas kernels: 88.7 us -> 81.4 us  [tail(): pl.pallas_call(functools.partial(tail_kernel, heads, dk, buckets, blocks,...]
    pallas_call x1, Pallas kernels: 92.4 us -> 86.2 us  [ff_all(): pl.pallas_call(functools.partial(ff_kernel, steps, extra), in_specs=[any_...]
where the time goes in v4:
time: 260 us
  Pallas kernels  209 us (80%)
  local copies, waits for them, and re-layouts  25.8 us (10%)
  waiting for transfers between devices  19.9 us (8%)
  starting transfers between devices  3 us (1%)
    pallas_call x1, Pallas kernels, ff_all(): pl.pallas_call(functools.partial(ff_kernel, steps, extra), in_specs=[any_...  86.2 us
    pallas_call x1, Pallas kernels, tail(): pl.pallas_call(functools.partial(tail_kernel, heads, dk, buckets, blocks,...  81.4 us
    pallas_call x1, Pallas kernels, front(): pl.pallas_call(functools.partial(front_kernel, heads, dk, buckets, blocks...  41 us
    unnamed x27, local copies, waits for them, and re-layouts  22.5 us
    ppermute x1, waiting for transfers between devices, per_device(): far = lax.ppermute(tok.astype(BF), 'mp', [(0, 1), (1, 0)])  19.9 us
  transfers between devices with their start and end apart: 1, of which 1 were waited for; matrix products, arithmetic and copies ran while one was open for 5% of the time, Pallas kernels for 0%

profile of v4, /device:TPU:0, one launch (start us, length us, event | category | flops | bytes accessed | tf_op | source)
XLA Modules:
  0.0 260.1 jit_solution(1110533743783211892)
XLA Ops:
  0.6 0.0 copy-start.5
  0.7 0.0 copy-start.6
  0.7 0.0 copy-start.7
  0.7 2.1 bitcast_convert_fusion
  2.7 3.0 %collective-permute-start = (bf16[1472,512]{1,0:T(8,128)(2,1)S(1)}, bf16[1472,512]{1,0:T(8,128)(2,1)S(1)}, u32[]{:S(2)}, u32[]{:S(2)}) collective-permute-start(bf16[1472,512]{1,0:T(8,128)(2,1)S(1)} %bitcast_convert_fusion), channel_id=1, source_target_pairs={{0,1},{1,0},{2,3},{3,2},{4,5},{5,4},{6,7},{7,6},{8,9},{9,8},{10,11... | collective-permute-start | bytes 4521992 | tf_op jit(solution)/shard_map/ppermute | solution.py:1173
  5.7 0.0 copy-done.5
  5.7 0.6 reshape.33.ag_ref
  6.3 0.0 copy-done.6
  6.3 0.6 reshape.34.fg_ref
  6.9 0.0 copy-done.7
  6.9 0.7 copy.22.rel_ref
  7.6 11.2 %copy.26 = bf16[1472,2,1792]{2,0,1:T(8,128)(2,1)} copy(bf16[1472,2,1792]{2,1,0:T(2,128)(2,1)} %param.22) | data formatting | bytes 21102592 | tf_op args[9]
  18.9 19.9 %collective-permute-done.far_hbm = bf16[1472,512]{1,0:T(8,128)(2,1)S(1)} collective-permute-done((bf16[1472,512]{1,0:T(8,128)(2,1)S(1)}, bf16[1472,512]{1,0:T(8,128)(2,1)S(1)}, u32[]{:S(2)}, u32[]{:S(2)}) %collective-permute-start) | collective-permute-done | bytes 1507360 | tf_op jit(solution)/shard_map/ppermute | solution.py:1173
  38.7 0.0 copy-start.8
  38.7 1.1 copy-done.8
  39.9 41.0 %shard_map.196 = (bf16[3,4,1024,256]{3,2,1,0:T(8,128)(2,1)}, f32[3,4,1,256]{3,2,1,0:T(1,128)}, bf16[576,1024]{1,0:T(8,128)(2,1)}, bf16[384,1024]{1,0:T(8,128)(2,...) custom-call(f32[32,3]{1,0:T(8,128)} %copy.22.rel_ref, ...), custom_call_target="tpu_custom_call" | custom-call | flops 6115295232 | bytes 28901376 | tf_op jit(solution)/shard_map/pallas_call | solution.py:294
  80.9 86.2 %shard_map.197 = (f32[3,96,256]{2,1,0:T(8,128)}, f32[1472,512]{1,0:T(8,128)}, f32[1472,512]{1,0:T(8,128)}, bf16[1472,384]{1,0:T(8,128)(2,1)}, bf16[1472,128]{1,0...) custom-call(bf16[1472,1024]{1,0:T(8,128)(2,1)} %get-tuple-element.39, ...), custom_call_target="tpu_custom_call" | custom-call | flops 48620371968 | bytes 39944192 | tf_op jit(solution)/shard_map/pallas_call | solution.py:618
  167.1 81.4 %shard_map.198 = (f32[1472,512]{1,0:T(8,128)}, f32[1472,512]{1,0:T(8,128)}, f32[3,92,192]{2,1,0:T(8,128)}, f32[92,192]{1,0:T(8,128)}, f32[56,128]{1,0:T(8,128)},...) custom-call(s32[1,1536]{1,0:T(1,128)} %constant.2.clone.bid_ref, bf16[576,1024]{1,0:T(8,128)(2,1)} %get-tuple-element.34.qkv_ref, ...), custom_call_target="tpu_custom_call" | custom-call | flops 13388218368 | bytes 28901376 | tf_op jit(solution)/shard_map/pallas_call | solution.py:1055
  248.5 0.7 slice.17
  249.2 1.4 slice_bitcast_fusion
  250.6 0.7 copy.24
  251.3 3.9 %copy.33 = f32[512,1472]{0,1:T(8,128)} copy(f32[512,1472]{0,1:T(8,128)} %bitcast.23) | data formatting | bytes 6029312
  255.2 0.0 copy-done
  255.2 1.6 copy.34
  256.8 0.0 copy-done.3
  256.9 0.7 copy.35
  257.6 0.0 copy-done.4
  257.6 0.6 copy.36
  258.2 0.0 copy-done.1
  258.2 1.1 copy.37
  259.3 0.0 copy-done.2
  259.3 0.8 copy.38
  (5 shorter events, 0.0 us)
Async XLA Ops:
  0.6 5.1 %copy-start.5 = (f32[1472]{0:T(1024)S(1)}, f32[1472]{0:T(1024)}, u32[]{:S(2)}) copy-start(f32[1472]{0:T(1024)} %param.17) | copy-start | bytes 17668
  0.7 5.7 %copy-start.6 = (f32[1472]{0:T(1024)S(1)}, f32[1472]{0:T(1024)}, u32[]{:S(2)}) copy-start(f32[1472]{0:T(1024)} %param.21) | copy-start | bytes 17668
  0.7 6.3 %copy-start.7 = (f32[32,3]{0,1:T(4,128)S(1)}, f32[32,3]{0,1:T(4,128)}, u32[]{:S(2)}) copy-start(f32[32,3]{0,1:T(4,128)} %param.19) | copy-start | bytes 1156
  2.7 36.0 %collective-permute-start = (bf16[1472,512]{1,0:T(8,128)(2,1)S(1)}, bf16[1472,512]{1,0:T(8,128)(2,1)S(1)}, u32[]{:S(2)}, u32[]{:S(2)}) collective-permute-start(bf16[1472,512]{1,0:T(8,128)(2,1)S(1)} %bitcast_convert_fusion), channel_id=1, source_target_pairs={{0,1},{1,0},{2,3},{3,2},{4,5},{5,4},{6,7},{7,6},{8,9},{9,8},{10,11... | collective-permute-start | bytes 4521992 | tf_op jit(solution)/shard_map/ppermute | solution.py:1173
  38.7 1.1 copy-start.8
  251.3 3.9 %copy-start = (f32[1472,512]{1,0:T(8,128)S(1)}, f32[1472,512]{1,0:T(8,128)}, u32[]{:S(2)}) copy-start(f32[1472,512]{1,0:T(8,128)} %get-tuple-element.53) | copy-start | bytes 9043972
  255.2 1.6 copy-start.3
  255.2 2.4 copy-start.4
  255.2 3.0 %copy-start.1 = (f32[92,2,1792]{2,1,0:T(2,128)S(1)}, f32[92,2,1792]{2,1,0:T(2,128)}, u32[]{:S(2)}) copy-start(f32[92,2,1792]{2,1,0:T(2,128)} %get-tuple-element.86) | copy-start | bytes 3956740
  256.9 2.4 copy-start.2

commit v5 on v4

--- a/solution.py
+++ b/solution.py
@@ -149,7 +149,13 @@
 
     w_copy = remote(wo_ref.at[part], wall.at[far_part], wsend.at[0], wrecv.at[0], other)
     w_pass = remote(wall.at[far_part], wall.at[far_part], wsend.at[1], wrecv.at[1], sibling)
-    c_copy = remote(cl.at[:, pl.ds(0, BLK)], ct_hbm.at[:, pl.ds(rows, BLK)], wsend.at[2], wrecv.at[2], other)
+    piece = d // 4
+
+    def c_copy(i):
+        rs = pl.ds(i * piece, piece)
+        return remote(
+            cl.at[rs, pl.ds(0, BLK)], ct_hbm.at[rs, pl.ds(rows, BLK)], wsend.at[2 + i], wrecv.at[2 + i], other
+        )
 
     def ctx_copy(b):
         there = (b + near_blocks) % blocks
@@ -167,7 +173,8 @@
         wall[0:cols, :] = wo_ref[...]
         local(2).wait()
         cl[...] = f3[...].astype(BF)
-        c_copy.start()
+        c_copy(0).start()
+        c_copy(1).start()
         out(3).start()
         agc[...] = column(ag_ref[...])
         fgc[...] = column(fg_ref[...])
@@ -250,8 +257,13 @@
     lax.fori_loop(0, heads, head, 0)
     ctx_copy(qb).start()
 
+    @pl.when(qb == 1)
+    def _():
+        c_copy(2).start()
+
     @pl.when(qb == blocks - 1)
     def _():
+        c_copy(3).start()
         w_pass.wait()
         wn[...] = wall[...].astype(F32).T.astype(BF)
         out(4).start()
@@ -269,7 +281,8 @@
             xt_out(b).start()
         out(0).start()
         out(2).start()
-        c_copy.wait()
+        for i in range(4):
+            c_copy(i).wait()
         for i in range(5):
             out(i).wait()
         for b in range(blocks):
@@ -329,7 +342,7 @@
             pltpu.VMEM((d, 2 * cols), BF),
             pltpu.VMEM((2 * cols, seq), BF),
             pltpu.VMEM((d, seq), BF),
-            dma((3,)), dma((5 + blocks,)), dma((3,)), dma((3,)), dma((blocks,)), dma((blocks,)),
+            dma((3,)), dma((5 + blocks,)), dma((6,)), dma((6,)), dma((blocks,)), dma((blocks,)),
         ],
         compiler_params=pltpu.CompilerParams(
             vmem_limit_bytes=FF_VMEM, collective_id=2, has_side_effects=True
@@ -345,7 +358,7 @@
 def ff_kernel(
     steps, extra,
     xt_hbm, w_hbm, ct_hbm, wo_hbm, mid_hbm, wq_hbm,
-    grads_ref, din_hbm, near_hbm, far_hbm, back_hbm, quarter_hbm, half_hbm, hand_hbm, wfar_hbm,
+    grads_ref, din_hbm, near_hbm, far_hbm, quarter_hbm, half_hbm, hand_hbm, wfar_hbm,
     xt, ct, wg, wu, wo, hid, dg, du, din, stage, r1, r2, r3, r4, xs, xr, of,
     csem, wsem, s1, s2, s3, s4, t1, t2, t3, t4, xsem, osem, hsem,
 ):
@@ -381,11 +394,10 @@
         ct_hbm.at[:, pl.ds(BLK, BLK)], ct.at[:, pl.ds(rows + BLK, BLK)], csem.at[5], csem.at[6], other
     )
     x_copy = remote(xs, xr, xsem.at[0], xsem.at[1], other)
-    back_copy = remote(of.at[:, pl.ds(0, 128)], back_hbm, xsem.at[2], xsem.at[3], other)
     wq_rows = wq_hbm.shape[0] // 2
     wq_part = pl.ds(core * wq_rows, wq_rows)
-    w_copy = remote(wq_hbm.at[wq_part], wfar_hbm.at[wq_part], xsem.at[4], xsem.at[5], other)
-    w_pass = remote(wfar_hbm.at[wq_part], wfar_hbm.at[wq_part], xsem.at[6], xsem.at[7], (sibling, mp))
+    w_copy = remote(wq_hbm.at[wq_part], wfar_hbm.at[wq_part], xsem.at[2], xsem.at[3], other)
+    w_pass = remote(wfar_hbm.at[wq_part], wfar_hbm.at[wq_part], xsem.at[4], xsem.at[5], (sibling, mp))
     mid_copy = pltpu.make_async_copy(mid_hbm, din.at[:, far_part], osem.at[3])
 
     deep = len(LEVELS)
@@ -574,11 +586,9 @@
         return carry
 
     lax.fori_loop(0, chunks, far_out, 0)
+    far_copy = pltpu.make_async_copy(of, far_hbm, osem.at[0])
+    far_copy.start()
     x_copy.wait()
-    back_copy.start()
-    rest = far_hbm.shape[1]
-    far_copy = pltpu.make_async_copy(of.at[:, pl.ds(128, rest)], far_hbm, osem.at[0])
-    far_copy.start()
     din[:, near_part] += xr[...].astype(F32)
     din_copy = pltpu.make_async_copy(din.at[:, near_part], din_hbm, osem.at[2])
     din_copy.start()
@@ -602,7 +612,6 @@
     far_copy.wait()
     near_copy.wait()
     din_copy.wait()
-    back_copy.wait()
 
 
 def ff_all(xt, ct, w2, wo, mid, wq, extra):
@@ -618,13 +627,12 @@
     return pl.pallas_call(
         functools.partial(ff_kernel, steps, extra),
         in_specs=[any_spec] * 6,
-        out_specs=[pl.BlockSpec(memory_space=pltpu.VMEM)] + [any_spec] * 8,
+        out_specs=[pl.BlockSpec(memory_space=pltpu.VMEM)] + [any_spec] * 7,
         out_shape=[
             jax.ShapeDtypeStruct((3, spad, BLK), F32),
             jax.ShapeDtypeStruct((d, rows), F32),
             jax.ShapeDtypeStruct((d, rows), F32),
-            jax.ShapeDtypeStruct((d, rows - 128), BF),
-            jax.ShapeDtypeStruct((d, 128), BF),
+            jax.ShapeDtypeStruct((d, rows), BF),
             jax.ShapeDtypeStruct((2, 2, 3, spad, BLK), BF),
             jax.ShapeDtypeStruct((4, 3, spad, BLK), BF),
             jax.ShapeDtypeStruct((steps - deep, 8, 3, spad, BLK), BF),
@@ -652,7 +660,7 @@
             dma((3, steps)),
             dma((steps,)), dma((4,)), dma((3,)), dma((1,)),
             dma((steps,)), dma((4,)), dma((3,)), dma((1,)),
-            dma((8,)),
+            dma((6,)),
             dma((4,)),
             dma((steps,)),
         ],
@@ -670,11 +678,11 @@
 def tail_kernel(
     heads, dk, buckets, blocks, extra,
     bid_ref, qkv_ref, e_ref, inv_ref, wall_ref, ctx_ref, ag_ref, fg_ref, early_ref,
-    din_hbm, mid_hbm, cot_hbm, tok_hbm, nrm_hbm, wq_hbm, wfar_hbm, near_hbm, back_hbm, far_hbm,
+    din_hbm, mid_hbm, cot_hbm, tok_hbm, nrm_hbm, wq_hbm, wfar_hbm, far_hbm,
     quarter_hbm, half_hbm, hand_hbm,
-    ig_hbm, res_hbm, gq_ref, go_ref, small_ref, ffo_ref, ffi_ref,
-    f1, f2, f3, f4, nrm, wq, wn, wf, alow, dctx, dcs, osend, orecv, fsum, agc, fgc,
-    dp_s, dkv, tally, dproj, dfar, grad, back0, back,
+    ig_hbm, back_hbm, gq_ref, go_ref, small_ref, ffo_ref, ffi_ref,
+    f1, f2, f3, nrm, wq, wn, wf, alow, dctx, dcs, osend, orecv, fsum, agc, fgc,
+    dp_s, dkv, tally, dproj, dfar, grad,
     sa, sb_, a1, a2, a3, a4, b1, b2, b3, b4, hk, hm, hq, h2, h3, h4, sv, rv,
     lsem, ksem, xs_sem, xr_sem, cs_sem, cr_sem, bs_sem, br_sem, hs_sem, hr_sem,
 ):
@@ -692,8 +700,6 @@
     orders = (Y_FIRST, Z_FIRST)
     copies = (
         (din_hbm, f1), (mid_hbm, f2), (cot_hbm, f3), (tok_hbm, f2), (nrm_hbm, nrm), (wq_hbm, wq), (wfar_hbm, wq),
-        (back_hbm, back0), (near_hbm.at[:, pl.ds(0, BLK)], f4), (near_hbm.at[:, pl.ds(BLK, BLK)], f4),
-        (f4, res_hbm.at[:, pl.ds(0, BLK)]), (f4, res_hbm.at[:, pl.ds(BLK, BLK)]),
     )
 
     def local(i):
@@ -708,7 +714,7 @@
 
     def back_copy(i):
         part = pl.ds(i * 128, 128)
-        return x_copy(3 + i, far_hbm.at[:, part], back.at[:, part])
+        return x_copy(3 + i, far_hbm.at[:, part], back_hbm.at[:, part])
 
     def hop(side, level):
         half = 8 >> level
@@ -842,7 +848,7 @@
         lax.fori_loop(0, near_blocks, norm_rows, 0)
         dcs[...] = dot(wall_ref[cols : 2 * cols, :], alow[...], ((1,), (0,))).astype(BF)
         dctx_copy.start()
-        for i in (3, 4, 5, 7, 8):
+        for i in (3, 4, 5):
             local(i).start()
         for block in handed:
             keep_copy(block).start()
@@ -860,25 +866,20 @@
         local(5).wait()
         wn[...] = wq[...].astype(F32).T.astype(BF)
         local(6).start()
+        hand_absorb(2, 3)
         hand_absorb(3, 1)
         hand_absorb(3, 2)
-        hand_absorb(2, 3)
+        hand_absorb(1, 4)
 
     @pl.when(qb == 2)
     def _():
         local(6).wait()
         wf[...] = wq[...].astype(F32).T.astype(BF)
-        local(7).wait()
-        local(8).wait()
-        back_copy(0).wait()
-        f4[:, 0:128] += back0[...].astype(F32)
-        f4[:, 128:BLK] += back[:, 0:128].astype(F32)
-        local(10).start()
-        hand_absorb(1, 4)
 
     @pl.when(qb == 3)
     def _():
         hand_absorb(3, 3)
+        hand_absorb(2, 4)
 
     q_true = (qb + near_blocks * x) % blocks
 
@@ -915,6 +916,8 @@
         dproj[cols : 3 * cols, :] = dkv[...].astype(BF)
         dproj_copy.start()
         back_copy(2).start()
+        back_copy(3).start()
+        hand_absorb(1, 5)
         local(3).wait()
         local(4).wait()
         per = 4 * shard
@@ -933,8 +936,6 @@
                     k * shard : (k + 1) * shard, 2 * side * cols : 2 * (side + 1) * cols
                 ].astype(BF)
             hop(side, 0).start()
-        hand_absorb(1, 5)
-        hand_absorb(2, 4)
 
         def near_rows(r, carry):
             f3[:, lanes(r)] = dot(wn[...], dproj[:, lanes(r)], ((1,), (0,)))
@@ -980,8 +981,6 @@
         hand_absorb(2, 5)
         hand_absorb(1, 6)
         round_end(0)
-        local(10).wait()
-        local(9).start()
         absorb(1, 1)
         dproj_copy.wait()
 
@@ -1004,11 +1003,6 @@
         hand_absorb(2, 6)
         absorb(1, 2)
         round_end(2)
-        back_copy(1).wait()
-        back_copy(2).wait()
-        local(9).wait()
-        f4[...] += back[:, 128 : 128 + BLK].astype(F32)
-        local(11).start()
         absorb(0, 2)
         hand_absorb(3, 6)
         absorb(1, 3)
@@ -1016,12 +1010,13 @@
         absorb(0, 3)
         round_end(4)
         small_ref[...] = sv[5]
-        local(11).wait()
+        for i in range(4):
+            back_copy(i).wait()
         for r in range(near_blocks):
             out_copy(r).wait()
 
 
-def tail(qkv, e, inv, wall, ctx, again, fgain, early, din, mid, cot, tok, nrm, wq, wfar, near_out, back, far,
+def tail(qkv, e, inv, wall, ctx, again, fgain, early, din, mid, cot, tok, nrm, wq, wfar, far,
          quarter, half_way, hand, buckets, heads, dk, extra, f):
     d, rows = tok.shape
     seq = 2 * rows
@@ -1066,14 +1061,13 @@
             full(fgain),
             full(early),
         ]
-        + [any_spec] * 13,
+        + [any_spec] * 11,
         out_specs=[any_spec, any_spec] + [full(v) for v in outs],
-        out_shape=[jax.ShapeDtypeStruct((d, rows), F32), jax.ShapeDtypeStruct((d, rows), F32)] + outs,
+        out_shape=[jax.ShapeDtypeStruct((d, rows), F32), jax.ShapeDtypeStruct((d, rows), BF)] + outs,
         scratch_shapes=[
             pltpu.VMEM((d, rows), F32),
             pltpu.VMEM((d, rows), F32),
             pltpu.VMEM((d, rows), F32),
-            pltpu.VMEM((d, BLK), F32),
             pltpu.VMEM((d, seq), BF),
             pltpu.VMEM((3 * cols, d), BF),
             pltpu.VMEM((d, 3 * cols), BF),
@@ -1092,8 +1086,6 @@
             pltpu.VMEM((3 * cols, seq), BF),
             pltpu.VMEM((3 * cols, rows), BF),
             pltpu.VMEM((d, 4 * cols), F32),
-            pltpu.VMEM((d, 128), BF),
-            pltpu.VMEM((d, rows - 128), BF),
             a_chain[0],
             b_chain[0],
         ]
@@ -1108,9 +1100,9 @@
             pltpu.VMEM((later - 1, 1, 3, spad, BLK), BF),
             pltpu.VMEM((6, lines, 128), F32),
             pltpu.VMEM((5, lines, 128), F32),
-            dma((12 + near,)),
+            dma((7 + near,)),
             dma((later,)),
-            dma((6,)), dma((6,)),
+            dma((7,)), dma((7,)),
             dma((2, 4)), dma((2, 4)),
             dma((5,)), dma((5,)),
             dma((4, later)), dma((4, later)),
@@ -1123,8 +1115,43 @@
             bytes_accessed=2 * heads * seq * seq + 30 * rows * d,
             transcendentals=0,
         ),
-    )(bids, qkv, e, inv, wall, ctx, again, fgain, early, din, mid, cot, tok, nrm, wq, wfar, near_out, back, far,
+    )(bids, qkv, e, inv, wall, ctx, again, fgain, early, din, mid, cot, tok, nrm, wq, wfar, far,
       quarter, half_way, hand)
+
+
+def outputs_kernel(near_ref, back_ref, ig_ref, *refs):
+    n = (len(refs) - 3) // 2
+    sources, res_ref, ig_out, targets, sem = refs[:n], refs[n], refs[n + 1], refs[n + 2 : 2 * n + 2], refs[-1]
+
+    def copy(i):
+        return pltpu.make_async_copy(sources[i], targets[i], sem.at[i])
+
+    @pl.when(pl.program_id(0) == 0)
+    def _():
+        for i in range(n):
+            copy(i).start()
+
+    res_ref[...] = near_ref[...] + back_ref[...].astype(F32)
+    ig_out[...] = ig_ref[...]
+
+    @pl.when(pl.program_id(0) == pl.num_programs(0) - 1)
+    def _():
+        for i in range(n):
+            copy(i).wait()
+
+
+def outputs(near, back, ig, *grads):
+    d, rows = near.shape
+    block = pl.BlockSpec((d // 4, rows), lambda i: (i, 0))
+    any_spec = pl.BlockSpec(memory_space=pl.ANY)
+    return pl.pallas_call(
+        outputs_kernel,
+        grid=(4,),
+        in_specs=[block] * 3 + [any_spec] * len(grads),
+        out_specs=[block] * 2 + [any_spec] * len(grads),
+        out_shape=[jax.ShapeDtypeStruct(v.shape, F32) for v in (near, ig) + grads],
+        scratch_shapes=[pltpu.SemaphoreType.DMA((len(grads),))],
+    )(near, back, ig, *grads)
 
 
 def take(array, index):
@@ -1178,12 +1205,15 @@
     e, inv, qkv, ctx, nrm, xt, mid, ct, wall = front(
         rel_table, doc_lengths, pad_mask, again, fgain, wq, out_weight.T, tok, far, cot, heads, dk
     )
-    early, din, near_out, far_out, back, quarter, half_way, hand, wfar = ff_all(
+    early, din, near_out, far_out, quarter, half_way, hand, wfar = ff_all(
         xt, ct, w2, ff_out_weight, mid, wq, extra
     )
-    input_grad, result, grad_qkv, grad_out, small, ffo, ffi = tail(
-        qkv, e, inv, wall, ctx, again, fgain, early, din, mid, cot, tok, nrm, wq, wfar, near_out, back, far_out,
+    input_grad, back, grad_qkv, grad_out, small, ffo, ffi = tail(
+        qkv, e, inv, wall, ctx, again, fgain, early, din, mid, cot, tok, nrm, wq, wfar, far_out,
         quarter, half_way, hand, buckets, heads, dk, extra, ff_out_weight.shape[1],
+    )
+    result, input_grad, grad_qkv, grad_out, ffo, ffi = outputs(
+        near_out, back, input_grad, grad_qkv, grad_out, ffo, ffi
     )
     grad_qkv = jnp.transpose(grad_qkv, (1, 0, 2))
     if extra > 1:

time: 260 us -> 319 us (1.23)
  Pallas kernels: 209 us -> 276 us
  local copies, waits for them, and re-layouts: 25.8 us -> 17 us
    pallas_call x0 -> x1, Pallas kernels: none -> 76.4 us  [outputs(): pl.pallas_call(outputs_kernel, grid=(4,), in_specs=[block] * 3 + [any_spe...]
    unnamed x27 -> x11, local copies, waits for them, and re-layouts: 22.5 us -> 13.7 us
    pallas_call x1, Pallas kernels: 41 us -> 37.7 us  [front(): pl.pallas_call(functools.partial(front_kernel, heads, dk, buckets, blocks...]
    pallas_call x1, Pallas kernels: 86.2 us -> 82.9 us  [ff_all(): pl.pallas_call(functools.partial(ff_kernel, steps, extra), in_specs=[any_...]
  transfers between devices with their start and end apart: 1 -> 1, of which waited for: 1 -> 1; matrix products, arithmetic and copies ran while one was open for 5% -> 4% of each run, Pallas kernels for 0% -> 0%
where the time goes in v5:
time: 319 us
  Pallas kernels  276 us (87%)
  waiting for transfers between devices  19.9 us (6%)
  local copies, waits for them, and re-layouts  17 us (5%)
    pallas_call x1, Pallas kernels, ff_all(): pl.pallas_call(functools.partial(ff_kernel, steps, extra), in_specs=[any_...  82.9 us
    pallas_call x1, Pallas kernels, tail(): pl.pallas_call(functools.partial(tail_kernel, heads, dk, buckets, blocks,...  78.7 us
    pallas_call x1, Pallas kernels, outputs(): pl.pallas_call(outputs_kernel, grid=(4,), in_specs=[block] * 3 + [any_spe...  76.4 us
    pallas_call x1, Pallas kernels, front(): pl.pallas_call(functools.partial(front_kernel, heads, dk, buckets, blocks...  37.7 us
    ppermute x1, waiting for transfers between devices, per_device(): far = lax.ppermute(tok.astype(BF), 'mp', [(0, 1), (1, 0)])  19.9 us
    unnamed x11, local copies, waits for them, and re-layouts  13.7 us
  transfers between devices with their start and end apart: 1, of which 1 were waited for; matrix products, arithmetic and copies ran while one was open for 4% of the time, Pallas kernels for 0%

profile of v5, /device:TPU:0, one launch (start us, length us, event | category | flops | bytes accessed | tf_op | source)
XLA Modules:
  0.0 318.5 jit_solution(9247889526576221884)
XLA Ops:
  0.6 0.0 copy-start
  0.7 0.0 copy-start.1
  0.7 0.0 copy-start.2
  0.7 2.1 bitcast_convert_fusion
  2.7 3.0 collective-permute-start
  5.7 0.0 copy-done
  5.7 0.6 reshape.33.ag_ref
  6.3 0.0 copy-done.1
  6.3 0.6 reshape.34.fg_ref
  6.9 0.0 copy-done.2
  6.9 0.7 copy.22.rel_ref
  7.6 11.2 %copy.26 = bf16[1472,2,1792]{2,0,1:T(8,128)(2,1)} copy(bf16[1472,2,1792]{2,1,0:T(2,128)(2,1)} %param.22) | data formatting | bytes 21102592 | tf_op args[9]
  18.9 19.9 %collective-permute-done.far_hbm = bf16[1472,512]{1,0:T(8,128)(2,1)S(1)} collective-permute-done((bf16[1472,512]{1,0:T(8,128)(2,1)S(1)}, bf16[1472,512]{1,0:T(8,128)(2,1)S(1)}, u32[]{:S(2)}, u32[]{:S(2)}) %collective-permute-start) | collective-permute-done | bytes 1507360 | tf_op jit(solution)/shard_map/ppermute | solution.py:1200
  38.7 0.0 copy-start.3
  38.7 1.1 copy-done.3
  39.9 37.7 %shard_map.196 = (bf16[3,4,1024,256]{3,2,1,0:T(8,128)(2,1)}, f32[3,4,1,256]{3,2,1,0:T(1,128)}, bf16[576,1024]{1,0:T(8,128)(2,1)}, bf16[384,1024]{1,0:T(8,128)(2,...) custom-call(f32[32,3]{1,0:T(8,128)} %copy.22.rel_ref, ...), custom_call_target="tpu_custom_call" | custom-call | flops 6115295232 | bytes 28901376 | tf_op jit(solution)/shard_map/pallas_call | solution.py:307
  77.5 82.9 %shard_map.197 = (f32[3,96,256]{2,1,0:T(8,128)}, f32[1472,512]{1,0:T(8,128)}, f32[1472,512]{1,0:T(8,128)}, bf16[1472,512]{1,0:T(8,128)(2,1)}, bf16[2,2,3,96,256]...) custom-call(bf16[1472,1024]{1,0:T(8,128)(2,1)} %get-tuple-element.39, ...), custom_call_target="tpu_custom_call" | custom-call | flops 48620371968 | bytes 39944192 | tf_op jit(solution)/shard_map/pallas_call | solution.py:627
  160.4 78.7 %shard_map.198 = (f32[1472,512]{1,0:T(8,128)}, bf16[1472,512]{1,0:T(8,128)(2,1)}, f32[3,92,192]{2,1,0:T(8,128)}, f32[92,192]{1,0:T(8,128)}, f32[56,128]{1,0:T(8,...) custom-call(s32[1,1536]{1,0:T(1,128)} %constant.2.clone.bid_ref, bf16[576,1024]{1,0:T(8,128)(2,1)} %get-tuple-element.43.qkv_ref, ...), custom_call_target="tpu_custom_call" | custom-call | flops 13388218368 | bytes 28901376 | tf_op jit(solution)/shard_map/pallas_call | solution.py:1050
  239.1 0.7 slice.17
  239.9 1.4 slice_bitcast_fusion
  241.2 0.7 copy.24
  241.9 76.4 %shard_map.199 = (f32[1472,512]{1,0:T(8,128)}, f32[1472,512]{1,0:T(8,128)}, f32[3,92,192]{2,1,0:T(8,128)}, f32[92,192]{1,0:T(8,128)}, f32[92,1792]{1,0:T(8,128)}, /*index=5*/f32[92,2,1792]{2,1,0:T(2,128)}) custom-call(f32[1472,512]{1,0:T(8,128)} %get-tuple-element.42.near_ref, bf16[1472,512]{1,0:T(8,128)(2,1)} %get-tuple-element.56.back_ref, ...), custom_call_target="tpu_custom_call" | custom-call | tf_op jit(solution)/shard_map/pallas_call | solution.py:1147
Async XLA Ops:
  0.6 5.1 %copy-start = (f32[1472]{0:T(1024)S(1)}, f32[1472]{0:T(1024)}, u32[]{:S(2)}) copy-start(f32[1472]{0:T(1024)} %param.17) | copy-start | bytes 17668
  0.7 5.7 %copy-start.1 = (f32[1472]{0:T(1024)S(1)}, f32[1472]{0:T(1024)}, u32[]{:S(2)}) copy-start(f32[1472]{0:T(1024)} %param.21) | copy-start | bytes 17668
  0.7 6.3 %copy-start.2 = (f32[32,3]{0,1:T(4,128)S(1)}, f32[32,3]{0,1:T(4,128)}, u32[]{:S(2)}) copy-start(f32[32,3]{0,1:T(4,128)} %param.19) | copy-start | bytes 1156
  2.7 36.0 %collective-permute-start = (bf16[1472,512]{1,0:T(8,128)(2,1)S(1)}, bf16[1472,512]{1,0:T(8,128)(2,1)S(1)}, u32[]{:S(2)}, u32[]{:S(2)}) collective-permute-start(bf16[1472,512]{1,0:T(8,128)(2,1)S(1)} %bitcast_convert_fusion), channel_id=1, source_target_pairs={{0,1},{1,0},{2,3},{3,2},{4,5},{5,4},{6,7},{7,6},{8,9},{9,8},{10,11... | collective-permute-start | bytes 4521992 | tf_op jit(solution)/shard_map/ppermute | solution.py:1200
  38.7 1.1 copy-start.3

commit v6 on v5

--- a/solution.py
+++ b/solution.py
@@ -1119,39 +1119,34 @@
       quarter, half_way, hand)
 
 
-def outputs_kernel(near_ref, back_ref, ig_ref, *refs):
+def outputs_kernel(near_ref, back_ref, ig_ref, ffi_ref, *refs):
     n = (len(refs) - 3) // 2
-    sources, res_ref, ig_out, targets, sem = refs[:n], refs[n], refs[n + 1], refs[n + 2 : 2 * n + 2], refs[-1]
-
-    def copy(i):
-        return pltpu.make_async_copy(sources[i], targets[i], sem.at[i])
+    sources, res_ref, ig_out, ffi_out, targets = refs[:n], refs[n], refs[n + 1], refs[n + 2], refs[n + 3 :]
+    res_ref[...] = near_ref[...] + back_ref[...].astype(F32)
+    ig_out[...] = ig_ref[...]
+    ffi_out[...] = ffi_ref[...]
 
     @pl.when(pl.program_id(0) == 0)
     def _():
         for i in range(n):
-            copy(i).start()
-
-    res_ref[...] = near_ref[...] + back_ref[...].astype(F32)
-    ig_out[...] = ig_ref[...]
-
-    @pl.when(pl.program_id(0) == pl.num_programs(0) - 1)
-    def _():
-        for i in range(n):
-            copy(i).wait()
-
-
-def outputs(near, back, ig, *grads):
+            targets[i][...] = sources[i][...]
+
+
+def outputs(near, back, ig, ffi, *grads):
     d, rows = near.shape
     block = pl.BlockSpec((d // 4, rows), lambda i: (i, 0))
-    any_spec = pl.BlockSpec(memory_space=pl.ANY)
+    shard, two, f = ffi.shape
+    part = pl.BlockSpec((shard // 4, two, f), lambda i: (i, 0, 0))
+    one = pl.Buffered(1)
+    whole = [pl.BlockSpec(v.shape, lambda i, n=v.ndim: (0,) * n, pipeline_mode=one) for v in grads]
     return pl.pallas_call(
         outputs_kernel,
         grid=(4,),
-        in_specs=[block] * 3 + [any_spec] * len(grads),
-        out_specs=[block] * 2 + [any_spec] * len(grads),
-        out_shape=[jax.ShapeDtypeStruct(v.shape, F32) for v in (near, ig) + grads],
-        scratch_shapes=[pltpu.SemaphoreType.DMA((len(grads),))],
-    )(near, back, ig, *grads)
+        in_specs=[block] * 3 + [part] + whole,
+        out_specs=[block] * 2 + [part] + whole,
+        out_shape=[jax.ShapeDtypeStruct(v.shape, F32) for v in (near, ig, ffi) + grads],
+        compiler_params=pltpu.CompilerParams(vmem_limit_bytes=40 << 20),
+    )(near, back, ig, ffi, *grads)
 
 
 def take(array, index):
@@ -1212,8 +1207,8 @@
         qkv, e, inv, wall, ctx, again, fgain, early, din, mid, cot, tok, nrm, wq, wfar, far_out,
         quarter, half_way, hand, buckets, heads, dk, extra, ff_out_weight.shape[1],
     )
-    result, input_grad, grad_qkv, grad_out, ffo, ffi = outputs(
-        near_out, back, input_grad, grad_qkv, grad_out, ffo, ffi
+    result, input_grad, ffi, grad_qkv, grad_out, ffo = outputs(
+        near_out, back, input_grad, ffi, grad_qkv, grad_out, ffo
     )
     grad_qkv = jnp.transpose(grad_qkv, (1, 0, 2))
     if extra > 1:

time: 319 us -> 256 us (0.80)
  Pallas kernels: 276 us -> 203 us
  local copies, waits for them, and re-layouts: 17 us -> 26.4 us
    pallas_call x1, Pallas kernels: 76.4 us -> 3.69 us  [outputs(): pl.pallas_call(outputs_kernel, grid=(4,), in_specs=[block] * 3 + [part] +...]
    unnamed x11 -> x25, local copies, waits for them, and re-layouts: 13.7 us -> 23.1 us
  transfers between devices with their start and end apart: 1 -> 1, of which waited for: 1 -> 1; matrix products, arithmetic and copies ran while one was open for 4% -> 5% of each run, Pallas kernels for 0% -> 0%
where the time goes in v6:
time: 256 us; the launch traced here: 255 us
  Pallas kernels  203 us (79%)
  local copies, waits for them, and re-layouts  26.4 us (10%)
  waiting for transfers between devices  19.9 us (8%)
  starting transfers between devices  3 us (1%)
    pallas_call x1, Pallas kernels, ff_all(): pl.pallas_call(functools.partial(ff_kernel, steps, extra), in_specs=[any_...  82.9 us
    pallas_call x1, Pallas kernels, tail(): pl.pallas_call(functools.partial(tail_kernel, heads, dk, buckets, blocks,...  78.4 us
    pallas_call x1, Pallas kernels, front(): pl.pallas_call(functools.partial(front_kernel, heads, dk, buckets, blocks...  37.7 us
    unnamed x25, local copies, waits for them, and re-layouts  23.1 us
    ppermute x1, waiting for transfers between devices, per_device(): far = lax.ppermute(tok.astype(BF), 'mp', [(0, 1), (1, 0)])  19.9 us
  transfers between devices with their start and end apart: 1, of which 1 were waited for; matrix products, arithmetic and copies ran while one was open for 5% of the time, Pallas kernels for 0%

profile of v6, /device:TPU:0, one launch (start us, length us, event | category | flops | bytes accessed | tf_op | source)
XLA Modules:
  0.0 254.8 jit_solution(6075171840721287110)
XLA Ops:
  0.6 0.0 copy-start.7
  0.7 0.0 copy-start.8
  0.7 0.0 copy-start.9
  0.7 2.1 bitcast_convert_fusion
  2.7 3.0 %collective-permute-start = (bf16[1472,512]{1,0:T(8,128)(2,1)S(1)}, bf16[1472,512]{1,0:T(8,128)(2,1)S(1)}, u32[]{:S(2)}, u32[]{:S(2)}) collective-permute-start(bf16[1472,512]{1,0:T(8,128)(2,1)S(1)} %bitcast_convert_fusion), channel_id=1, source_target_pairs={{0,1},{1,0},{2,3},{3,2},{4,5},{5,4},{6,7},{7,6},{8,9},{9,8},{10,11... | collective-permute-start | bytes 4521992 | tf_op jit(solution)/shard_map/ppermute | solution.py:1195
  5.7 0.0 copy-done.7
  5.7 0.6 reshape.33.ag_ref
  6.3 0.0 copy-done.8
  6.3 0.6 reshape.34.fg_ref
  6.9 0.0 copy-done.9
  6.9 0.7 copy.22.rel_ref
  7.6 11.2 %copy.26 = bf16[1472,2,1792]{2,0,1:T(8,128)(2,1)} copy(bf16[1472,2,1792]{2,1,0:T(2,128)(2,1)} %param.22) | data formatting | bytes 21102592 | tf_op args[9]
  18.9 19.9 %collective-permute-done.far_hbm = bf16[1472,512]{1,0:T(8,128)(2,1)S(1)} collective-permute-done((bf16[1472,512]{1,0:T(8,128)(2,1)S(1)}, bf16[1472,512]{1,0:T(8,128)(2,1)S(1)}, u32[]{:S(2)}, u32[]{:S(2)}) %collective-permute-start) | collective-permute-done | bytes 1507360 | tf_op jit(solution)/shard_map/ppermute | solution.py:1195
  38.7 0.0 copy-start.10
  38.7 1.1 copy-done.10
  39.9 37.7 %shard_map.196 = (bf16[3,4,1024,256]{3,2,1,0:T(8,128)(2,1)}, f32[3,4,1,256]{3,2,1,0:T(1,128)}, bf16[576,1024]{1,0:T(8,128)(2,1)}, bf16[384,1024]{1,0:T(8,128)(2,...) custom-call(f32[32,3]{1,0:T(8,128)} %copy.22.rel_ref, ...), custom_call_target="tpu_custom_call" | custom-call | flops 6115295232 | bytes 28901376 | tf_op jit(solution)/shard_map/pallas_call | solution.py:307
  77.5 82.9 %shard_map.197 = (f32[3,96,256]{2,1,0:T(8,128)}, f32[1472,512]{1,0:T(8,128)}, f32[1472,512]{1,0:T(8,128)}, bf16[1472,512]{1,0:T(8,128)(2,1)}, bf16[2,2,3,96,256]...) custom-call(bf16[1472,1024]{1,0:T(8,128)(2,1)} %get-tuple-element.39, ...), custom_call_target="tpu_custom_call" | custom-call | flops 48620371968 | bytes 39944192 | tf_op jit(solution)/shard_map/pallas_call | solution.py:627
  160.5 78.4 %shard_map.198 = (f32[1472,512]{1,0:T(8,128)}, bf16[1472,512]{1,0:T(8,128)(2,1)}, f32[3,92,192]{2,1,0:T(8,128)}, f32[92,192]{1,0:T(8,128)}, f32[56,128]{1,0:T(8,...) custom-call(s32[1,1536]{1,0:T(1,128)} %constant.2.clone.bid_ref, bf16[576,1024]{1,0:T(8,128)(2,1)} %get-tuple-element.43.qkv_ref, ...), custom_call_target="tpu_custom_call" | custom-call | flops 13388218368 | bytes 28901376 | tf_op jit(solution)/shard_map/pallas_call | solution.py:1050
  238.8 0.7 slice.17
  239.6 1.4 slice_bitcast_fusion
  240.9 0.7 copy.24
  241.6 0.0 copy-start
  241.6 1.9 copy-done
  243.5 0.0 copy-start.1
  243.5 1.9 copy-done.1
  245.3 0.0 copy-start.2
  245.3 1.4 copy-done.2
  246.7 1.3 copy-done.3
  248.0 1.1 copy-done.4
  249.1 1.0 copy-done.5
  250.1 0.9 copy-done.6
  251.0 3.7 %shard_map.199 = (f32[1472,512]{1,0:T(8,128)}, f32[1472,512]{1,0:T(8,128)}, f32[92,2,1792]{2,1,0:T(2,128)}, f32[3,92,192]{2,1,0:T(8,128)}, f32[92,192]{1,0:T(8,128)}, /*index=5*/f32[92,1792]{1,0:T(8,128)}) custom-call(f32[1472,512]{1,0:T(8,128)S(1)} %copy-done, bf16[1472,512]{1,0:T(8,128)(2,1)S(1)} %copy-done.2, f32[1472,512]{1,0:T(8,128)S(1)} %copy-done.1, ...), custom_call_target="tpu_custom_call" | custom-call | tf_op jit(solution)/shard_map/pallas_call | solution.py:1142
  (4 shorter events, 0.0 us)
Async XLA Ops:
  0.6 5.1 %copy-start.7 = (f32[1472]{0:T(1024)S(1)}, f32[1472]{0:T(1024)}, u32[]{:S(2)}) copy-start(f32[1472]{0:T(1024)} %param.17) | copy-start | bytes 17668
  0.7 5.7 %copy-start.8 = (f32[1472]{0:T(1024)S(1)}, f32[1472]{0:T(1024)}, u32[]{:S(2)}) copy-start(f32[1472]{0:T(1024)} %param.21) | copy-start | bytes 17668
  0.7 6.3 %copy-start.9 = (f32[32,3]{0,1:T(4,128)S(1)}, f32[32,3]{0,1:T(4,128)}, u32[]{:S(2)}) copy-start(f32[32,3]{0,1:T(4,128)} %param.19) | copy-start | bytes 1156
  2.7 36.0 %collective-permute-start = (bf16[1472,512]{1,0:T(8,128)(2,1)S(1)}, bf16[1472,512]{1,0:T(8,128)(2,1)S(1)}, u32[]{:S(2)}, u32[]{:S(2)}) collective-permute-start(bf16[1472,512]{1,0:T(8,128)(2,1)S(1)} %bitcast_convert_fusion), channel_id=1, source_target_pairs={{0,1},{1,0},{2,3},{3,2},{4,5},{5,4},{6,7},{7,6},{8,9},{9,8},{10,11... | collective-permute-start | bytes 4521992 | tf_op jit(solution)/shard_map/ppermute | solution.py:1195
  38.7 1.1 copy-start.10
  241.6 1.9 copy-start
  243.5 1.9 copy-start.1
  245.3 1.4 copy-start.2
  246.7 1.3 copy-start.3
  248.0 1.1 copy-start.4
  249.1 1.0 copy-start.5
  250.1 0.9 copy-start.6

commit v7 on v6

--- a/solution.py
+++ b/solution.py
@@ -675,6 +675,15 @@
     )(xt, w2, ct, wo, mid, wq)
 
 
+EVENTS = (
+    ((0, 0), ((2, 3), (3, 2))),
+    ((0, 2), ((1, 4),)),
+    ((2, 0), ((3, 3),)),
+    ((2, 1), ((2, 4),)),
+    ((3, 2), ((1, 5),)),
+)
+
+
 def tail_kernel(
     heads, dk, buckets, blocks, extra,
     bid_ref, qkv_ref, e_ref, inv_ref, wall_ref, ctx_ref, ag_ref, fg_ref, early_ref,
@@ -697,7 +706,7 @@
     near_blocks = blocks // 2
     near_part, far_part = pl.ds(0, rows), pl.ds(rows, rows)
     halves = ((sa, a1, a2, a3, a4), (sb_, b1, b2, b3, b4))
-    orders = (Y_FIRST, Z_FIRST)
+    orders = (Y_FIRST, Y_FIRST)
     copies = (
         (din_hbm, f1), (mid_hbm, f2), (cot_hbm, f3), (tok_hbm, f2), (nrm_hbm, nrm), (wq_hbm, wq), (wfar_hbm, wq),
     )
@@ -740,7 +749,7 @@
             outs[i][...] = both[:, i * cols : (i + 1) * cols]
 
     deep = len(LEVELS)
-    handed = (1, 2, 3, 4, 5, 6)
+    handed = (3, 4, 2, 5, 6, 1)
 
     def keep_copy(block):
         level = levels_of(block)
@@ -819,7 +828,7 @@
             local(i).start()
         meet([(p, x) for p in peers] + [other])
         back_copy(0).start()
-        for block in handed:
+        for block in handed[:-1]:
             hand_hop(levels_of(block), block).start()
         agc[...] = column(ag_ref[...])
         fgc[...] = column(fg_ref[...])
@@ -866,24 +875,21 @@
         local(5).wait()
         wn[...] = wq[...].astype(F32).T.astype(BF)
         local(6).start()
-        hand_absorb(2, 3)
-        hand_absorb(3, 1)
-        hand_absorb(3, 2)
-        hand_absorb(1, 4)
 
     @pl.when(qb == 2)
     def _():
         local(6).wait()
         wf[...] = wq[...].astype(F32).T.astype(BF)
 
-    @pl.when(qb == 3)
-    def _():
-        hand_absorb(3, 3)
-        hand_absorb(2, 4)
-
     q_true = (qb + near_blocks * x) % blocks
 
     def head(h, carry):
+        for at, events in EVENTS:
+            @pl.when((qb == at[0]) & (h == at[1]))
+            def _():
+                for level, block in events:
+                    hand_absorb(level, block)
+
         def head_rows(group):
             return pl.ds(pl.multiple_of(group * cols + h * dk, dk), dk)
 
@@ -917,7 +923,6 @@
         dproj_copy.start()
         back_copy(2).start()
         back_copy(3).start()
-        hand_absorb(1, 5)
         local(3).wait()
         local(4).wait()
         per = 4 * shard
@@ -936,14 +941,17 @@
                     k * shard : (k + 1) * shard, 2 * side * cols : 2 * (side + 1) * cols
                 ].astype(BF)
             hop(side, 0).start()
+        hand_absorb(2, 5)
 
         def near_rows(r, carry):
             f3[:, lanes(r)] = dot(wn[...], dproj[:, lanes(r)], ((1,), (0,)))
             return carry
 
         lax.fori_loop(0, near_blocks, near_rows, 0)
+        absorb(1, 0)
         absorb(0, 0)
-        absorb(1, 0)
+        hand_hop(3, 1).start()
+        hand_absorb(1, 6)
         ids = bid_ref[...]
         hot = ids == lax.broadcasted_iota(jnp.int32, (buckets, SPAN), 0)
         out_lane = lax.broadcasted_iota(jnp.int32, (buckets, 128), 1)
@@ -978,8 +986,6 @@
             sv[0, buckets + lines + i : buckets + lines + i + 1, 0:n] = fgain[:, 128 * i : 128 * i + n]
         round_copy(0).start()
         hand_absorb(3, 4)
-        hand_absorb(2, 5)
-        hand_absorb(1, 6)
         round_end(0)
         absorb(1, 1)
         dproj_copy.wait()
@@ -1004,6 +1010,7 @@
         absorb(1, 2)
         round_end(2)
         absorb(0, 2)
+        hand_absorb(3, 1)
         hand_absorb(3, 6)
         absorb(1, 3)
         round_end(3)
@@ -1119,8 +1126,9 @@
       quarter, half_way, hand)
 
 
-def outputs_kernel(near_ref, back_ref, ig_ref, ffi_ref, *refs):
-    n = (len(refs) - 3) // 2
+def outputs_kernel(near_ref, back_ref, ig_ref, ffi_ref, rel_ref, *refs):
+    n = (len(refs) - 4) // 2
+    refs, rel_out = refs[:-1], refs[-1]
     sources, res_ref, ig_out, ffi_out, targets = refs[:n], refs[n], refs[n + 1], refs[n + 2], refs[n + 3 :]
     res_ref[...] = near_ref[...] + back_ref[...].astype(F32)
     ig_out[...] = ig_ref[...]
@@ -1130,9 +1138,10 @@
     def _():
         for i in range(n):
             targets[i][...] = sources[i][...]
-
-
-def outputs(near, back, ig, ffi, *grads):
+        rel_out[...] = rel_ref[...].T[0 : rel_out.shape[0], 0 : rel_out.shape[1]]
+
+
+def outputs(near, back, ig, ffi, small, rel_shape, *grads):
     d, rows = near.shape
     block = pl.BlockSpec((d // 4, rows), lambda i: (i, 0))
     shard, two, f = ffi.shape
@@ -1142,11 +1151,12 @@
     return pl.pallas_call(
         outputs_kernel,
         grid=(4,),
-        in_specs=[block] * 3 + [part] + whole,
-        out_specs=[block] * 2 + [part] + whole,
-        out_shape=[jax.ShapeDtypeStruct(v.shape, F32) for v in (near, ig, ffi) + grads],
-        compiler_params=pltpu.CompilerParams(vmem_limit_bytes=40 << 20),
-    )(near, back, ig, ffi, *grads)
+        in_specs=[block] * 3 + [part, pl.BlockSpec((rel_shape[1], 128), lambda i: (0, 0))] + whole,
+        out_specs=[block] * 2 + [part] + whole + [pl.BlockSpec(rel_shape, lambda i: (0, 0))],
+        out_shape=[jax.ShapeDtypeStruct(v.shape, F32) for v in (near, ig, ffi) + grads]
+        + [jax.ShapeDtypeStruct(rel_shape, F32)],
+        compiler_params=pltpu.CompilerParams(vmem_limit_bytes=FF_VMEM),
+    )(near, back, ig, ffi, small, *grads)
 
 
 def take(array, index):
@@ -1207,21 +1217,21 @@
         qkv, e, inv, wall, ctx, again, fgain, early, din, mid, cot, tok, nrm, wq, wfar, far_out,
         quarter, half_way, hand, buckets, heads, dk, extra, ff_out_weight.shape[1],
     )
-    result, input_grad, ffi, grad_qkv, grad_out, ffo = outputs(
-        near_out, back, input_grad, ffi, grad_qkv, grad_out, ffo
+    for b in range(extra.bit_length() - 1):
+        small = small + hop(small, 1 << b)
+    result, input_grad, ffi, grad_qkv, grad_out, ffo, rel_grad = outputs(
+        near_out, back, input_grad, ffi, small, (heads * n_mp, buckets), grad_qkv, grad_out, ffo
     )
     grad_qkv = jnp.transpose(grad_qkv, (1, 0, 2))
     if extra > 1:
         grad_qkv, grad_out, ffo, ffi = (finish(g) for g in (grad_qkv, grad_out, ffo, ffi))
-    for b in range(extra.bit_length() - 1):
-        small = small + hop(small, 1 << b)
     lines = -(-d // 128)
     return (
         result.T,
         input_grad.T,
         small[buckets : buckets + lines].reshape(-1)[:d],
         grad_qkv,
-        small[:buckets, : heads * n_mp],
+        rel_grad.T,
         grad_out,
         small[buckets + lines : buckets + 2 * lines].reshape(-1)[:d],
         ffi,

time: 256 us -> 246 us (0.961)
  local copies, waits for them, and re-layouts: 26.4 us -> 15.6 us
    unnamed x25 -> x10, local copies, waits for them, and re-layouts: 23.1 us -> 13 us
    pallas_call x1, Pallas kernels: 3.69 us -> 7.59 us  [outputs(): pl.pallas_call(outputs_kernel, grid=(4,), in_specs=[block] * 3 + [part, p...]
    pallas_call x1, Pallas kernels: 78.4 us -> 74.9 us  [tail(): pl.pallas_call(functools.partial(tail_kernel, heads, dk, buckets, blocks,...]
where the time goes in v7:
time: 246 us; the launch traced here: 245 us
  Pallas kernels  203 us (83%)
  waiting for transfers between devices  19.9 us (8%)
  local copies, waits for them, and re-layouts  15.6 us (6%)
  starting transfers between devices  3 us (1%)
    pallas_call x1, Pallas kernels, ff_all(): pl.pallas_call(functools.partial(ff_kernel, steps, extra), in_specs=[any_...  82.9 us
    pallas_call x1, Pallas kernels, tail(): pl.pallas_call(functools.partial(tail_kernel, heads, dk, buckets, blocks,...  74.9 us
    pallas_call x1, Pallas kernels, front(): pl.pallas_call(functools.partial(front_kernel, heads, dk, buckets, blocks...  37.7 us
    ppermute x1, waiting for transfers between devices, per_device(): far = lax.ppermute(tok.astype(BF), 'mp', [(0, 1), (1, 0)])  19.9 us
    unnamed x10, local copies, waits for them, and re-layouts  13 us
    pallas_call x1, Pallas kernels, outputs(): pl.pallas_call(outputs_kernel, grid=(4,), in_specs=[block] * 3 + [part, p...  7.59 us
  transfers between devices with their start and end apart: 1, of which 1 were waited for; matrix products, arithmetic and copies ran while one was open for 5% of the time, Pallas kernels for 0%

profile of v7, /device:TPU:0, one launch (start us, length us, event | category | flops | bytes accessed | tf_op | source)
XLA Modules:
  0.0 244.5 jit_solution(3814886223480636380)
XLA Ops:
  0.6 0.0 copy-start
  0.7 0.0 copy-start.1
  0.7 0.0 copy-start.2
  0.7 2.1 bitcast_convert_fusion
  2.7 3.0 %collective-permute-start = (bf16[1472,512]{1,0:T(8,128)(2,1)S(1)}, bf16[1472,512]{1,0:T(8,128)(2,1)S(1)}, u32[]{:S(2)}, u32[]{:S(2)}) collective-permute-start(bf16[1472,512]{1,0:T(8,128)(2,1)S(1)} %bitcast_convert_fusion), channel_id=1, source_target_pairs={{0,1},{1,0},{2,3},{3,2},{4,5},{5,4},{6,7},{7,6},{8,9},{9,8},{10,11... | collective-permute-start | bytes 4521992 | tf_op jit(solution)/shard_map/ppermute | solution.py:1205
  5.7 0.0 copy-done
  5.7 0.6 reshape.33.ag_ref
  6.3 0.0 copy-done.1
  6.3 0.6 reshape.34.fg_ref
  6.9 0.0 copy-done.2
  6.9 0.7 copy.22.rel_ref
  7.6 11.2 %copy.25 = bf16[1472,2,1792]{2,0,1:T(8,128)(2,1)} copy(bf16[1472,2,1792]{2,1,0:T(2,128)(2,1)} %param.22) | data formatting | bytes 21102592 | tf_op args[9]
  18.9 19.9 %collective-permute-done.far_hbm = bf16[1472,512]{1,0:T(8,128)(2,1)S(1)} collective-permute-done((bf16[1472,512]{1,0:T(8,128)(2,1)S(1)}, bf16[1472,512]{1,0:T(8,128)(2,1)S(1)}, u32[]{:S(2)}, u32[]{:S(2)}) %collective-permute-start) | collective-permute-done | bytes 1507360 | tf_op jit(solution)/shard_map/ppermute | solution.py:1205
  38.7 0.0 copy-start.3
  38.7 1.1 copy-done.3
  39.9 37.7 %shard_map.196 = (bf16[3,4,1024,256]{3,2,1,0:T(8,128)(2,1)}, f32[3,4,1,256]{3,2,1,0:T(1,128)}, bf16[576,1024]{1,0:T(8,128)(2,1)}, bf16[384,1024]{1,0:T(8,128)(2,...) custom-call(f32[32,3]{1,0:T(8,128)} %copy.22.rel_ref, ...), custom_call_target="tpu_custom_call" | custom-call | flops 6115295232 | bytes 28901376 | tf_op jit(solution)/shard_map/pallas_call | solution.py:307
  77.5 82.9 %shard_map.197 = (f32[3,96,256]{2,1,0:T(8,128)}, f32[1472,512]{1,0:T(8,128)}, f32[1472,512]{1,0:T(8,128)}, bf16[1472,512]{1,0:T(8,128)(2,1)}, bf16[2,2,3,96,256]...) custom-call(bf16[1472,1024]{1,0:T(8,128)(2,1)} %get-tuple-element.40, ...), custom_call_target="tpu_custom_call" | custom-call | flops 48620371968 | bytes 39944192 | tf_op jit(solution)/shard_map/pallas_call | solution.py:627
  160.4 74.9 %shard_map.198 = (f32[1472,512]{1,0:T(8,128)}, bf16[1472,512]{1,0:T(8,128)(2,1)}, f32[3,92,192]{2,1,0:T(8,128)}, f32[92,192]{1,0:T(8,128)}, f32[56,128]{1,0:T(8,...) custom-call(s32[1,1536]{1,0:T(1,128)} %constant.2.clone.bid_ref, bf16[576,1024]{1,0:T(8,128)(2,1)} %get-tuple-element.44.qkv_ref, ...), custom_call_target="tpu_custom_call" | custom-call | flops 13388218368 | bytes 28901376 | tf_op jit(solution)/shard_map/pallas_call | solution.py:1057
  235.4 1.4 slice_bitcast_fusion
  236.7 7.6 %shard_map.199 = (f32[1472,512]{1,0:T(8,128)}, f32[1472,512]{1,0:T(8,128)}, f32[92,2,1792]{2,1,0:T(2,128)}, f32[3,92,192]{2,1,0:T(8,128)}, f32[92,192]{1,0:T(8,1...) custom-call(f32[1472,512]{1,0:T(8,128)} %get-tuple-element.43.near_ref, bf16[1472,512]{1,0:T(8,128)(2,1)} %get-tuple-element.57.back_ref, ...), custom_call_target="tpu_custom_call" | custom-call | tf_op jit(solution)/shard_map/pallas_call | solution.py:1151
Async XLA Ops:
  0.6 5.1 %copy-start = (f32[1472]{0:T(1024)S(1)}, f32[1472]{0:T(1024)}, u32[]{:S(2)}) copy-start(f32[1472]{0:T(1024)} %param.17) | copy-start | bytes 17668
  0.7 5.7 %copy-start.1 = (f32[1472]{0:T(1024)S(1)}, f32[1472]{0:T(1024)}, u32[]{:S(2)}) copy-start(f32[1472]{0:T(1024)} %param.21) | copy-start | bytes 17668
  0.7 6.3 %copy-start.2 = (f32[32,3]{0,1:T(4,128)S(1)}, f32[32,3]{0,1:T(4,128)}, u32[]{:S(2)}) copy-start(f32[32,3]{0,1:T(4,128)} %param.19) | copy-start | bytes 1156
  2.7 36.0 %collective-permute-start = (bf16[1472,512]{1,0:T(8,128)(2,1)S(1)}, bf16[1472,512]{1,0:T(8,128)(2,1)S(1)}, u32[]{:S(2)}, u32[]{:S(2)}) collective-permute-start(bf16[1472,512]{1,0:T(8,128)(2,1)S(1)} %bitcast_convert_fusion), channel_id=1, source_target_pairs={{0,1},{1,0},{2,3},{3,2},{4,5},{5,4},{6,7},{7,6},{8,9},{9,8},{10,11... | collective-permute-start | bytes 4521992 | tf_op jit(solution)/shard_map/ppermute | solution.py:1205
  38.7 1.1 copy-start.3

commit v8 on v7

--- a/solution.py
+++ b/solution.py
@@ -140,12 +140,13 @@
 
     def out(i):
         src, dst = (
-            (call, ctx_hbm), (nrm, nrm_hbm), (f1, mid_hbm), (cl, ct_hbm.at[:, pl.ds(0, rows)]), (wall, wall_hbm)
+            (call, ctx_hbm), (nrm, nrm_hbm), (f1.at[:, lanes(0)], mid_hbm.at[:, lanes(0)]), (cl, ct_hbm.at[:, pl.ds(0, rows)]), (wall, wall_hbm),
+            (f1.at[:, pl.ds(BLK, rows - BLK)], mid_hbm.at[:, pl.ds(BLK, rows - BLK)]),
         )[i]
         return pltpu.make_async_copy(src, dst, osem.at[i])
 
     def xt_out(b):
-        return pltpu.make_async_copy(xo.at[:, lanes(b)], xt_hbm.at[:, lanes(b)], osem.at[5 + b])
+        return pltpu.make_async_copy(xo.at[:, lanes(b)], xt_hbm.at[:, lanes(b)], osem.at[6 + b])
 
     w_copy = remote(wo_ref.at[part], wall.at[far_part], wsend.at[0], wrecv.at[0], other)
     w_pass = remote(wall.at[far_part], wall.at[far_part], wsend.at[1], wrecv.at[1], sibling)
@@ -275,15 +276,17 @@
             if b < near_blocks:
                 v = v + f1[:, ls]
                 f1[:, ls] = v
+                if b == 0:
+                    out(2).start()
             else:
                 v = v + fb[:, b * BLK - rows : (b + 1) * BLK - rows].astype(F32)
             xo[:, ls] = (v * norm_scale(v) * fgc[...]).astype(BF)
             xt_out(b).start()
         out(0).start()
-        out(2).start()
+        out(5).start()
         for i in range(4):
             c_copy(i).wait()
-        for i in range(5):
+        for i in range(6):
             out(i).wait()
         for b in range(blocks):
             xt_out(b).wait()
@@ -342,7 +345,7 @@
             pltpu.VMEM((d, 2 * cols), BF),
             pltpu.VMEM((2 * cols, seq), BF),
             pltpu.VMEM((d, seq), BF),
-            dma((3,)), dma((5 + blocks,)), dma((6,)), dma((6,)), dma((blocks,)), dma((blocks,)),
+            dma((3,)), dma((6 + blocks,)), dma((6,)), dma((6,)), dma((blocks,)), dma((blocks,)),
         ],
         compiler_params=pltpu.CompilerParams(
             vmem_limit_bytes=FF_VMEM, collective_id=2, has_side_effects=True
@@ -559,7 +562,7 @@
             absorb_first(m)
 
         for at, events in (
-            (21, ((1, 0),)), (23, ((1, 1),)), (25, ((2, 0),)), (27, ((1, 2), (2, 1))),
+            (21, ((1, 0),)), (23, ((1, 1),)), (25, ((2, 0),)), (27, ((1, 2),)),
         ):
             @pl.when(u == at)
             def _():
@@ -586,23 +589,24 @@
         return carry
 
     lax.fori_loop(0, chunks, far_out, 0)
+    absorb(2, 1)
     far_copy = pltpu.make_async_copy(of, far_hbm, osem.at[0])
     far_copy.start()
+    mid_copy.wait()
+
+    def near_out(n, carry):
+        at = lanes(n + chunks)
+        din[:, at] = din[:, at] + out_part(n)
+        return carry
+
+    lax.fori_loop(0, chunks, near_out, 0)
+    near_copy = pltpu.make_async_copy(din.at[:, far_part], near_hbm, osem.at[1])
+    near_copy.start()
+    absorb_first(end)
     x_copy.wait()
     din[:, near_part] += xr[...].astype(F32)
     din_copy = pltpu.make_async_copy(din.at[:, near_part], din_hbm, osem.at[2])
     din_copy.start()
-    mid_copy.wait()
-
-    def near_out(n, carry):
-        at = lanes(n + chunks)
-        din[:, at] = din[:, at] + out_part(n)
-        return carry
-
-    lax.fori_loop(0, chunks, near_out, 0)
-    near_copy = pltpu.make_async_copy(din.at[:, far_part], near_hbm, osem.at[1])
-    near_copy.start()
-    absorb_first(end)
     absorb(3, 0)
     absorb(2, 2)
     absorb(1, 3)

time: 246 us -> 244 us (level)
    pallas_call x1, Pallas kernels: 82.9 us -> 79.4 us  [ff_all(): pl.pallas_call(functools.partial(ff_kernel, steps, extra), in_specs=[any_...]
where the time goes in v8:
time: 244 us; the launch traced here: 243 us
  Pallas kernels  202 us (83%)
  waiting for transfers between devices  19.9 us (8%)
  local copies, waits for them, and re-layouts  15.6 us (6%)
  starting transfers between devices  3 us (1%)
    pallas_call x1, Pallas kernels, ff_all(): pl.pallas_call(functools.partial(ff_kernel, steps, extra), in_specs=[any_...  79.4 us
    pallas_call x1, Pallas kernels, tail(): pl.pallas_call(functools.partial(tail_kernel, heads, dk, buckets, blocks,...  77.3 us
    pallas_call x1, Pallas kernels, front(): pl.pallas_call(functools.partial(front_kernel, heads, dk, buckets, blocks...  37.7 us
    ppermute x1, waiting for transfers between devices, per_device(): far = lax.ppermute(tok.astype(BF), 'mp', [(0, 1), (1, 0)])  19.9 us
    unnamed x10, local copies, waits for them, and re-layouts  13 us
    pallas_call x1, Pallas kernels, outputs(): pl.pallas_call(outputs_kernel, grid=(4,), in_specs=[block] * 3 + [part, p...  7.59 us
  transfers between devices with their start and end apart: 1, of which 1 were waited for; matrix products, arithmetic and copies ran while one was open for 5% of the time, Pallas kernels for 0%

profile of v8, /device:TPU:0, one launch (start us, length us, event | category | flops | bytes accessed | tf_op | source)
XLA Modules:
  0.0 243.4 jit_solution(3943946317104738191)
XLA Ops:
  0.6 0.0 copy-start
  0.7 0.0 copy-start.1
  0.7 0.0 copy-start.2
  0.7 2.1 bitcast_convert_fusion
  2.7 3.0 %collective-permute-start = (bf16[1472,512]{1,0:T(8,128)(2,1)S(1)}, bf16[1472,512]{1,0:T(8,128)(2,1)S(1)}, u32[]{:S(2)}, u32[]{:S(2)}) collective-permute-start(bf16[1472,512]{1,0:T(8,128)(2,1)S(1)} %bitcast_convert_fusion), channel_id=1, source_target_pairs={{0,1},{1,0},{2,3},{3,2},{4,5},{5,4},{6,7},{7,6},{8,9},{9,8},{10,11... | collective-permute-start | bytes 4521992 | tf_op jit(solution)/shard_map/ppermute | solution.py:1209
  5.7 0.0 copy-done
  5.7 0.6 reshape.33.ag_ref
  6.3 0.0 copy-done.1
  6.3 0.6 reshape.34.fg_ref
  6.9 0.0 copy-done.2
  6.9 0.7 copy.22.rel_ref
  7.6 11.2 %copy.25 = bf16[1472,2,1792]{2,0,1:T(8,128)(2,1)} copy(bf16[1472,2,1792]{2,1,0:T(2,128)(2,1)} %param.22) | data formatting | bytes 21102592 | tf_op args[9]
  18.9 19.9 %collective-permute-done.far_hbm = bf16[1472,512]{1,0:T(8,128)(2,1)S(1)} collective-permute-done((bf16[1472,512]{1,0:T(8,128)(2,1)S(1)}, bf16[1472,512]{1,0:T(8,128)(2,1)S(1)}, u32[]{:S(2)}, u32[]{:S(2)}) %collective-permute-start) | collective-permute-done | bytes 1507360 | tf_op jit(solution)/shard_map/ppermute | solution.py:1209
  38.7 0.0 copy-start.3
  38.7 1.1 copy-done.3
  39.9 37.7 %shard_map.196 = (bf16[3,4,1024,256]{3,2,1,0:T(8,128)(2,1)}, f32[3,4,1,256]{3,2,1,0:T(1,128)}, bf16[576,1024]{1,0:T(8,128)(2,1)}, bf16[384,1024]{1,0:T(8,128)(2,...) custom-call(f32[32,3]{1,0:T(8,128)} %copy.22.rel_ref, ...), custom_call_target="tpu_custom_call" | custom-call | flops 6115295232 | bytes 28901376 | tf_op jit(solution)/shard_map/pallas_call | solution.py:310
  77.5 79.4 %shard_map.197 = (f32[3,96,256]{2,1,0:T(8,128)}, f32[1472,512]{1,0:T(8,128)}, f32[1472,512]{1,0:T(8,128)}, bf16[1472,512]{1,0:T(8,128)(2,1)}, bf16[2,2,3,96,256]...) custom-call(bf16[1472,1024]{1,0:T(8,128)(2,1)} %get-tuple-element.40, ...), custom_call_target="tpu_custom_call" | custom-call | flops 48620371968 | bytes 39944192 | tf_op jit(solution)/shard_map/pallas_call | solution.py:631
  157.0 77.3 %shard_map.198 = (f32[1472,512]{1,0:T(8,128)}, bf16[1472,512]{1,0:T(8,128)(2,1)}, f32[3,92,192]{2,1,0:T(8,128)}, f32[92,192]{1,0:T(8,128)}, f32[56,128]{1,0:T(8,...) custom-call(s32[1,1536]{1,0:T(1,128)} %constant.2.clone.bid_ref, bf16[576,1024]{1,0:T(8,128)(2,1)} %get-tuple-element.44.qkv_ref, ...), custom_call_target="tpu_custom_call" | custom-call | flops 13388218368 | bytes 28901376 | tf_op jit(solution)/shard_map/pallas_call | solution.py:1061
  234.3 1.4 slice_bitcast_fusion
  235.6 7.6 %shard_map.199 = (f32[1472,512]{1,0:T(8,128)}, f32[1472,512]{1,0:T(8,128)}, f32[92,2,1792]{2,1,0:T(2,128)}, f32[3,92,192]{2,1,0:T(8,128)}, f32[92,192]{1,0:T(8,1...) custom-call(f32[1472,512]{1,0:T(8,128)} %get-tuple-element.43.near_ref, bf16[1472,512]{1,0:T(8,128)(2,1)} %get-tuple-element.57.back_ref, ...), custom_call_target="tpu_custom_call" | custom-call | tf_op jit(solution)/shard_map/pallas_call | solution.py:1155
Async XLA Ops:
  0.6 5.1 %copy-start = (f32[1472]{0:T(1024)S(1)}, f32[1472]{0:T(1024)}, u32[]{:S(2)}) copy-start(f32[1472]{0:T(1024)} %param.17) | copy-start | bytes 17668
  0.7 5.7 %copy-start.1 = (f32[1472]{0:T(1024)S(1)}, f32[1472]{0:T(1024)}, u32[]{:S(2)}) copy-start(f32[1472]{0:T(1024)} %param.21) | copy-start | bytes 17668
  0.7 6.3 %copy-start.2 = (f32[32,3]{0,1:T(4,128)S(1)}, f32[32,3]{0,1:T(4,128)}, u32[]{:S(2)}) copy-start(f32[32,3]{0,1:T(4,128)} %param.19) | copy-start | bytes 1156
  2.7 36.0 %collective-permute-start = (bf16[1472,512]{1,0:T(8,128)(2,1)S(1)}, bf16[1472,512]{1,0:T(8,128)(2,1)S(1)}, u32[]{:S(2)}, u32[]{:S(2)}) collective-permute-start(bf16[1472,512]{1,0:T(8,128)(2,1)S(1)} %bitcast_convert_fusion), channel_id=1, source_target_pairs={{0,1},{1,0},{2,3},{3,2},{4,5},{5,4},{6,7},{7,6},{8,9},{9,8},{10,11... | collective-permute-start | bytes 4521992 | tf_op jit(solution)/shard_map/ppermute | solution.py:1209
  38.7 1.1 copy-start.3

commit v9 on v8

--- a/solution.py
+++ b/solution.py
@@ -1147,14 +1147,14 @@
 
 def outputs(near, back, ig, ffi, small, rel_shape, *grads):
     d, rows = near.shape
-    block = pl.BlockSpec((d // 4, rows), lambda i: (i, 0))
+    block = pl.BlockSpec((d // 2, rows), lambda i: (i, 0))
     shard, two, f = ffi.shape
-    part = pl.BlockSpec((shard // 4, two, f), lambda i: (i, 0, 0))
+    part = pl.BlockSpec((shard // 2, two, f), lambda i: (i, 0, 0))
     one = pl.Buffered(1)
     whole = [pl.BlockSpec(v.shape, lambda i, n=v.ndim: (0,) * n, pipeline_mode=one) for v in grads]
     return pl.pallas_call(
         outputs_kernel,
-        grid=(4,),
+        grid=(2,),
         in_specs=[block] * 3 + [part, pl.BlockSpec((rel_shape[1], 128), lambda i: (0, 0))] + whole,
         out_specs=[block] * 2 + [part] + whole + [pl.BlockSpec(rel_shape, lambda i: (0, 0))],
         out_shape=[jax.ShapeDtypeStruct(v.shape, F32) for v in (near, ig, ffi) + grads]

time: 244 us -> 243 us (level)
  no operation moved by 1% of the time
where the time goes in v9:
time: 243 us; the launch traced here: 242 us
  Pallas kernels  201 us (83%)
  waiting for transfers between devices  19.9 us (8%)
  local copies, waits for them, and re-layouts  15.6 us (6%)
  starting transfers between devices  3 us (1%)
    pallas_call x1, Pallas kernels, ff_all(): pl.pallas_call(functools.partial(ff_kernel, steps, extra), in_specs=[any_...  79.4 us
    pallas_call x1, Pallas kernels, tail(): pl.pallas_call(functools.partial(tail_kernel, heads, dk, buckets, blocks,...  77.3 us
    pallas_call x1, Pallas kernels, front(): pl.pallas_call(functools.partial(front_kernel, heads, dk, buckets, blocks...  37.7 us
    ppermute x1, waiting for transfers between devices, per_device(): far = lax.ppermute(tok.astype(BF), 'mp', [(0, 1), (1, 0)])  19.9 us
    unnamed x10, local copies, waits for them, and re-layouts  13 us
    pallas_call x1, Pallas kernels, outputs(): pl.pallas_call(outputs_kernel, grid=(2,), in_specs=[block] * 3 + [part, p...  6.49 us
  transfers between devices with their start and end apart: 1, of which 1 were waited for; matrix products, arithmetic and copies ran while one was open for 5% of the time, Pallas kernels for 0%

profile of v9, /device:TPU:0, one launch (start us, length us, event | category | flops | bytes accessed | tf_op | source)
XLA Modules:
  0.0 242.3 jit_solution(3900697175797291485)
XLA Ops:
  0.6 0.0 copy-start
  0.7 0.0 copy-start.1
  0.7 0.0 copy-start.2
  0.7 2.1 bitcast_convert_fusion
  2.7 3.0 %collective-permute-start = (bf16[1472,512]{1,0:T(8,128)(2,1)S(1)}, bf16[1472,512]{1,0:T(8,128)(2,1)S(1)}, u32[]{:S(2)}, u32[]{:S(2)}) collective-permute-start(bf16[1472,512]{1,0:T(8,128)(2,1)S(1)} %bitcast_convert_fusion), channel_id=1, source_target_pairs={{0,1},{1,0},{2,3},{3,2},{4,5},{5,4},{6,7},{7,6},{8,9},{9,8},{10,11... | collective-permute-start | bytes 4521992 | tf_op jit(solution)/shard_map/ppermute | solution.py:1209
  5.7 0.0 copy-done
  5.7 0.6 reshape.33.ag_ref
  6.3 0.0 copy-done.1
  6.3 0.6 reshape.34.fg_ref
  6.9 0.0 copy-done.2
  6.9 0.7 copy.22.rel_ref
  7.6 11.2 %copy.25 = bf16[1472,2,1792]{2,0,1:T(8,128)(2,1)} copy(bf16[1472,2,1792]{2,1,0:T(2,128)(2,1)} %param.22) | data formatting | bytes 21102592 | tf_op args[9]
  18.9 19.9 %collective-permute-done.far_hbm = bf16[1472,512]{1,0:T(8,128)(2,1)S(1)} collective-permute-done((bf16[1472,512]{1,0:T(8,128)(2,1)S(1)}, bf16[1472,512]{1,0:T(8,128)(2,1)S(1)}, u32[]{:S(2)}, u32[]{:S(2)}) %collective-permute-start) | collective-permute-done | bytes 1507360 | tf_op jit(solution)/shard_map/ppermute | solution.py:1209
  38.7 0.0 copy-start.3
  38.7 1.1 copy-done.3
  39.9 37.7 %shard_map.196 = (bf16[3,4,1024,256]{3,2,1,0:T(8,128)(2,1)}, f32[3,4,1,256]{3,2,1,0:T(1,128)}, bf16[576,1024]{1,0:T(8,128)(2,1)}, bf16[384,1024]{1,0:T(8,128)(2,...) custom-call(f32[32,3]{1,0:T(8,128)} %copy.22.rel_ref, ...), custom_call_target="tpu_custom_call" | custom-call | flops 6115295232 | bytes 28901376 | tf_op jit(solution)/shard_map/pallas_call | solution.py:310
  77.5 79.4 %shard_map.197 = (f32[3,96,256]{2,1,0:T(8,128)}, f32[1472,512]{1,0:T(8,128)}, f32[1472,512]{1,0:T(8,128)}, bf16[1472,512]{1,0:T(8,128)(2,1)}, bf16[2,2,3,96,256]...) custom-call(bf16[1472,1024]{1,0:T(8,128)(2,1)} %get-tuple-element.40, ...), custom_call_target="tpu_custom_call" | custom-call | flops 48620371968 | bytes 39944192 | tf_op jit(solution)/shard_map/pallas_call | solution.py:631
  157.0 77.3 %shard_map.198 = (f32[1472,512]{1,0:T(8,128)}, bf16[1472,512]{1,0:T(8,128)(2,1)}, f32[3,92,192]{2,1,0:T(8,128)}, f32[92,192]{1,0:T(8,128)}, f32[56,128]{1,0:T(8,...) custom-call(s32[1,1536]{1,0:T(1,128)} %constant.2.clone.bid_ref, bf16[576,1024]{1,0:T(8,128)(2,1)} %get-tuple-element.44.qkv_ref, ...), custom_call_target="tpu_custom_call" | custom-call | flops 13388218368 | bytes 28901376 | tf_op jit(solution)/shard_map/pallas_call | solution.py:1061
  234.3 1.4 slice_bitcast_fusion
  235.6 6.5 %shard_map.199 = (f32[1472,512]{1,0:T(8,128)}, f32[1472,512]{1,0:T(8,128)}, f32[92,2,1792]{2,1,0:T(2,128)}, f32[3,92,192]{2,1,0:T(8,128)}, f32[92,192]{1,0:T(8,1...) custom-call(f32[1472,512]{1,0:T(8,128)} %get-tuple-element.43.near_ref, bf16[1472,512]{1,0:T(8,128)(2,1)} %get-tuple-element.57.back_ref, ...), custom_call_target="tpu_custom_call" | custom-call | tf_op jit(solution)/shard_map/pallas_call | solution.py:1155
Async XLA Ops:
  0.6 5.1 %copy-start = (f32[1472]{0:T(1024)S(1)}, f32[1472]{0:T(1024)}, u32[]{:S(2)}) copy-start(f32[1472]{0:T(1024)} %param.17) | copy-start | bytes 17668
  0.7 5.7 %copy-start.1 = (f32[1472]{0:T(1024)S(1)}, f32[1472]{0:T(1024)}, u32[]{:S(2)}) copy-start(f32[1472]{0:T(1024)} %param.21) | copy-start | bytes 17668
  0.7 6.3 %copy-start.2 = (f32[32,3]{0,1:T(4,128)S(1)}, f32[32,3]{0,1:T(4,128)}, u32[]{:S(2)}) copy-start(f32[32,3]{0,1:T(4,128)} %param.19) | copy-start | bytes 1156
  2.7 36.0 %collective-permute-start = (bf16[1472,512]{1,0:T(8,128)(2,1)S(1)}, bf16[1472,512]{1,0:T(8,128)(2,1)S(1)}, u32[]{:S(2)}, u32[]{:S(2)}) collective-permute-start(bf16[1472,512]{1,0:T(8,128)(2,1)S(1)} %bitcast_convert_fusion), channel_id=1, source_target_pairs={{0,1},{1,0},{2,3},{3,2},{4,5},{5,4},{6,7},{7,6},{8,9},{9,8},{10,11... | collective-permute-start | bytes 4521992 | tf_op jit(solution)/shard_map/ppermute | solution.py:1209
  38.7 1.1 copy-start.3

commit v10 on v9

--- a/solution.py
+++ b/solution.py
@@ -1138,9 +1138,11 @@
     ig_out[...] = ig_ref[...]
     ffi_out[...] = ffi_ref[...]
 
+    targets[-1][...] = sources[-1][...]
+
     @pl.when(pl.program_id(0) == 0)
     def _():
-        for i in range(n):
+        for i in range(n - 1):
             targets[i][...] = sources[i][...]
         rel_out[...] = rel_ref[...].T[0 : rel_out.shape[0], 0 : rel_out.shape[1]]
 
@@ -1152,6 +1154,7 @@
     part = pl.BlockSpec((shard // 2, two, f), lambda i: (i, 0, 0))
     one = pl.Buffered(1)
     whole = [pl.BlockSpec(v.shape, lambda i, n=v.ndim: (0,) * n, pipeline_mode=one) for v in grads]
+    whole[-1] = pl.BlockSpec((shard, f // 2), lambda i: (0, i))
     return pl.pallas_call(
         outputs_kernel,
         grid=(2,),

time: 243 us -> 243 us (level)
  no operation moved by 1% of the time
where the time goes in v10:
time: 243 us; the launch traced here: 242 us
  Pallas kernels  201 us (83%)
  waiting for transfers between devices  19.9 us (8%)
  local copies, waits for them, and re-layouts  15.6 us (6%)
  starting transfers between devices  3 us (1%)
    pallas_call x1, Pallas kernels, ff_all(): pl.pallas_call(functools.partial(ff_kernel, steps, extra), in_specs=[any_...  79.4 us
    pallas_call x1, Pallas kernels, tail(): pl.pallas_call(functools.partial(tail_kernel, heads, dk, buckets, blocks,...  77.3 us
    pallas_call x1, Pallas kernels, front(): pl.pallas_call(functools.partial(front_kernel, heads, dk, buckets, blocks...  37.7 us
    ppermute x1, waiting for transfers between devices, per_device(): far = lax.ppermute(tok.astype(BF), 'mp', [(0, 1), (1, 0)])  19.9 us
    unnamed x10, local copies, waits for them, and re-layouts  13 us
    pallas_call x1, Pallas kernels, outputs(): pl.pallas_call(outputs_kernel, grid=(2,), in_specs=[block] * 3 + [part, p...  6.53 us
  transfers between devices with their start and end apart: 1, of which 1 were waited for; matrix products, arithmetic and copies ran while one was open for 5% of the time, Pallas kernels for 0%

profile of v10, /device:TPU:0, one launch (start us, length us, event | category | flops | bytes accessed | tf_op | source)
XLA Modules:
  0.0 242.3 jit_solution(10301121289071479055)
XLA Ops:
  0.6 0.0 copy-start
  0.7 0.0 copy-start.1
  0.7 0.0 copy-start.2
  0.7 2.1 bitcast_convert_fusion
  2.7 3.0 %collective-permute-start = (bf16[1472,512]{1,0:T(8,128)(2,1)S(1)}, bf16[1472,512]{1,0:T(8,128)(2,1)S(1)}, u32[]{:S(2)}, u32[]{:S(2)}) collective-permute-start(bf16[1472,512]{1,0:T(8,128)(2,1)S(1)} %bitcast_convert_fusion), channel_id=1, source_target_pairs={{0,1},{1,0},{2,3},{3,2},{4,5},{5,4},{6,7},{7,6},{8,9},{9,8},{10,11... | collective-permute-start | bytes 4521992 | tf_op jit(solution)/shard_map/ppermute | solution.py:1212
  5.7 0.0 copy-done
  5.7 0.6 reshape.33.ag_ref
  6.3 0.0 copy-done.1
  6.3 0.6 reshape.34.fg_ref
  6.9 0.0 copy-done.2
  6.9 0.7 copy.22.rel_ref
  7.6 11.2 %copy.25 = bf16[1472,2,1792]{2,0,1:T(8,128)(2,1)} copy(bf16[1472,2,1792]{2,1,0:T(2,128)(2,1)} %param.22) | data formatting | bytes 21102592 | tf_op args[9]
  18.9 19.9 %collective-permute-done.far_hbm = bf16[1472,512]{1,0:T(8,128)(2,1)S(1)} collective-permute-done((bf16[1472,512]{1,0:T(8,128)(2,1)S(1)}, bf16[1472,512]{1,0:T(8,128)(2,1)S(1)}, u32[]{:S(2)}, u32[]{:S(2)}) %collective-permute-start) | collective-permute-done | bytes 1507360 | tf_op jit(solution)/shard_map/ppermute | solution.py:1212
  38.7 0.0 copy-start.3
  38.7 1.1 copy-done.3
  39.9 37.7 %shard_map.196 = (bf16[3,4,1024,256]{3,2,1,0:T(8,128)(2,1)}, f32[3,4,1,256]{3,2,1,0:T(1,128)}, bf16[576,1024]{1,0:T(8,128)(2,1)}, bf16[384,1024]{1,0:T(8,128)(2,...) custom-call(f32[32,3]{1,0:T(8,128)} %copy.22.rel_ref, ...), custom_call_target="tpu_custom_call" | custom-call | flops 6115295232 | bytes 28901376 | tf_op jit(solution)/shard_map/pallas_call | solution.py:310
  77.5 79.4 %shard_map.197 = (f32[3,96,256]{2,1,0:T(8,128)}, f32[1472,512]{1,0:T(8,128)}, f32[1472,512]{1,0:T(8,128)}, bf16[1472,512]{1,0:T(8,128)(2,1)}, bf16[2,2,3,96,256]...) custom-call(bf16[1472,1024]{1,0:T(8,128)(2,1)} %get-tuple-element.40, ...), custom_call_target="tpu_custom_call" | custom-call | flops 48620371968 | bytes 39944192 | tf_op jit(solution)/shard_map/pallas_call | solution.py:631
  157.0 77.3 %shard_map.198 = (f32[1472,512]{1,0:T(8,128)}, bf16[1472,512]{1,0:T(8,128)(2,1)}, f32[3,92,192]{2,1,0:T(8,128)}, f32[92,192]{1,0:T(8,128)}, f32[56,128]{1,0:T(8,...) custom-call(s32[1,1536]{1,0:T(1,128)} %constant.2.clone.bid_ref, bf16[576,1024]{1,0:T(8,128)(2,1)} %get-tuple-element.44.qkv_ref, ...), custom_call_target="tpu_custom_call" | custom-call | flops 13388218368 | bytes 28901376 | tf_op jit(solution)/shard_map/pallas_call | solution.py:1061
  234.3 1.4 slice_bitcast_fusion
  235.6 6.5 %shard_map.199 = (f32[1472,512]{1,0:T(8,128)}, f32[1472,512]{1,0:T(8,128)}, f32[92,2,1792]{2,1,0:T(2,128)}, f32[3,92,192]{2,1,0:T(8,128)}, f32[92,192]{1,0:T(8,1...) custom-call(f32[1472,512]{1,0:T(8,128)} %get-tuple-element.43.near_ref, bf16[1472,512]{1,0:T(8,128)(2,1)} %get-tuple-element.57.back_ref, ...), custom_call_target="tpu_custom_call" | custom-call | tf_op jit(solution)/shard_map/pallas_call | solution.py:1158
Async XLA Ops:
  0.6 5.1 %copy-start = (f32[1472]{0:T(1024)S(1)}, f32[1472]{0:T(1024)}, u32[]{:S(2)}) copy-start(f32[1472]{0:T(1024)} %param.17) | copy-start | bytes 17668
  0.7 5.7 %copy-start.1 = (f32[1472]{0:T(1024)S(1)}, f32[1472]{0:T(1024)}, u32[]{:S(2)}) copy-start(f32[1472]{0:T(1024)} %param.21) | copy-start | bytes 17668
  0.7 6.3 %copy-start.2 = (f32[32,3]{0,1:T(4,128)S(1)}, f32[32,3]{0,1:T(4,128)}, u32[]{:S(2)}) copy-start(f32[32,3]{0,1:T(4,128)} %param.19) | copy-start | bytes 1156
  2.7 36.0 %collective-permute-start = (bf16[1472,512]{1,0:T(8,128)(2,1)S(1)}, bf16[1472,512]{1,0:T(8,128)(2,1)S(1)}, u32[]{:S(2)}, u32[]{:S(2)}) collective-permute-start(bf16[1472,512]{1,0:T(8,128)(2,1)S(1)} %bitcast_convert_fusion), channel_id=1, source_target_pairs={{0,1},{1,0},{2,3},{3,2},{4,5},{5,4},{6,7},{7,6},{8,9},{9,8},{10,11... | collective-permute-start | bytes 4521992 | tf_op jit(solution)/shard_map/ppermute | solution.py:1212
  38.7 1.1 copy-start.3
